TPU v7x, 32 devices: a whole 2x2x4 slice. The times are simulated.
32 devices in a mesh: dp: 8 (over z, x), seq: 4 (over y, core).
Axes of the slice: x: 2, y: 2, z: 4, core: 2. Of those that a mesh axis runs over, the one named last changes fastest.
Arguments:
- x_content: bfloat16 [16, 512, 768], P('dp', 'seq'), may hold values from -6 to 6
- x_query: bfloat16 [16, 512, 768], P('dp', 'seq'), may hold values from -6 to 6
- cot_content: bfloat16 [16, 512, 768], P('dp', 'seq'), may hold values from -6 to 6
- cot_query: bfloat16 [16, 512, 768], P('dp', 'seq'), may hold values from -6 to 6
- w_query: bfloat16 [768, 768], P('dp'), may hold values from -0.21875 to 0.21875
- b_query: bfloat16 [768], P('dp'), may hold values from -1.75 to 1.75
- w_key: bfloat16 [768, 768], P('dp'), may hold values from -0.21875 to 0.21875
- w_value: bfloat16 [768, 768], P('dp'), may hold values from -0.21875 to 0.21875
- b_value: bfloat16 [768], P('dp'), may hold values from -1.75 to 1.75
- w_out: bfloat16 [768, 768], P('dp'), may hold values from -0.875 to 0.875
- b_out: bfloat16 [768], P('dp'), may hold values from -1.75 to 1.75
- gain_attn: bfloat16 [768], P('dp'), may hold values from 0.5 to 1.5
- shift_attn: bfloat16 [768], P('dp'), may hold values from -1.75 to 1.75
- w_up: bfloat16 [768, 3072], P('dp'), may hold values from -0.21875 to 0.21875
- b_up: bfloat16 [3072], P('dp'), may hold values from -1.75 to 1.75
- w_down: bfloat16 [3072, 768], P('dp'), may hold values from -0.109375 to 0.109375
- b_down: bfloat16 [768], P('dp'), may hold values from -1.75 to 1.75
- gain_ffn: bfloat16 [768], P('dp'), may hold values from 0.5 to 1.5
- shift_ffn: bfloat16 [768], P('dp'), may hold values from -1.75 to 1.75
- rel_table: bfloat16 [32, 12], replicated, may hold values from -4 to 4
- lengths: int32 [16], P('dp'), may hold values from 192 to 512, as said below
- positions: int32 [16, 512], P('dp'), may hold values from 0 to 511, as said below
- predicted: int32 [16, 512], P('dp', 'seq'), may hold values 0 or 1
Outputs:
- y_content: float32 [16, 512, 768], P('dp', 'seq')
- y_query: float32 [16, 512, 768], P('dp', 'seq')
- grad_content: float32 [16, 512, 768], P('dp', 'seq')
- grad_query: float32 [16, 512, 768], P('dp', 'seq')
- grad_w_query: float32 [768, 768], P('dp')
- grad_b_query: float32 [768], P('dp')
- grad_w_key: float32 [768, 768], P('dp')
- grad_w_value: float32 [768, 768], P('dp')
- grad_b_value: float32 [768], P('dp')
- grad_w_out: float32 [768, 768], P('dp')
- grad_b_out: float32 [768], P('dp')
- grad_gain_attn: float32 [768], P('dp')
- grad_shift_attn: float32 [768], P('dp')
- grad_w_up: float32 [768, 3072], P('dp')
- grad_b_up: float32 [3072], P('dp')
- grad_w_down: float32 [3072, 768], P('dp')
- grad_b_down: float32 [768], P('dp')
- grad_gain_ffn: float32 [768], P('dp')
- grad_shift_ffn: float32 [768], P('dp')
- grad_rel_table: float32 [32, 12], replicated
Inputs may be any that keep to these rules, and one draw needn't show every extreme that they name: `lengths`: one sequence of each aligned group of 2 has exactly 512 tokens. `positions`: in row s the slots below lengths[s] hold a permutation of 0 to lengths[s] - 1; the others hold lengths[s] to 511 in order.
All inputs are finite; a program needn't handle non-finite values. No bound on the sum of `predicted` on one device may be relied on, other than what follows from the above.
Results may differ from a plain program's by a relative error of at most 0.018.
Values may be sent and summed in bfloat16 or wider, within the bound.
A program may use at most 192 MiB of HBM per device.

v0:
```python
import jax
import jax.numpy as jnp
from jax import lax
from jax.sharding import PartitionSpec as P

H = 12
HD = 64
NB = 32


bucket_marks = (12, 16, 23, 32, 46, 64, 91)


def bucket_ids(pos_rows, pos_cols):
    delta = pos_cols[..., None, :] - pos_rows[..., :, None]
    dist = jnp.abs(delta)
    far = jnp.full(dist.shape, 8, jnp.int32)
    for mark in bucket_marks:
        far = far + (dist >= mark).astype(jnp.int32)
    near = jnp.where(dist < 8, dist, far)
    return near + 16 * (delta > 0).astype(jnp.int32)


def norm_apply(value, gain, shift):
    center = value - jnp.mean(value, axis=-1, keepdims=True)
    var = jnp.mean(center * center, axis=-1, keepdims=True)
    return center * lax.rsqrt(var + 1e-05) * gain + shift


def per_device(
    x_content,
    x_query,
    cot_content,
    cot_query,
    w_query,
    b_query,
    w_key,
    w_value,
    b_value,
    w_out,
    b_out,
    gain_attn,
    shift_attn,
    w_up,
    b_up,
    w_down,
    b_down,
    gain_ffn,
    shift_ffn,
    rel_table,
    lengths,
    positions,
    predicted,
):
    f32 = jnp.float32
    bf16 = jnp.bfloat16
    scale = HD ** (-0.5)
    seqs, block, width = x_content.shape
    span = positions.shape[1]
    gathered = (
        lax.all_gather(w_query, "dp", axis=0, tiled=True),
        lax.all_gather(b_query, "dp", axis=0, tiled=True),
        lax.all_gather(w_key, "dp", axis=0, tiled=True),
        lax.all_gather(w_value, "dp", axis=0, tiled=True),
        lax.all_gather(b_value, "dp", axis=0, tiled=True),
        lax.all_gather(w_out, "dp", axis=0, tiled=True),
        lax.all_gather(b_out, "dp", axis=0, tiled=True),
        lax.all_gather(gain_attn, "dp", axis=0, tiled=True),
        lax.all_gather(shift_attn, "dp", axis=0, tiled=True),
        lax.all_gather(w_up, "dp", axis=0, tiled=True),
        lax.all_gather(b_up, "dp", axis=0, tiled=True),
        lax.all_gather(w_down, "dp", axis=0, tiled=True),
        lax.all_gather(b_down, "dp", axis=0, tiled=True),
        lax.all_gather(gain_ffn, "dp", axis=0, tiled=True),
        lax.all_gather(shift_ffn, "dp", axis=0, tiled=True),
    )
    wq, bq, wk, wv, bv, wo, bo, g1, b1, w1, c1, w2, c2, g2, b2 = gathered
    base = lax.axis_index("seq") * block
    slot_q = base + jnp.arange(block)
    slot_k = jnp.arange(span)
    valid_k = slot_k[None, :] < lengths[:, None]
    valid_q = slot_q[None, :] < lengths[:, None]
    allow_c = valid_k[:, None, :] & (slot_k[None, :] <= slot_q[:, None])[None]
    allow_q = valid_k[:, None, :] & (slot_k[None, :] < jnp.maximum(slot_q[:, None], 1))[None]
    allowed = jnp.stack([allow_c, allow_q])
    pos_q = lax.dynamic_slice_in_dim(positions, base, block, 1)
    onehot = (bucket_ids(pos_q, positions)[..., None] == jnp.arange(NB)).astype(f32)
    table = rel_table.astype(f32)
    bias = jnp.einsum("sqkn,nh->shqk", onehot, table, precision=lax.Precision.HIGHEST)
    xs = jnp.stack([x_content, x_query])
    key_local = jnp.einsum("sqd,de->sqe", x_content, wk, preferred_element_type=f32).astype(bf16)
    value_local = (
        jnp.einsum("sqd,de->sqe", x_content, wv, preferred_element_type=f32) + bv.astype(f32)
    ).astype(bf16)
    keys, values = (
        lax.all_gather(key_local, "seq", axis=1, tiled=True),
        lax.all_gather(value_local, "seq", axis=1, tiled=True),
    )
    query = (
        jnp.einsum("tsqd,de->tsqe", xs, wq, preferred_element_type=f32) + bq.astype(f32)
    ).astype(bf16)
    query4 = query.reshape(2, seqs, block, H, HD)

    def scores_of(keys_now):
        keys4 = keys_now.reshape(seqs, span, H, HD)
        raw = jnp.einsum("tsqhe,skhe->tshqk", query4, keys4, preferred_element_type=f32)
        return jnp.where(allowed[:, :, None], raw * scale + bias[None], -1e30)

    scores = scores_of(keys)
    top = jnp.max(scores, axis=-1, keepdims=True)
    expo = jnp.exp(scores - top)
    total = jnp.sum(expo, axis=-1, keepdims=True)
    probs = expo / total
    log_total = top + jnp.log(total)
    values4 = values.reshape(seqs, span, H, HD)
    mixed = jnp.einsum("tshqk,skhe->tsqhe", probs.astype(bf16), values4, preferred_element_type=f32)
    attended = mixed.reshape(2, seqs, block, width).astype(bf16)
    out = jnp.einsum("tsqd,de->tsqe", attended, wo, preferred_element_type=f32) + bo.astype(f32)
    resid_one = xs.astype(f32) + out
    hidden, pull_one = jax.vjp(norm_apply, resid_one, g1.astype(f32), b1.astype(f32))
    hidden_low = hidden.astype(bf16)
    upper = jnp.einsum("tsqd,df->tsqf", hidden_low, w1, preferred_element_type=f32) + c1.astype(f32)
    active_full, pull_gelu = jax.vjp(lambda value: jax.nn.gelu(value, approximate=False), upper)
    active = active_full.astype(bf16)
    feed = jnp.einsum("tsqf,fd->tsqd", active, w2, preferred_element_type=f32) + c2.astype(f32)
    result, pull_two = jax.vjp(norm_apply, hidden + feed, g2.astype(f32), b2.astype(f32))
    keep = jnp.stack([valid_q, valid_q & (predicted > 0)])[..., None].astype(f32)
    outputs = result * keep
    cotangent = jnp.stack([cot_content, cot_query]).astype(f32) * keep
    d_resid_two, d_g2, d_b2 = pull_two(cotangent)
    d_c2 = jnp.sum(d_resid_two, axis=(0, 1, 2))
    d_feed_low = d_resid_two.astype(bf16)
    d_w2 = jnp.einsum("tsqf,tsqd->fd", active, d_feed_low, preferred_element_type=f32)
    d_active = jnp.einsum("tsqd,fd->tsqf", d_feed_low, w2, preferred_element_type=f32)
    (d_upper,) = pull_gelu(d_active)
    d_c1 = jnp.sum(d_upper, axis=(0, 1, 2))
    d_upper_low = d_upper.astype(bf16)
    d_w1 = jnp.einsum("tsqd,tsqf->df", hidden_low, d_upper_low, preferred_element_type=f32)
    d_hidden = d_resid_two + jnp.einsum(
        "tsqf,df->tsqd", d_upper_low, w1, preferred_element_type=f32
    )
    d_resid_one, d_g1, d_b1 = pull_one(d_hidden)
    d_bo = jnp.sum(d_resid_one, axis=(0, 1, 2))
    d_out_low = d_resid_one.astype(bf16)
    d_wo = jnp.einsum("tsqd,tsqe->de", attended, d_out_low, preferred_element_type=f32)
    d_attended = jnp.einsum("tsqe,de->tsqd", d_out_low, wo, preferred_element_type=f32).astype(bf16)
    d_mixed = d_attended.reshape(2, seqs, block, H, HD)
    probs_again = jnp.exp(scores_of(keys) - log_total)
    d_probs = jnp.einsum("tsqhe,skhe->tshqk", d_mixed, values4, preferred_element_type=f32)
    d_scores = probs_again * (d_probs - jnp.sum(d_probs * probs_again, axis=-1, keepdims=True))
    d_table = jnp.einsum(
        "shqk,sqkn->nh", jnp.sum(d_scores, axis=0), onehot, precision=lax.Precision.HIGHEST
    )
    d_raw = (d_scores * scale).astype(bf16)
    keys4 = keys.reshape(seqs, span, H, HD)
    d_query = jnp.einsum("tshqk,skhe->tsqhe", d_raw, keys4, preferred_element_type=f32).reshape(
        2, seqs, block, width
    )
    d_keys = jnp.einsum("tshqk,tsqhe->skhe", d_raw, query4, preferred_element_type=f32).reshape(
        seqs, span, width
    )
    d_values = jnp.einsum(
        "tshqk,tsqhe->skhe", probs_again.astype(bf16), d_mixed, preferred_element_type=f32
    ).reshape(seqs, span, width)
    d_key_own, d_value_own = (
        lax.psum_scatter(
            d_keys.astype(jnp.bfloat16), "seq", scatter_dimension=1, tiled=True
        ).astype(jnp.float32),
        lax.psum_scatter(
            d_values.astype(jnp.bfloat16), "seq", scatter_dimension=1, tiled=True
        ).astype(jnp.float32),
    )
    d_bq = jnp.sum(d_query, axis=(0, 1, 2))
    d_query_low = d_query.astype(bf16)
    d_wq = jnp.einsum("tsqd,tsqe->de", xs, d_query_low, preferred_element_type=f32)
    d_bv = jnp.sum(d_value_own, axis=(0, 1))
    d_key_low = d_key_own.astype(bf16)
    d_value_low = d_value_own.astype(bf16)
    d_wk = jnp.einsum("sqd,sqe->de", x_content, d_key_low, preferred_element_type=f32)
    d_wv = jnp.einsum("sqd,sqe->de", x_content, d_value_low, preferred_element_type=f32)
    d_inputs = d_resid_one + jnp.einsum(
        "tsqe,de->tsqd", d_query_low, wq, preferred_element_type=f32
    )
    grad_content = (
        d_inputs[0]
        + jnp.einsum("sqe,de->sqd", d_key_low, wk, preferred_element_type=f32)
        + jnp.einsum("sqe,de->sqd", d_value_low, wv, preferred_element_type=f32)
    )
    grad_query = d_inputs[1]
    shards = (
        lax.psum_scatter(d_wq, "dp", scatter_dimension=0, tiled=True),
        lax.psum_scatter(d_bq, "dp", scatter_dimension=0, tiled=True),
        lax.psum_scatter(d_wk, "dp", scatter_dimension=0, tiled=True),
        lax.psum_scatter(d_wv, "dp", scatter_dimension=0, tiled=True),
        lax.psum_scatter(d_bv, "dp", scatter_dimension=0, tiled=True),
        lax.psum_scatter(d_wo, "dp", scatter_dimension=0, tiled=True),
        lax.psum_scatter(d_bo, "dp", scatter_dimension=0, tiled=True),
        lax.psum_scatter(d_g1, "dp", scatter_dimension=0, tiled=True),
        lax.psum_scatter(d_b1, "dp", scatter_dimension=0, tiled=True),
        lax.psum_scatter(d_w1, "dp", scatter_dimension=0, tiled=True),
        lax.psum_scatter(d_c1, "dp", scatter_dimension=0, tiled=True),
        lax.psum_scatter(d_w2, "dp", scatter_dimension=0, tiled=True),
        lax.psum_scatter(d_c2, "dp", scatter_dimension=0, tiled=True),
        lax.psum_scatter(d_g2, "dp", scatter_dimension=0, tiled=True),
        lax.psum_scatter(d_b2, "dp", scatter_dimension=0, tiled=True),
    )
    summed = (
        lax.psum(shards[0].astype(jnp.bfloat16), "seq").astype(jnp.float32),
        lax.psum(shards[1].astype(jnp.bfloat16), "seq").astype(jnp.float32),
        lax.psum(shards[2].astype(jnp.bfloat16), "seq").astype(jnp.float32),
        lax.psum(shards[3].astype(jnp.bfloat16), "seq").astype(jnp.float32),
        lax.psum(shards[4].astype(jnp.bfloat16), "seq").astype(jnp.float32),
        lax.psum(shards[5].astype(jnp.bfloat16), "seq").astype(jnp.float32),
        lax.psum(shards[6].astype(jnp.bfloat16), "seq").astype(jnp.float32),
        lax.psum(shards[7].astype(jnp.bfloat16), "seq").astype(jnp.float32),
        lax.psum(shards[8].astype(jnp.bfloat16), "seq").astype(jnp.float32),
        lax.psum(shards[9].astype(jnp.bfloat16), "seq").astype(jnp.float32),
        lax.psum(shards[10].astype(jnp.bfloat16), "seq").astype(jnp.float32),
        lax.psum(shards[11].astype(jnp.bfloat16), "seq").astype(jnp.float32),
        lax.psum(shards[12].astype(jnp.bfloat16), "seq").astype(jnp.float32),
        lax.psum(shards[13].astype(jnp.bfloat16), "seq").astype(jnp.float32),
        lax.psum(shards[14].astype(jnp.bfloat16), "seq").astype(jnp.float32),
    )
    table_total = lax.psum(d_table, ("dp", "seq"))
    return (
        outputs[0],
        outputs[1],
        grad_content,
        grad_query,
        summed[0],
        summed[1],
        summed[2],
        summed[3],
        summed[4],
        summed[5],
        summed[6],
        summed[7],
        summed[8],
        summed[9],
        summed[10],
        summed[11],
        summed[12],
        summed[13],
        summed[14],
        table_total,
    )


def solution(mesh):
    in_specs = (
        P("dp", "seq", None),
        P("dp", "seq", None),
        P("dp", "seq", None),
        P("dp", "seq", None),
        P("dp", None),
        P("dp"),
        P("dp", None),
        P("dp", None),
        P("dp"),
        P("dp", None),
        P("dp"),
        P("dp"),
        P("dp"),
        P("dp", None),
        P("dp"),
        P("dp", None),
        P("dp"),
        P("dp"),
        P("dp"),
        P(),
        P("dp"),
        P("dp", None),
        P("dp", "seq"),
    )
    out_specs = (
        P("dp", "seq", None),
        P("dp", "seq", None),
        P("dp", "seq", None),
        P("dp", "seq", None),
        P("dp", None),
        P("dp"),
        P("dp", None),
        P("dp", None),
        P("dp"),
        P("dp", None),
        P("dp"),
        P("dp"),
        P("dp"),
        P("dp", None),
        P("dp"),
        P("dp", None),
        P("dp"),
        P("dp"),
        P("dp"),
        P(),
    )
    return jax.shard_map(
        per_device, mesh=mesh, in_specs=in_specs, out_specs=out_specs, check_vma=False
    )
```

profile of v0, /device:TPU:1, one launch (start us, length us, event | category | flops | bytes accessed | tf_op | source)
XLA Modules:
  0.0 1197.8 jit_solution(14665695956869375109)
XLA Ops:
  9.5 42.6 %all-gather.14.cloned.1.call-done = bf16[768,768]{1,0:T(8,128)(2,1)} async-done(((bf16[96,768]{1,0:T(8,128)(2,1)}), bf16[768,768]{1,0:T(8,128)(2,1)}) %all-gather.14.cloned.1.call-update) | async-done | bytes 1179664 | tf_op jit(solution)/shard_map/all_gather | solution.py:63
  52.1 2.6 convolution_convert_fusion.1
  63.5 28.1 %all-reduce.18 = (bf16[768]{0:T(1024)(128)(2,1)S(1)}, bf16[768]{0:T(1024)(128)(2,1)S(1)}, bf16[768]{0:T(1024)(128)(2,1)S(1)}, bf16[768]{0:T(1024)(128)(2,1)S(1)}...) all-reduce(bf16[768]{0:T(1024)(128)(2,1)S(1)} %dynamic-update-slice, ...), channel_id=1, replica_groups=mesh['dp'=8,'seq'=4] {'dp'}, use_global_device_ids=true, to_apply=%add.1 | all-reduce | flops 6144 | bytes 24576
  91.6 2.8 all-gather.10.cloned.1.call-done
  94.4 2.6 fusion.45
  100.1 21.8 %all-gather = bf16[8,1,384]{2,1,0:T(2,128)(2,1)S(1)} all-gather(bf16[1,1,384]{2,1,0:T(2,128)(2,1)S(1)} %reshape.338), channel_id=1, replica_groups=mesh['dp'=8,'seq'=4] {'dp'}, dimensions={0}, use_global_device_ids=true | all-gather | bytes 6912 | tf_op jit(solution)/shard_map/all_gather | solution.py:71
  123.3 2.3 iota_compare_fusion
  125.6 74.6 %copy.168 = pred[2,128,512,32]{2,3,1,0:T(32,128)(4,1)S(1)} copy(pred[2,128,512,32]{1,3,0,2:T(32,128)(4,1)S(1)} %iota_compare_fusion) | data formatting | bytes 8388608 | tf_op jit(solution)/shard_map/eq | solution.py:87
  200.3 5.3 convolution_bitcast_fusion.2
  205.5 9.2 copy.169
  217.5 2.1 add_convert_fusion
  220.0 2.0 copy.164
  222.0 4.7 fusion.90
  226.8 4.5 copy-done.2
  231.3 3.6 fusion.3
  234.9 2.1 copy.163
  237.0 7.6 fusion.43
  245.5 2.6 fusion.91
  250.8 52.1 %all-gather.22.cloned.1.call-done = bf16[768,3072]{1,0:T(8,128)(2,1)} async-done(((bf16[96,3072]{1,0:T(8,128)(2,1)}), bf16[768,3072]{1,0:T(8,128)(2,1)}) %all-gather.22.cloned.1.call-update) | async-done | bytes 4718608 | tf_op jit(solution)/shard_map/all_gather | solution.py:70
  302.9 7.0 fusion.36
  309.9 2.6 copy-done.6
  312.5 15.9 %multiply_convert_fusion.1 = (bf16[2,2,128,3072]{3,2,1,0:T(8,128)(2,1)}, f32[2,2,128,3072]{3,2,1,0:T(8,128)}) fusion(f32[2,2,128,3072]{3,2,1,0:T(8,128)S(1)} %get-tuple-element.187, f32[3072]{0:T(1024)S(1)} %bitcast.239, u8[2,128,3072]{2,1,0:T(8,128)(4,1)S(1)} %get-tuple-element.121, u8[2,128,3072]{2,1,0:T(8,128)(4,1)S(1)} %get-tuple-element.120), kind=kLoop, calls=%fused_computation.27 | loop fusion | flops 111673344 | bytes 17313792 | tf_op jit(solution)/shard_map/convert_element_type | solution.py:124
  328.4 54.7 %all-gather.24.cloned.1.call-done = bf16[3072,768]{1,0:T(8,128)(2,1)} async-done(((bf16[384,768]{1,0:T(8,128)(2,1)}), bf16[3072,768]{1,0:T(8,128)(2,1)}) %all-gather.24.cloned.1.call-update) | async-done | bytes 4718608 | tf_op jit(solution)/shard_map/all_gather | solution.py:72
  383.1 6.3 fusion.92
  391.4 2.6 multiply_reduce_fusion
  394.0 8.8 fusion.88
  402.9 7.3 multiply_reduce_fusion.1
  414.8 2.3 copy.173
  417.1 18.4 %fusion.87 = (f32[2,12,128,512]{2,3,1,0:T(8,128)}, bf16[2,2,12,128,512]{3,4,0,2,1:T(8,128)(2,1)}) fusion(f32[2,2,12,128,512]{3,4,0,2,1:T(8,128)} %copy-done.2, f32[2,2,12,128]{3,0,2,1:T(2,128)} %bitcast.236, bf16[2,512,12,64,1]{1,3,4,2,0:T(8,128)(2,1)} %bitcast.226, bf16[2,2,128,12,64]{2,4,3,1,0:T(8,128)(2,1)} %bitcast.223), kind=kOutput, calls=%fused_computation.171 | convolution fusion | flops 828905984 | bytes 27549696 | tf_op jit(solution)/shard_map/sub | solution.py:150
  435.5 5.0 fusion.10
  441.9 5.0 copy.231
  446.9 2.8 copy.239
  449.8 6.8 fusion.8
  458.0 5.0 copy.233
  463.0 2.8 copy.240
  465.9 5.2 bitcast_convert_fusion.2
  472.0 2.3 convolution_bitcast_fusion.6
  474.4 2.3 convolution_bitcast_fusion.3
  478.8 1.9 convolution_bitcast_fusion.5
  480.7 3.1 copy.235
  483.8 24.2 %reduce-scatter.27.cloned.1.call-done = bf16[128,1536]{1,0:T(8,128)(2,1)} async-done(((bf16[512,1536]{1,0:T(8,128)(2,1)}), bf16[128,1536]{1,0:T(8,128)(2,1)}) %reduce-scatter.27.cloned.1.call-update) | async-done | bytes 393232
  509.6 1.9 convolution_bitcast_fusion.4
  511.5 3.1 copy.237
  514.7 7.5 convolution_bitcast_fusion.1
  522.2 1.8 copy-done.23
  524.1 6.3 convolution_bitcast_fusion
  532.7 13.1 %fusion.56 = f32[32,12]{0,1:T(8,128)S(1)} fusion(f32[2,12,128,512]{2,3,1,0:T(8,128)} %get-tuple-element.167, s32[2,128,512]{1,0,2:T(2,128)S(1)} %copy-done.15), kind=kOutput, calls=%fused_computation.108 | convolution fusion | flops 608174080 | bytes 6817280 | tf_op jit(solution)/shard_map/shqk,sqkn->nh/dot_general | solution.py:151
  545.8 39.4 %psum.127 = f32[32,12]{0,1:T(8,128)} all-reduce(f32[32,12]{0,1:T(8,128)S(1)} %fusion.56), channel_id=1, replica_groups=mesh['dp'=8,'seq'=4] {'dp','seq'}, use_global_device_ids=true, to_apply=%region_53.54 | all-reduce | flops 384 | bytes 3072 | tf_op jit(solution)/shard_map/psum | solution.py:224
  586.6 3.3 convolution_add_fusion
  591.5 59.7 %reduce-scatter.19.cloned.1.call-done = f32[96,768]{1,0:T(8,128)} async-done(((f32[768,768]{1,0:T(8,128)}), f32[96,768]{1,0:T(8,128)}) %reduce-scatter.19.cloned.1.call-update) | async-done | bytes 294928 | tf_op jit(solution)/shard_map/reduce_scatter | solution.py:196
  652.9 69.8 %reduce-scatter.29.cloned.1.call-done = f32[96,768]{1,0:T(8,128)} async-done(((f32[768,768]{1,0:T(8,128)}), f32[96,768]{1,0:T(8,128)}) %reduce-scatter.29.cloned.1.call-update) | async-done | bytes 294928
  722.7 1.8 copy.236
  724.5 69.6 %reduce-scatter.31.cloned.1.call-done = f32[96,768]{1,0:T(8,128)} async-done(((f32[768,768]{1,0:T(8,128)}), f32[96,768]{1,0:T(8,128)}) %reduce-scatter.31.cloned.1.call-update) | async-done | bytes 294928
  794.1 1.8 copy.238
  795.9 165.1 %reduce-scatter.21.cloned.1.call-done = f32[96,3072]{1,0:T(8,128)} async-done(((f32[768,3072]{1,0:T(8,128)}), f32[96,3072]{1,0:T(8,128)}) %reduce-scatter.21.cloned.1.call-update) | async-done | bytes 1179664 | tf_op jit(solution)/shard_map/reduce_scatter | solution.py:200
  961.0 2.2 convert_element_type.319
  963.1 163.7 %reduce-scatter.23.cloned.1.call-done = f32[384,768]{1,0:T(8,128)} async-done(((f32[3072,768]{1,0:T(8,128)}), f32[384,768]{1,0:T(8,128)}) %reduce-scatter.23.cloned.1.call-update) | async-done | bytes 1179664 | tf_op jit(solution)/shard_map/reduce_scatter | solution.py:202
  1126.9 2.1 convert_element_type.323
  1130.2 29.1 %all-reduce.17 = (bf16[768]{0:T(1024)(128)(2,1)S(1)}, bf16[768]{0:T(1024)(128)(2,1)S(1)}, bf16[768]{0:T(1024)(128)(2,1)S(1)}, bf16[768]{0:T(1024)(128)(2,1)S(1)}...) all-reduce(f32[768]{0:T(1024)S(1)} %copy-done.44, ...), channel_id=5, replica_groups=mesh['dp'=8,'seq'=4] {'dp'}, use_global_device_ids=true, to_apply=%region_16.17.clone | all-reduce | flops 9216 | bytes 55296
  1160.0 12.9 %all-reduce.19 = (bf16[96]{0:T(256)(128)(2,1)S(1)}, bf16[96]{0:T(256)(128)(2,1)S(1)}, bf16[96]{0:T(256)(128)(2,1)S(1)}, bf16[96]{0:T(256)(128)(2,1)S(1)}, bf16[9...) all-reduce(bf16[96]{0:T(256)(128)(2,1)S(1)} %dynamic-slice.43, ...), channel_id=1, replica_groups=mesh['dp'=8,'seq'=4] {'seq'}, use_global_device_ids=true, to_apply=%region_17.18 | all-reduce | flops 1152 | bytes 4608 | tf_op jit(solution)/shard_map/psum | solution.py:209
  1180.7 1.7 convert_element_type.301
  1182.4 1.8 copy.195
  1184.2 1.8 copy.196
  1187.6 2.2 convert_element_type.320
  (245 shorter events, 53.5 us)
Async XLA Ops:
  7.2 193.1 %copy-start = (bf16[32,12]{0,1:T(8,128)(2,1)S(1)}, bf16[32,12]{0,1:T(8,128)(2,1)}, u32[]{:S(2)}) copy-start(bf16[32,12]{0,1:T(8,128)(2,1)} %param.42) | copy-start | bytes 2308
  7.2 44.9 %all-gather.14.cloned.1.call-start = ((), (), s32[]{:S(2)}) async-start(), calls=%async_computation.10 | async-start | bytes 1327104 | tf_op jit(solution)/shard_map/all_gather | solution.py:63
  7.9 86.5 %all-gather.10.cloned.1.call-start = ((), (), s32[]{:S(2)}) async-start(), calls=%async_computation.8 | async-start | bytes 1327104 | tf_op jit(solution)/shard_map/all_gather | solution.py:64
  8.7 208.8 %all-gather.18.cloned.1.call-start = ((), (), s32[]{:S(2)}) async-start(), calls=%async_computation.12 | async-start | bytes 1327104 | tf_op jit(solution)/shard_map/all_gather | solution.py:61
  9.4 89.9 %copy-start.54 = (s32[2]{0:T(128)S(1)}, s32[2]{0:T(128)}, u32[]{:S(2)}) copy-start(s32[2]{0:T(128)} %param.43) | copy-start | bytes 28
  9.4 90.6 %copy-start.55 = (bf16[384]{0:T(512)(128)(2,1)S(1)}, bf16[384]{0:T(512)(128)(2,1)}, u32[]{:S(2)}) copy-start(bf16[384]{0:T(512)(128)(2,1)} %param.37) | copy-start | bytes 2308
  9.4 113.0 %copy-start.52 = (s32[2,512]{1,0:T(2,128)S(1)}, s32[2,512]{1,0:T(2,128)}, u32[]{:S(2)}) copy-start(s32[2,512]{1,0:T(2,128)} %param.44) | copy-start | bytes 12292
  9.5 210.5 %all-gather.16.cloned.1.call-start = ((), (), s32[]{:S(2)}) async-start(), calls=%async_computation.11 | async-start | bytes 1966080 | tf_op jit(solution)/shard_map/all_gather | solution.py:96
  54.8 180.1 %all-gather.12.cloned.1.call-start = ((), (), s32[]{:S(2)}) async-start(), calls=%async_computation.9 | async-start | bytes 1966080 | tf_op jit(solution)/shard_map/all_gather | solution.py:97
  97.1 148.4 %all-gather.20.cloned.1.call-start = ((), (), s32[]{:S(2)}) async-start(), calls=%async_computation.13 | async-start | bytes 1327104 | tf_op jit(solution)/shard_map/all_gather | solution.py:66
  97.7 205.2 %all-gather.22.cloned.1.call-start = ((), (), s32[]{:S(2)}) async-start(), calls=%async_computation.14 | async-start | bytes 5308416 | tf_op jit(solution)/shard_map/all_gather | solution.py:70
  98.4 284.7 %all-gather.24.cloned.1.call-start = ((), (), s32[]{:S(2)}) async-start(), calls=%async_computation.15 | async-start | bytes 5308416 | tf_op jit(solution)/shard_map/all_gather | solution.py:72
  99.2 378.0 %reduce-scatter.25.cloned.1.call-start = ((), (), s32[]{:S(2)}) async-start(), calls=%async_computation.20 | async-start | bytes 1966080
  123.3 77.0 %copy-start.14 = (s32[2,128,512]{1,0,2:T(2,128)}, s32[2,128,512]{1,0,2:T(2,128)S(1)}, u32[]{:S(2)}) copy-start(s32[2,128,512]{1,0,2:T(2,128)S(1)} %copy.167) | copy-start | bytes 1572868
  205.5 10.5 copy-start.56
  205.5 12.0 copy-start.12
  205.5 12.0 copy-start.32
  219.9 6.8 copy-start.4
  226.7 4.5 copy-start.2
  226.8 8.1 copy-start.34
  237.0 7.6 copy-start.24
  245.5 4.6 copy-start.35
  245.5 4.6 copy-start.36
  309.9 2.6 copy-start.6
  383.1 6.3 copy-start.19
  383.1 6.3 copy-start.20
  383.1 6.3 copy-start.37
  383.1 10.9 copy-start.8
  390.1 3.9 copy-start.7
  394.0 8.9 copy-start.30
  394.0 8.9 copy-start.39
  394.0 8.9 copy-start.45
  394.0 8.9 copy-start.48
  402.9 7.3 copy-start.42
  410.2 3.0 copy-start.27
  410.8 6.3 copy-start.50
  449.7 58.2 %reduce-scatter.27.cloned.1.call-start = ((), (), s32[]{:S(2)}) async-start(), calls=%async_computation.21 | async-start | bytes 1966080
  465.8 124.1 %reduce-scatter.17.cloned.1.call-start = ((), (), s32[]{:S(2)}) async-start(), calls=%async_computation.16 | async-start | bytes 2654208 | tf_op jit(solution)/shard_map/reduce_scatter | solution.py:191
  465.8 6.2 copy-start.33
  472.0 2.4 copy-start.5
  472.0 2.4 copy-start.22
  474.4 176.9 %reduce-scatter.19.cloned.1.call-start = ((), (), s32[]{:S(2)}) async-start(), calls=%async_computation.17 | async-start | bytes 2654208 | tf_op jit(solution)/shard_map/reduce_scatter | solution.py:196
  476.7 246.0 %reduce-scatter.29.cloned.1.call-start = ((), (), s32[]{:S(2)}) async-start(), calls=%async_computation.22 | async-start | bytes 2654208
  483.7 25.8 %copy-start.13 = (bf16[2,128,768]{2,1,0:T(8,128)(2,1)S(1)}, bf16[2,128,768]{2,1,0:T(8,128)(2,1)}, u32[]{:S(2)}) copy-start(bf16[2,128,768]{2,1,0:T(8,128)(2,1)} %param.23) | copy-start | bytes 1179652
  483.8 310.3 %reduce-scatter.31.cloned.1.call-start = ((), (), s32[]{:S(2)}) async-start(), calls=%async_computation.23 | async-start | bytes 2654208
  511.5 3.2 copy-start.40
  511.5 3.2 copy-start.46
  511.5 3.2 copy-start.49
  511.5 3.2 copy-start.53
  514.6 446.4 %reduce-scatter.21.cloned.1.call-start = ((), (), s32[]{:S(2)}) async-start(), calls=%async_computation.18 | async-start | bytes 10616832 | tf_op jit(solution)/shard_map/reduce_scatter | solution.py:200
  522.2 604.7 %reduce-scatter.23.cloned.1.call-start = ((), (), s32[]{:S(2)}) async-start(), calls=%async_computation.19 | async-start | bytes 10616832 | tf_op jit(solution)/shard_map/reduce_scatter | solution.py:202
  530.3 2.4 copy-start.15
  530.4 650.3 %all-reduce.23.cloned.1.call-start = ((), (), s32[]{:S(2)}) async-start(), calls=%async_computation.24 | async-start | bytes 3735552 | tf_op jit(solution)/shard_map/psum | solution.py:210
  532.7 52.5 %copy-start.9 = (f32[2,2,128,768]{3,2,1,0:T(8,128)S(1)}, f32[2,2,128,768]{3,2,1,0:T(8,128)}, u32[]{:S(2)}) copy-start(f32[2,2,128,768]{3,2,1,0:T(8,128)} %get-tuple-element.172) | copy-start | bytes 4718596
  545.8 40.7 %copy-start.11 = (f32[2,2,128,768]{3,2,1,0:T(8,128)S(1)}, f32[2,2,128,768]{3,2,1,0:T(8,128)}, u32[]{:S(2)}) copy-start(f32[2,2,128,768]{3,2,1,0:T(8,128)} %copy-done.10) | copy-start | bytes 4718596
  545.8 40.7 %copy-start.51 = (f32[2,2,128]{2,1,0:T(2,128)S(1)}, f32[2,2,128]{2,1,0:T(2,128)}, u32[]{:S(2)}) copy-start(f32[2,2,128]{2,1,0:T(2,128)} %copy-done.50) | copy-start | bytes 6148
  652.9 476.2 %copy-start.25 = (f32[2,2,128,768]{3,2,1,0:T(8,128)S(1)}, f32[2,2,128,768]{3,2,1,0:T(8,128)}, u32[]{:S(2)}) copy-start(f32[2,2,128,768]{3,2,1,0:T(8,128)} %convolution_add_fusion) | copy-start | bytes 4718596
  963.1 167.0 %copy-start.43 = (f32[768]{0:T(1024)S(1)}, f32[768]{0:T(1024)}, u32[]{:S(2)}) copy-start(f32[768]{0:T(1024)} %get-tuple-element.129) | copy-start | bytes 9220
  963.1 167.0 %copy-start.44 = (f32[768]{0:T(1024)S(1)}, f32[768]{0:T(1024)}, u32[]{:S(2)}) copy-start(f32[768]{0:T(1024)} %reduce_sum.225) | copy-start | bytes 9220
  963.1 214.5 %copy-start.16 = (bf16[768,768]{1,0:T(8,128)(2,1)S(1)}, bf16[768,768]{1,0:T(8,128)(2,1)}, u32[]{:S(2)}) copy-start(bf16[768,768]{1,0:T(8,128)(2,1)} %all-gather.14.cloned.1.call-done) | copy-start | bytes 3538948
  963.1 214.5 %copy-start.18 = (bf16[2,128,768]{1,2,0:T(8,128)(2,1)S(1)}, bf16[2,128,768]{1,2,0:T(8,128)(2,1)}, u32[]{:S(2)}) copy-start(bf16[2,128,768]{1,2,0:T(8,128)(2,1)} %copy-done.17) | copy-start | bytes 1179652
  1172.9 6.4 copy-start.26
  1179.3 11.6 copy-start.1
  1180.7 9.1 copy-start.31
  (10 other events, 12.8 us)
Sparse Core Ops, SparseCore 0:
  10.2 41.8 all-gather.13
  54.3 40.0 all-gather.9
  96.6 39.8 all-gather.17
  138.5 20.0 all-gather.15
  160.6 19.6 all-gather.11
  182.3 39.3 all-gather.19
  223.9 78.9 all-gather.21
  305.0 78.0 all-gather.23
  449.9 27.3 reduce-scatter.24
  479.8 28.1 reduce-scatter.26
  511.5 68.4 reduce-scatter.16
  583.3 67.9 reduce-scatter.18
  654.7 67.9 reduce-scatter.28
  726.0 68.0 reduce-scatter.30
  797.5 163.3 reduce-scatter.20
  964.4 162.4 reduce-scatter.22
  1130.6 47.4 all-reduce.22
where the time goes:
time: 1210 us; the launch traced here: 1200 us
  waiting for transfers between devices  709 us (59%)
  local copies, waits for them, and re-layouts  151 us (12%)
  matrix products  136 us (11%)
  blocking collectives  131 us (11%)
  other arithmetic  52.6 us (4%)
  between operations  17.3 us (1%)
    unnamed x21, waiting for transfers between devices  168 us
    reduce_scatter x1, waiting for transfers between devices, per_device(): lax.psum_scatter(d_w1, 'dp', scatter_dimension=0, tiled=True)  165 us
    reduce_scatter x1, waiting for transfers between devices, per_device(): lax.psum_scatter(d_w2, 'dp', scatter_dimension=0, tiled=True)  164 us
    eq x1, local copies, waits for them, and re-layouts, per_device(): bucket_ids(pos_q, positions)[..., None] == jnp.arange(NB)  74.6 us
    reduce_scatter x1, waiting for transfers between devices, per_device(): lax.psum_scatter(d_wo, 'dp', scatter_dimension=0, tiled=True)  59.7 us
    unnamed x2, blocking collectives  57.2 us
    all_gather x1, waiting for transfers between devices, per_device(): lax.all_gather(w_down, 'dp', axis=0, tiled=True)  54.7 us
    unnamed x155, local copies, waits for them, and re-layouts  54 us
  transfers between devices with their start and end apart: 17, of which 11 were waited for; matrix products, arithmetic and copies ran while one was open for 21% of the time, Pallas kernels for 0%

commit v1 on v0

v1 whole, which is shorter than its diff:
```python
import functools

import jax
import jax.numpy as jnp
from jax import lax
from jax.experimental import pallas as pl
from jax.experimental.pallas import tpu as pltpu
from jax.sharding import PartitionSpec as P

H = 12
HD = 64
NB = 32

bucket_marks = (12, 16, 23, 32, 46, 64, 91)


def bucket_ids(pos_rows, pos_cols):
    delta = pos_cols[..., None, :] - pos_rows[..., :, None]
    dist = jnp.abs(delta)
    far = jnp.full(dist.shape, 8, jnp.int32)
    for mark in bucket_marks:
        far = far + (dist >= mark).astype(jnp.int32)
    near = jnp.where(dist < 8, dist, far)
    return near + 16 * (delta > 0).astype(jnp.int32)


def norm_apply(value, gain, shift):
    center = value - jnp.mean(value, axis=-1, keepdims=True)
    var = jnp.mean(center * center, axis=-1, keepdims=True)
    return center * lax.rsqrt(var + 1e-05) * gain + shift


MESH = pl.DeviceIdType.MESH
UNITS = 12
SKEW = 128


def place(mesh_sizes):
    dp, sq = lax.axis_index("dp"), lax.axis_index("seq")
    row, side = dp // 2, dp % 2
    deck, core = sq // 2, sq % 2
    return dp, sq, row, side, deck, core


def tile_of(unit, shard, shards):
    down = unit // 8
    return (1 - down) * (unit * shards + shard) + down * (8 * shards + shard * 4 + unit - 8)


def gather_kernel(
    shards, seqn,
    wq, wk, wv, wo, wu, wd, xc, vec,
    full, xall, vall,
    own, xown, load_sem, keep_sem, zup_sem, zdn_sem, xs_sem, ys_sem, cp_sem, cy_sem,
    zr_sem, xr_sem, yr_sem, cpr_sem, cyr_sem, xc_send, xc_recv, vec_send, vec_recv,
):
    dp, sq, row, side, deck, core = place(None)
    rows = shards // 2
    up = ((row + 1) * 2 + side, sq)
    down = ((row - 1) * 2 + side, sq)
    across = (row * 2 + 1 - side, sq)
    other_deck = (dp, (1 - deck) * 2 + core)
    sibling = (dp, deck * 2 + 1 - core)

    barrier = pltpu.get_barrier_semaphore()

    def greet(step, carry):
        pl.semaphore_signal(barrier, inc=1, device_id=(lax.rem(dp + step, shards), sq), device_id_type=MESH)
        return carry

    lax.fori_loop(1, shards, greet, 0)
    pl.semaphore_signal(barrier, inc=1, device_id=other_deck, device_id_type=MESH)
    pl.semaphore_signal(barrier, inc=1, device_id=sibling, device_id_type=MESH)

    pieces = [wq, wk, wv, wo] + [wu.at[:, pl.ds(j * 768, 768)] for j in range(4)] + [wd.at[j] for j in range(4)]
    loads = [pltpu.make_async_copy(piece, own.at[u], load_sem.at[u]) for u, piece in enumerate(pieces)]
    for load in loads:
        load.start()
    xload = pltpu.make_async_copy(xc, xown, load_sem.at[UNITS])
    xload.start()
    pl.semaphore_wait(barrier, shards + 1)

    plane = pl.ds(pl.multiple_of(core * 384 + deck * SKEW, 128), 256)
    solo = pl.ds(pl.multiple_of(core * 384 + deck * 256, 128), 128)

    def remote(src, dst, send, recv, device):
        return pltpu.make_async_remote_copy(
            src_ref=src, dst_ref=dst, send_sem=send, recv_sem=recv, device_id=device, device_id_type=MESH
        )

    def part(unit, shard, columns):
        return full.at[tile_of(unit, shard, shards), :, columns]

    def vec_copy(step):
        return remote(vec, vall.at[dp], vec_send, vec_recv, (lax.rem(dp + step, shards), sq))

    def send_vec(step, carry):
        vec_copy(step).start()
        return carry

    lax.fori_loop(1, shards, send_vec, 0)
    keep_vec = pltpu.make_async_copy(vec, vall.at[dp], keep_sem.at[UNITS + 1])
    keep_vec.start()

    for load in loads:
        load.wait()

    def keep_copy(u):
        return pltpu.make_async_copy(own.at[u], full.at[tile_of(u, dp, shards)], keep_sem.at[u])

    def first(u, carry):
        src = own.at[u, :, plane]
        dst = part(u, dp, plane)
        recv = zr_sem.at[u, row]

        @pl.when(row < rows - 1)
        def _():
            remote(src, dst, zup_sem.at[row], recv, up).start()

        @pl.when(row > 0)
        def _():
            remote(src, dst, zdn_sem.at[row], recv, down).start()

        remote(src, dst, xs_sem, xr_sem.at[u], across).start()
        keep_copy(u).start()
        return carry

    lax.fori_loop(0, UNITS, first, 0)

    xload.wait()
    keep_x = pltpu.make_async_copy(xown, xall.at[sq], keep_sem.at[UNITS])
    keep_x.start()
    x_deck = remote(xown, xall.at[sq], xc_send.at[0], xc_recv.at[0], other_deck)
    x_deck.start()
    x_core = remote(xown, xall.at[sq], xc_send.at[1], xc_recv.at[1], sibling)
    x_core.start()

    def to_deck(u, shard):
        ref = part(u, shard, solo)
        remote(ref, ref, ys_sem, yr_sem.at[u], other_deck).start()

    def to_core(u, shard):
        ref = part(u, shard, plane)
        remote(ref, ref, cp_sem, cpr_sem.at[u], sibling).start()

    def step(n, carry):
        def hop(t, inner):
            u = n - (t - 1)

            @pl.when((u >= 0) & (u < UNITS))
            def _():
                @pl.when(row - t >= 0)
                def _():
                    s = row - t
                    ref = part(u, s * 2 + side, plane)
                    remote(ref, ref, zup_sem.at[s], zr_sem.at[u, s], up).wait_recv()

                    @pl.when(row < rows - 1)
                    def _():
                        remote(ref, ref, zup_sem.at[s], zr_sem.at[u, s], up).start()

                    remote(ref, ref, xs_sem, xr_sem.at[u], across).start()
                    to_deck(u, s * 2 + side)
                    to_core(u, s * 2 + side)

                @pl.when(row + t < rows)
                def _():
                    s = row + t
                    ref = part(u, s * 2 + side, plane)
                    remote(ref, ref, zdn_sem.at[s], zr_sem.at[u, s], down).wait_recv()

                    @pl.when(row > 0)
                    def _():
                        remote(ref, ref, zdn_sem.at[s], zr_sem.at[u, s], down).start()

                    remote(ref, ref, xs_sem, xr_sem.at[u], across).start()
                    to_deck(u, s * 2 + side)
                    to_core(u, s * 2 + side)

            return inner

        lax.fori_loop(1, rows, hop, 0)

        ux = n - (rows - 1)

        @pl.when((ux >= 0) & (ux < UNITS))
        def _():
            whole = full.at[pl.ds(0, rows), :, pl.ds(0, 256)]
            remote(whole, whole, xs_sem, xr_sem.at[ux], across).wait_recv()

            def pass_on(s, inner):
                to_deck(ux, s * 2 + 1 - side)
                to_core(ux, s * 2 + 1 - side)
                return inner

            lax.fori_loop(0, rows, pass_on, 0)

        uy = n - rows

        @pl.when((uy >= 0) & (uy < UNITS))
        def _():
            whole = full.at[pl.ds(0, shards - 1), :, pl.ds(0, 128)]
            remote(whole, whole, ys_sem, yr_sem.at[uy], other_deck).wait_recv()
            theirs = pl.ds(pl.multiple_of(core * 384 + (1 - deck) * 256, 128), 128)

            def pass_on(k, inner):
                ref = part(uy, lax.rem(dp + k, shards), theirs)
                remote(ref, ref, cy_sem, cyr_sem.at[uy], sibling).start()
                return inner

            lax.fori_loop(1, shards, pass_on, 0)

        return carry

    lax.fori_loop(0, UNITS + rows, step, 0)

    x_theirs = xall.at[(1 - deck) * 2 + core]
    x_deck.wait_recv()
    x_forward = remote(x_theirs, x_theirs, xc_send.at[2], xc_recv.at[2], sibling)
    x_forward.start()

    def finish(u, carry):
        planes = full.at[pl.ds(0, shards - 1), :, pl.ds(0, 256)]
        solos = full.at[pl.ds(0, shards - 1), :, pl.ds(0, 128)]
        remote(planes, planes, cp_sem, cpr_sem.at[u], sibling).wait_recv()
        remote(solos, solos, cy_sem, cyr_sem.at[u], sibling).wait_recv()
        keep_copy(u).wait()
        return carry

    lax.fori_loop(0, UNITS, finish, 0)
    x_deck.wait_send()
    x_core.wait()
    x_forward.wait()
    keep_x.wait()
    keep_vec.wait()
    rest = vall.at[pl.ds(0, shards - 1)]
    remote(rest, rest, vec_send, vec_recv, sibling).wait()

    def sent(s, carry):
        ref = full.at[pl.ds(0, UNITS), :, pl.ds(0, 256)]

        @pl.when((s <= row) & (row < rows - 1))
        def _():
            remote(ref, ref, zup_sem.at[s], zr_sem.at[0, 0], sibling).wait_send()

        @pl.when((s >= row) & (row > 0))
        def _():
            remote(ref, ref, zdn_sem.at[s], zr_sem.at[0, 0], sibling).wait_send()

        return carry

    lax.fori_loop(0, rows, sent, 0)
    ref = full.at[pl.ds(0, UNITS * rows), :, pl.ds(0, 256)]
    remote(ref, ref, xs_sem, xr_sem.at[0], sibling).wait_send()
    ref = full.at[pl.ds(0, UNITS * (shards - 1)), :, pl.ds(0, 128)]
    remote(ref, ref, ys_sem, yr_sem.at[0], sibling).wait_send()
    remote(ref, ref, cy_sem, cyr_sem.at[0], sibling).wait_send()
    ref = full.at[pl.ds(0, UNITS * (shards - 1)), :, pl.ds(0, 256)]
    remote(ref, ref, cp_sem, cpr_sem.at[0], sibling).wait_send()


def gather(wq, wk, wv, wo, wu, wd, xc, vec, shards, seqn):
    rows_of = wq.shape[0]
    width = wq.shape[1]
    bf16 = jnp.bfloat16
    anywhere = pl.BlockSpec(memory_space=pl.ANY)
    dma = pltpu.SemaphoreType.DMA
    rows = shards // 2
    return pl.pallas_call(
        functools.partial(gather_kernel, shards, seqn),
        out_shape=(
            jax.ShapeDtypeStruct((UNITS * shards, rows_of, width), bf16),
            jax.ShapeDtypeStruct((seqn,) + xc.shape, bf16),
            jax.ShapeDtypeStruct((shards,) + vec.shape, jnp.float32),
        ),
        in_specs=[anywhere] * 7 + [pl.BlockSpec(memory_space=pltpu.VMEM)],
        out_specs=(anywhere, anywhere, anywhere),
        scratch_shapes=[
            pltpu.VMEM((UNITS, rows_of, width), bf16),
            pltpu.VMEM(xc.shape, bf16),
            dma((UNITS + 1,)),
            dma((UNITS + 2,)),
            dma((rows,)),
            dma((rows,)),
            dma(()),
            dma(()),
            dma(()),
            dma(()),
            dma((UNITS, rows)),
            dma((UNITS,)),
            dma((UNITS,)),
            dma((UNITS,)),
            dma((UNITS,)),
            dma((3,)),
            dma((3,)),
            dma(()),
            dma(()),
        ],
        compiler_params=pltpu.CompilerParams(collective_id=0, has_side_effects=True),
        name="gather_weights",
    )(wq, wk, wv, wo, wu, wd.reshape(4, rows_of, width), xc, vec)


def reduce_kernel(
    shards, seqn,
    grads, dxs, small,
    out, dx_out, small_out,
    acc, got_core, got_deck, got_across, line, from_below, from_above, got_plane, half, got_half,
    dx_own, dx_core, dx_deck, got_small, mid_small, got_mid,
    load_sem, core_send, core_recv, deck_send, deck_recv, across_send, across_recv,
    up_send, up_recv, down_send, down_recv, plane_send, plane_recv, half_send, half_recv,
    dx_load, dx_send, dx_recv, small_send, small_recv, mid_send, mid_recv,
):
    dp, sq, row, side, deck, core = place(None)
    rows = shards // 2
    f32, bf16 = jnp.float32, jnp.bfloat16
    up = ((row + 1) * 2 + side, sq)
    down = ((row - 1) * 2 + side, sq)
    across = (row * 2 + 1 - side, sq)
    other_deck = (dp, (1 - deck) * 2 + core)
    sibling = (dp, deck * 2 + 1 - core)

    barrier = pltpu.get_barrier_semaphore()

    def greet(step, carry):
        pl.semaphore_signal(barrier, inc=1, device_id=(lax.rem(dp + step, shards), sq), device_id_type=MESH)
        return carry

    def greet_seq(step, carry):
        pl.semaphore_signal(barrier, inc=1, device_id=(dp, lax.rem(sq + step, seqn)), device_id_type=MESH)
        return carry

    lax.fori_loop(1, shards, greet, 0)
    lax.fori_loop(1, seqn, greet_seq, 0)

    mine = pl.ds(pl.multiple_of(core * 384, 128), 384)
    siblings = pl.ds(pl.multiple_of((1 - core) * 384, 128), 384)
    plane = pl.ds(pl.multiple_of(deck * 128, 128), 256)
    solo = pl.ds(pl.multiple_of(deck * 256, 128), 128)
    other_solo = pl.ds(pl.multiple_of((1 - deck) * 256, 128), 128)

    def remote(src, dst, send, recv, device):
        return pltpu.make_async_remote_copy(
            src_ref=src, dst_ref=dst, send_sem=send, recv_sem=recv, device_id=device, device_id_type=MESH
        )

    def load_all(u, carry):
        def one(s, inner):
            for b in range(2):
                tile = tile_of(u, s * 2 + b, shards)
                pltpu.make_async_copy(grads.at[tile, :, mine], acc.at[u, s, b], load_sem.at[u]).start()
            return inner

        return lax.fori_loop(0, rows, one, carry)

    lax.fori_loop(0, UNITS, load_all, 0)
    for k in range(2):
        pltpu.make_async_copy(dxs.at[k * 2 + core], dx_own.at[k], dx_load.at[k]).start()
    got_small[dp] = small[dp]
    pl.semaphore_wait(barrier, shards + seqn - 2)

    def send_core(u, carry):
        def one(s, inner):
            for b in range(2):
                tile = tile_of(u, s * 2 + b, shards)
                remote(grads.at[tile, :, siblings], got_core.at[u, s, b], core_send, core_recv.at[u], sibling).start()
            return inner

        return lax.fori_loop(0, rows, one, carry)

    lax.fori_loop(0, UNITS, send_core, 0)
    for k in range(2):
        remote(dxs.at[k * 2 + 1 - core], dx_core.at[k], dx_send.at[k], dx_recv.at[k], sibling).start()

    def send_small(step, carry):
        to = lax.rem(dp + step, shards)
        remote(small.at[to], got_small.at[dp], small_send, small_recv, (to, sq)).start()
        return carry

    lax.fori_loop(1, shards, send_small, 0)

    def total(left, right):
        return (left.astype(f32) + right.astype(f32)).astype(bf16)

    def step(n, carry):
        @pl.when(n < UNITS)
        def _():
            u = n
            pltpu.make_async_copy(acc.at[u], acc.at[u], load_sem.at[u]).wait()
            remote(got_core.at[u], got_core.at[u], core_send, core_recv.at[u], sibling).wait_recv()

            def add(s, inner):
                for b in range(2):
                    acc[u, s, b] = total(acc[u, s, b], got_core[u, s, b])
                return inner

            lax.fori_loop(0, rows, add, 0)
            remote(acc.at[u, :, :, :, other_solo], got_deck.at[u], deck_send.at[u], deck_recv.at[u], other_deck).start()

        u2 = n - 1

        @pl.when((u2 >= 0) & (u2 < UNITS))
        def _():
            u = u2
            remote(got_deck.at[u], got_deck.at[u], deck_send.at[u], deck_recv.at[u], other_deck).wait_recv()

            def add(s, inner):
                for b in range(2):
                    acc[u, s, b, :, solo] = total(acc[u, s, b, :, solo], got_deck[u, s, b])
                return inner

            lax.fori_loop(0, rows, add, 0)
            remote(
                acc.at[u, :, 1 - side, :, plane], got_across.at[u], across_send.at[u], across_recv.at[u], across
            ).start()

        u3 = n - 2

        @pl.when((u3 >= 0) & (u3 < UNITS))
        def _():
            u = u3
            remote(got_across.at[u], got_across.at[u], across_send.at[u], across_recv.at[u], across).wait_recv()

            def add(s, inner):
                line[u, s] = total(acc[u, s, side, :, plane], got_across[u, s])
                return inner

            lax.fori_loop(0, rows, add, 0)

        u_up = n - 3 - row

        @pl.when((u_up >= 0) & (u_up < UNITS))
        def _():
            u = u_up

            def one(s, inner):
                @pl.when(row > 0)
                def _():
                    remote(line.at[u, s], from_below.at[u, s], up_send.at[u, s], up_recv.at[u, s], up).wait_recv()
                    line[u, s] = total(line[u, s], from_below[u, s])

                @pl.when(s > row)
                def _():
                    remote(line.at[u, s], from_below.at[u, s], up_send.at[u, s], up_recv.at[u, s], up).start()

                return inner

            lax.fori_loop(row, rows, one, 0)

        u_down = n - 3 - (rows - 1 - row)

        @pl.when((u_down >= 0) & (u_down < UNITS))
        def _():
            u = u_down

            def one(s, inner):
                @pl.when(row < rows - 1)
                def _():
                    remote(line.at[u, s], from_above.at[u, s], down_send.at[u, s], down_recv.at[u, s], down).wait_recv()
                    line[u, s] = total(line[u, s], from_above[u, s])

                @pl.when(s < row)
                def _():
                    remote(line.at[u, s], from_above.at[u, s], down_send.at[u, s], down_recv.at[u, s], down).start()

                return inner

            lax.fori_loop(0, row + 1, one, 0)

        u_f = n - 3 - rows

        @pl.when((u_f >= 0) & (u_f < UNITS))
        def _():
            u = u_f
            remote(line.at[u, row], got_plane.at[u], plane_send.at[u], plane_recv.at[u], other_deck).start()

        u_h = n - 4 - rows

        @pl.when((u_h >= 0) & (u_h < UNITS))
        def _():
            u = u_h
            remote(line.at[u, row], got_plane.at[u], plane_send.at[u], plane_recv.at[u], other_deck).wait_recv()
            half[u, :, plane] = line[u, row]
            half[u, :, other_solo] = got_plane[u, :, pl.ds(pl.multiple_of((1 - deck) * 128, 128), 128)]
            half[u, :, pl.ds(128, 128)] = total(
                half[u, :, pl.ds(128, 128)], got_plane[u, :, pl.ds(pl.multiple_of(deck * 128, 128), 128)]
            )
            remote(half.at[u], got_half.at[u], half_send.at[u], half_recv.at[u], sibling).start()

        u_o = n - 5 - rows

        @pl.when((u_o >= 0) & (u_o < UNITS))
        def _():
            u = u_o
            remote(half.at[u], got_half.at[u], half_send.at[u], half_recv.at[u], sibling).wait_recv()
            out[u, :, mine] = half[u].astype(f32)
            out[u, :, siblings] = got_half[u].astype(f32)

        return carry

    lax.fori_loop(0, 3, step, 0)
    for k in range(2):
        pltpu.make_async_copy(dx_own.at[k], dx_own.at[k], dx_load.at[k]).wait()
        remote(dx_core.at[k], dx_core.at[k], dx_send.at[k], dx_recv.at[k], sibling).wait()
        dx_own[k] = total(dx_own[k], dx_core[k])
    deck_dx = remote(dx_own.at[1 - deck], dx_deck, dx_send.at[2], dx_recv.at[2], other_deck)
    deck_dx.start()
    rest = got_small.at[pl.ds(0, shards - 1)]
    remote(rest, rest, small_send, small_recv, sibling).wait()
    summed = got_small[0]
    for i in range(1, shards):
        summed = summed + got_small[i]
    mid_small[...] = summed
    got_mid[sq] = summed

    def send_mid(step, carry):
        remote(mid_small, got_mid.at[sq], mid_send, mid_recv, (dp, lax.rem(sq + step, seqn))).start()
        return carry

    lax.fori_loop(1, seqn, send_mid, 0)
    lax.fori_loop(3, UNITS + 6 + rows, step, 0)

    rest = got_mid.at[pl.ds(0, seqn - 1)]
    remote(rest, rest, mid_send, mid_recv, sibling).wait()
    summed = got_mid[0]
    for i in range(1, seqn):
        summed = summed + got_mid[i]
    small_out[...] = summed
    deck_dx.wait()
    dx_out[...] = dx_own[deck].astype(f32) + dx_deck[...].astype(f32)

    ref = got_core
    remote(ref, ref, core_send, core_recv.at[0], sibling).wait_send()

    def sent(u, carry):
        remote(got_deck.at[u], got_deck.at[u], deck_send.at[u], deck_recv.at[u], other_deck).wait_send()
        remote(got_across.at[u], got_across.at[u], across_send.at[u], across_recv.at[u], across).wait_send()
        remote(got_plane.at[u], got_plane.at[u], plane_send.at[u], plane_recv.at[u], other_deck).wait_send()
        remote(half.at[u], half.at[u], half_send.at[u], half_recv.at[u], sibling).wait_send()

        def one(s, inner):
            @pl.when(s > row)
            def _():
                remote(line.at[u, s], from_below.at[u, s], up_send.at[u, s], up_recv.at[u, s], up).wait_send()

            @pl.when(s < row)
            def _():
                remote(line.at[u, s], from_above.at[u, s], down_send.at[u, s], down_recv.at[u, s], down).wait_send()

            return inner

        return lax.fori_loop(0, rows, one, carry)

    lax.fori_loop(0, UNITS, sent, 0)


def reduce_grads(grads, dxs, small, shards, seqn):
    rows_of, width = grads.shape[1:]
    f32, bf16 = jnp.float32, jnp.bfloat16
    anywhere = pl.BlockSpec(memory_space=pl.ANY)
    vmem = pl.BlockSpec(memory_space=pltpu.VMEM)
    dma = pltpu.SemaphoreType.DMA
    rows = shards // 2
    own = dxs.shape[1:]
    return pl.pallas_call(
        functools.partial(reduce_kernel, shards, seqn),
        out_shape=(
            jax.ShapeDtypeStruct((UNITS, rows_of, width), f32),
            jax.ShapeDtypeStruct(own, f32),
            jax.ShapeDtypeStruct(small.shape[1:], f32),
        ),
        in_specs=[anywhere, anywhere, vmem],
        out_specs=(vmem, vmem, vmem),
        scratch_shapes=[
            pltpu.VMEM((UNITS, rows, 2, rows_of, 384), bf16),
            pltpu.VMEM((UNITS, rows, 2, rows_of, 384), bf16),
            pltpu.VMEM((UNITS, rows, 2, rows_of, 128), bf16),
            pltpu.VMEM((UNITS, rows, rows_of, 256), bf16),
            pltpu.VMEM((UNITS, rows, rows_of, 256), bf16),
            pltpu.VMEM((UNITS, rows, rows_of, 256), bf16),
            pltpu.VMEM((UNITS, rows, rows_of, 256), bf16),
            pltpu.VMEM((UNITS, rows_of, 256), bf16),
            pltpu.VMEM((UNITS, rows_of, 384), bf16),
            pltpu.VMEM((UNITS, rows_of, 384), bf16),
            pltpu.VMEM((2,) + own, bf16),
            pltpu.VMEM((2,) + own, bf16),
            pltpu.VMEM(own, bf16),
            pltpu.VMEM(small.shape, f32),
            pltpu.VMEM(small.shape[1:], f32),
            pltpu.VMEM((seqn,) + small.shape[1:], f32),
            dma((UNITS,)),
            dma(()),
            dma((UNITS,)),
            dma((UNITS,)),
            dma((UNITS,)),
            dma((UNITS,)),
            dma((UNITS,)),
            dma((UNITS, rows)),
            dma((UNITS, rows)),
            dma((UNITS, rows)),
            dma((UNITS, rows)),
            dma((UNITS,)),
            dma((UNITS,)),
            dma((UNITS,)),
            dma((UNITS,)),
            dma((2,)),
            dma((3,)),
            dma((3,)),
            dma(()),
            dma(()),
            dma(()),
            dma(()),
        ],
        compiler_params=pltpu.CompilerParams(
            collective_id=1, has_side_effects=True, vmem_limit_bytes=60 * 1024 * 1024
        ),
        name="reduce_grads",
    )(grads, dxs, small)

def per_device(
    x_content, x_query, cot_content, cot_query,
    w_query, b_query, w_key, w_value, b_value, w_out, b_out, gain_attn, shift_attn,
    w_up, b_up, w_down, b_down, gain_ffn, shift_ffn, rel_table, lengths, positions, predicted,
    *, shards, seqn,
):
    f32 = jnp.float32
    bf16 = jnp.bfloat16
    scale = HD ** (-0.5)
    seqs, block, width = x_content.shape
    span = positions.shape[1]
    r = w_query.shape[0]
    vec = jnp.concatenate(
        [b_query, b_value, b_out, gain_attn, shift_attn, b_down, gain_ffn, shift_ffn, b_up]
    ).astype(f32)[None]
    full, xall, vall = gather(w_query, w_key, w_value, w_out, w_up, w_down, x_content, vec, shards, seqn)
    weights = full.reshape(UNITS, width, width)
    wq, wk, wv, wo = (weights[i] for i in range(4))
    w1, w2 = weights[4:8], weights[8:12]
    bq, bv, bo, g1, b1, c2, g2, b2 = (vall[:, 0, i * r : (i + 1) * r].reshape(width) for i in range(8))
    c1 = vall[:, 0, 8 * r :].reshape(4, width)
    x_every = jnp.transpose(xall, (1, 0, 2, 3)).reshape(seqs, span, width)

    base = lax.axis_index("seq") * block
    slot_q = base + jnp.arange(block)
    slot_k = jnp.arange(span)
    valid_k = slot_k[None, :] < lengths[:, None]
    valid_q = slot_q[None, :] < lengths[:, None]
    allow_c = valid_k[:, None, :] & (slot_k[None, :] <= slot_q[:, None])[None]
    allow_q = valid_k[:, None, :] & (slot_k[None, :] < jnp.maximum(slot_q[:, None], 1))[None]
    allowed = jnp.stack([allow_c, allow_q])
    pos_q = lax.dynamic_slice_in_dim(positions, base, block, 1)
    onehot = (bucket_ids(pos_q, positions)[..., None] == jnp.arange(NB)).astype(f32)
    table = rel_table.astype(f32)
    bias = jnp.einsum("sqkn,nh->shqk", onehot, table, precision=lax.Precision.HIGHEST)
    xs = jnp.stack([x_content, x_query])
    keys = jnp.einsum("sqd,de->sqe", x_every, wk, preferred_element_type=f32).astype(bf16)
    values = (jnp.einsum("sqd,de->sqe", x_every, wv, preferred_element_type=f32) + bv).astype(bf16)
    query = (jnp.einsum("tsqd,de->tsqe", xs, wq, preferred_element_type=f32) + bq).astype(bf16)
    query4 = query.reshape(2, seqs, block, H, HD)
    keys4 = keys.reshape(seqs, span, H, HD)
    values4 = values.reshape(seqs, span, H, HD)

    raw = jnp.einsum("tsqhe,skhe->tshqk", query4, keys4, preferred_element_type=f32)
    scores = jnp.where(allowed[:, :, None], raw * scale + bias[None], -1e30)
    top = jnp.max(scores, axis=-1, keepdims=True)
    expo = jnp.exp(scores - top)
    probs = expo / jnp.sum(expo, axis=-1, keepdims=True)
    mixed = jnp.einsum("tshqk,skhe->tsqhe", probs.astype(bf16), values4, preferred_element_type=f32)
    attended = mixed.reshape(2, seqs, block, width).astype(bf16)
    out = jnp.einsum("tsqd,de->tsqe", attended, wo, preferred_element_type=f32) + bo
    resid_one = xs.astype(f32) + out
    hidden, pull_one = jax.vjp(norm_apply, resid_one, g1, b1)
    hidden_low = hidden.astype(bf16)
    upper = jnp.einsum("tsqd,jdf->tsqjf", hidden_low, w1, preferred_element_type=f32) + c1
    active_full, pull_gelu = jax.vjp(lambda value: jax.nn.gelu(value, approximate=False), upper)
    active = active_full.astype(bf16)
    feed = jnp.einsum("tsqjf,jfd->tsqd", active, w2, preferred_element_type=f32) + c2
    result, pull_two = jax.vjp(norm_apply, hidden + feed, g2, b2)
    keep = jnp.stack([valid_q, valid_q & (predicted > 0)])[..., None].astype(f32)
    outputs = result * keep
    cotangent = jnp.stack([cot_content, cot_query]).astype(f32) * keep
    d_resid_two, d_g2, d_b2 = pull_two(cotangent)
    d_c2 = jnp.sum(d_resid_two, axis=(0, 1, 2))
    d_feed_low = d_resid_two.astype(bf16)
    d_w2 = jnp.einsum("tsqjf,tsqd->jfd", active, d_feed_low, preferred_element_type=f32)
    d_active = jnp.einsum("tsqd,jfd->tsqjf", d_feed_low, w2, preferred_element_type=f32)
    (d_upper,) = pull_gelu(d_active)
    d_c1 = jnp.sum(d_upper, axis=(0, 1, 2)).reshape(4 * width)
    d_upper_low = d_upper.astype(bf16)
    d_w1 = jnp.einsum("tsqd,tsqjf->jdf", hidden_low, d_upper_low, preferred_element_type=f32)
    d_hidden = d_resid_two + jnp.einsum("tsqjf,jdf->tsqd", d_upper_low, w1, preferred_element_type=f32)
    d_resid_one, d_g1, d_b1 = pull_one(d_hidden)
    d_bo = jnp.sum(d_resid_one, axis=(0, 1, 2))
    d_out_low = d_resid_one.astype(bf16)
    d_wo = jnp.einsum("tsqd,tsqe->de", attended, d_out_low, preferred_element_type=f32)
    d_attended = jnp.einsum("tsqe,de->tsqd", d_out_low, wo, preferred_element_type=f32).astype(bf16)
    d_mixed = d_attended.reshape(2, seqs, block, H, HD)
    d_probs = jnp.einsum("tsqhe,skhe->tshqk", d_mixed, values4, preferred_element_type=f32)
    d_scores = probs * (d_probs - jnp.sum(d_probs * probs, axis=-1, keepdims=True))
    d_table = jnp.einsum(
        "shqk,sqkn->nh", jnp.sum(d_scores, axis=0), onehot, precision=lax.Precision.HIGHEST
    )
    d_raw = (d_scores * scale).astype(bf16)
    d_query = jnp.einsum("tshqk,skhe->tsqhe", d_raw, keys4, preferred_element_type=f32).reshape(
        2, seqs, block, width
    )
    d_keys = jnp.einsum("tshqk,tsqhe->skhe", d_raw, query4, preferred_element_type=f32).reshape(
        seqs, span, width
    )
    d_values = jnp.einsum(
        "tshqk,tsqhe->skhe", probs.astype(bf16), d_mixed, preferred_element_type=f32
    ).reshape(seqs, span, width)
    d_bq = jnp.sum(d_query, axis=(0, 1, 2))
    d_bv = jnp.sum(d_values, axis=(0, 1))
    d_query_low = d_query.astype(bf16)
    d_key_low = d_keys.astype(bf16)
    d_value_low = d_values.astype(bf16)
    d_wq = jnp.einsum("tsqd,tsqe->de", xs, d_query_low, preferred_element_type=f32)
    d_wk = jnp.einsum("sqd,sqe->de", x_every, d_key_low, preferred_element_type=f32)
    d_wv = jnp.einsum("sqd,sqe->de", x_every, d_value_low, preferred_element_type=f32)
    d_inputs = d_resid_one + jnp.einsum("tsqe,de->tsqd", d_query_low, wq, preferred_element_type=f32)
    d_every = jnp.einsum("sqe,de->sqd", d_key_low, wk, preferred_element_type=f32) + jnp.einsum(
        "sqe,de->sqd", d_value_low, wv, preferred_element_type=f32
    )
    dxs = jnp.transpose(d_every.astype(bf16).reshape(seqs, seqn, block, width), (1, 0, 2, 3))
    grads = jnp.concatenate(
        [jnp.stack([d_wq, d_wk, d_wv, d_wo]).astype(bf16), d_w1.astype(bf16), d_w2.astype(bf16)]
    ).reshape(UNITS * shards, r, width)
    small = jnp.concatenate(
        [d.reshape(shards, 1, r) for d in (d_bq, d_bv, d_bo, d_g1, d_b1, d_c2, d_g2, d_b2)]
        + [d_c1.reshape(shards, 1, 4 * r), jnp.broadcast_to(d_table.reshape(1, 1, NB * H), (shards, 1, NB * H))],
        axis=-1,
    )
    sums, dx, tiny = reduce_grads(grads, dxs.reshape(seqn, seqs * block, width), small, shards, seqn)
    grad_content = d_inputs[0] + dx.reshape(seqs, block, width)
    tiny = tiny[0]
    pieces = [tiny[i * r : (i + 1) * r] for i in range(8)]
    g_bq, g_bv, g_bo, g_g1, g_b1, g_c2, g_g2, g_b2 = pieces
    g_c1 = tiny[8 * r : 12 * r]
    g_table = tiny[12 * r :].reshape(NB, H)
    g_w1 = jnp.transpose(sums[4:8], (1, 0, 2)).reshape(r, 4 * width)
    g_w2 = sums[8:12].reshape(4 * r, width)
    return (
        outputs[0], outputs[1], grad_content, d_inputs[1],
        sums[0], g_bq, sums[1], sums[2], g_bv, sums[3], g_bo, g_g1, g_b1,
        g_w1, g_c1, g_w2, g_c2, g_g2, g_b2, g_table,
    )

def solution(mesh):
    in_specs = (
        P("dp", "seq", None),
        P("dp", "seq", None),
        P("dp", "seq", None),
        P("dp", "seq", None),
        P("dp", None),
        P("dp"),
        P("dp", None),
        P("dp", None),
        P("dp"),
        P("dp", None),
        P("dp"),
        P("dp"),
        P("dp"),
        P("dp", None),
        P("dp"),
        P("dp", None),
        P("dp"),
        P("dp"),
        P("dp"),
        P(),
        P("dp"),
        P("dp", None),
        P("dp", "seq"),
    )
    out_specs = (
        P("dp", "seq", None),
        P("dp", "seq", None),
        P("dp", "seq", None),
        P("dp", "seq", None),
        P("dp", None),
        P("dp"),
        P("dp", None),
        P("dp", None),
        P("dp"),
        P("dp", None),
        P("dp"),
        P("dp"),
        P("dp"),
        P("dp", None),
        P("dp"),
        P("dp", None),
        P("dp"),
        P("dp"),
        P("dp"),
        P(),
    )
    return jax.shard_map(
        functools.partial(per_device, shards=mesh.shape["dp"], seqn=mesh.shape["seq"]),
        mesh=mesh, in_specs=in_specs, out_specs=out_specs, check_vma=False
    )
```

time: 1210 us -> 484 us (0.40)
  waiting for transfers between devices: 709 us -> 0 us
  Pallas kernels: 0 us -> 176 us
  blocking collectives: 131 us -> 0 us
  matrix products: 136 us -> 119 us
  between operations: 17.3 us -> 2.17 us
    reduce_scatter x4 -> x0, waiting for transfers between devices: 389 us -> none  [the longest x1 165 us: per_device(): lax.psum_scatter(d_w1, 'dp', scatter_dimension=0, tiled=True)]
    pallas_call x0 -> x2, Pallas kernels: none -> 176 us  [the longest x1 102 us: reduce_grads(): pl.pallas_call(functools.partial(reduce_kernel, shards, seqn), out_shape=...]
    unnamed x21 -> x0, waiting for transfers between devices: 168 us -> none
    all_gather x8 -> x0, waiting for transfers between devices: 152 us -> none  [the longest x1 54.7 us: per_device(): lax.all_gather(w_down, 'dp', axis=0, tiled=True)]
    unnamed x2 -> x0, blocking collectives: 57.2 us -> none
    psum x2 -> x0, blocking collectives: 52.3 us -> none  [the longest x1 39.4 us: per_device(): table_total = lax.psum(d_table, ('dp', 'seq'))]
    unnamed x155 -> x139, local copies, waits for them, and re-layouts: 54 us -> 5.65 us
    all_gather x1 -> x0, blocking collectives: 21.8 us -> none  [per_device(): lax.all_gather(b_up, 'dp', axis=0, tiled=True)]
  transfers between devices with their start and end apart: 17 -> 0, of which waited for: 11 -> 0; matrix products, arithmetic and copies ran while one was open for 21% -> 0% of each run, Pallas kernels for 0% -> 0%
where the time goes in v1:
time: 484 us; the launch traced here: 480 us
  Pallas kernels  176 us (36%)
  local copies, waits for them, and re-layouts  139 us (29%)
  matrix products  119 us (25%)
  other arithmetic  43.5 us (9%)
    pallas_call x1, Pallas kernels, reduce_grads(): pl.pallas_call(functools.partial(reduce_kernel, shards, seqn), out_shape=...  102 us
    eq x1, local copies, waits for them, and re-layouts, per_device(): bucket_ids(pos_q, positions)[..., None] == jnp.arange(NB)  74.6 us
    pallas_call x1, Pallas kernels, gather(): pl.pallas_call(functools.partial(gather_kernel, shards, seqn), out_shape=...  74.4 us
    sub x1, matrix products, per_device(): d_probs - jnp.sum(d_probs * probs, axis=-1, keepdims=True)  17.6 us
    convert_element_type x1, other arithmetic, per_device(): active = active_full.astype(bf16)  15.6 us
    dot_general x1, matrix products, per_device(): jnp.einsum('shqk,sqkn->nh', jnp.sum(d_scores, axis=0), onehot, precision=...  13.5 us
    sub x1, matrix products, per_device(): expo = jnp.exp(scores - top)  9.71 us

profile of v1, /device:TPU:1, one launch (start us, length us, event | category | flops | bytes accessed | tf_op | source)
XLA Modules:
  0.0 479.9 jit_solution(6192451366415546462)
XLA Ops:
  4.8 0.9 concatenate.48
  7.3 1.3 fusion.84
  8.9 2.3 iota_compare_fusion
  11.2 74.6 %copy.190 = pred[2,128,512,32]{2,3,1,0:T(32,128)(4,1)S(1)} copy(pred[2,128,512,32]{1,3,0,2:T(32,128)(4,1)S(1)} %iota_compare_fusion) | data formatting | bytes 8388608 | tf_op jit(solution)/shard_map/eq | solution.py:652
  85.8 5.2 %convolution_bitcast_fusion = f32[2,12,128,512]{3,1,2,0:T(8,128)} fusion(pred[2,128,512,32]{2,3,1,0:T(32,128)(4,1)S(1)} %copy.190, bf16[32,12]{0,1:T(8,128)(2,1)S(1)} %copy-done), kind=kOutput, calls=%fused_computation.49 | convolution fusion | flops 100663296 | bytes 10486528 | tf_op jit(solution)/shard_map/sqkn,nh->shqk/dot_general | solution.py:654
  91.1 9.2 %copy.191 = f32[2,12,128,512]{2,3,1,0:T(8,128)} copy(f32[2,12,128,512]{3,1,2,0:T(8,128)} %convolution_bitcast_fusion) | data formatting | bytes 12582912 | tf_op jit(solution)/shard_map/sqkn,nh->shqk/transpose | solution.py:654
  100.2 74.4 %gather_weights.1 = (bf16[96,96,768]{2,1,0:T(8,128)(2,1)}, bf16[4,2,128,768]{3,2,1,0:T(8,128)(2,1)}, f32[8,1,1152]{2,1,0:T(1,128)}) custom-call(bf16[96,768]{1,0:T(8,128)(2,1)} %wq.1, bf16[96,768]{1,0:T(8,128)(2,1)} %wk.1, bf16[96,768]{1,0:T(8,128)(2,1)} %wv.1, bf16[96,768]{1,0:T(8,128)(2,1)} %wo.1, bf16[96,3072]{1,0:T(8,128)(2,1)} %wu.1, ...), custom_call_target="tpu_custom_call" | custom-call | tf_op jit(solution)/shard_map/gather_weights/pallas_call | solution.py:269
  174.6 1.5 copy.184
  181.2 4.2 fusion.98
  185.5 8.3 %fusion.97 = (bf16[32,96,768]{2,1,0:T(8,128)(2,1)}, bf16[32,96,768]{2,1,0:T(8,128)(2,1)}) fusion(bf16[96,96,768]{2,1,0:T(8,128)(2,1)} %get-tuple-element.27), kind=kLoop, calls=%fused_computation.192 | loop fusion | bytes 18874368 | tf_op jit(solution)/shard_map/slice | solution.py:638
  193.8 1.7 add_convert_fusion.2
  195.5 1.5 copy.187
  197.0 4.1 add_convert_fusion.1
  201.1 2.6 copy.185
  203.7 3.8 convolution_convert_fusion
  207.6 1.8 copy.186
  209.4 9.7 %fusion.102 = (f32[2,2,12,128]{3,0,2,1:T(2,128)S(1)}, f32[2,2,12,128,512]{3,4,0,2,1:T(8,128)}) fusion(f32[2,12,128,512]{2,3,1,0:T(8,128)} %copy.191, pred[2,2,128,512]{2,3,0,1:T(8,128)(4,1)S(1)} %copy-done.38, bf16[2,512,12,64,1]{1,3,4,2,0:T(8,128)(2,1)S(1)} %bitcast.283, bf16[2,2,128,12,64]{2,4,3,1,0:T(8,128)(2,1)S(1)} %bitcast.300), kind=kOutput, calls=%fused_computation.197 | convolution fusion | flops 418382336 | bytes 21520384 | tf_op jit(solution)/shard_map/sub | solution.py:666
  219.1 6.3 %fusion.93 = bf16[2,2,12,128,512]{3,4,0,2,1:T(8,128)(2,1)S(1)} fusion(f32[2,2,12,128,512]{3,4,0,2,1:T(8,128)} %get-tuple-element.191, f32[2,2,12,128]{3,0,2,1:T(2,128)S(1)} %get-tuple-element.190), kind=kLoop, calls=%fused_computation.189 | loop fusion | flops 6291456 | bytes 18898944 | tf_op jit(solution)/shard_map/convert_element_type | solution.py:668
  225.4 3.9 fusion.44
  229.5 0.9 fusion.107
  230.9 6.6 %fusion.35 = (u8[2,2,128,768]{3,2,1,0:T(8,128)(4,1)S(1)}, u8[2,2,128,768]{3,2,1,0:T(8,128)(4,1)S(1)}, f32[2,2,128,4,768]{4,2,3,1,0:T(8,128)S(1)}) fusion(f32[4,768]{1,0:T(4,128)S(1)} %add.211, bf16[4,768,768,1,1]{2,1,0,4,3:T(8,128)(2,1)} %bitcast.292, f32[768]{0:T(1024)S(1)} %copy-done.55, f32[768]{0:T(1024)S(1)} %copy-done.53, ...), kind=kOutput, calls=%fused_computation.84 | convolution fusion | flops 2439118848 | bytes 13391872 | tf_op jit(solution)/shard_map/tsqd,jdf->tsqjf/dot_general | solution.py:674
  237.5 15.6 %multiply_convert_fusion.1 = (bf16[2,2,128,4,768]{4,2,3,1,0:T(8,128)(2,1)S(1)}, f32[2,2,128,4,768]{4,2,3,1,0:T(8,128)}) fusion(f32[2,2,128,4,768]{4,2,3,1,0:T(8,128)S(1)} %get-tuple-element.194, f32[4,768]{1,0:T(4,128)S(1)} %add.211, u8[2,2,128,768]{3,2,1,0:T(8,128)(4,1)S(1)} %get-tuple-element.133, u8[2,2,128,768]{3,2,1,0:T(8,128)(4,1)S(1)} %get-tuple-element.132), kind=kLoop, calls=%fused_computation.27 | loop fusion | flops 111673344 | bytes 16527360 | tf_op jit(solution)/shard_map/convert_element_type | solution.py:676
  253.2 2.8 fusion.108
  257.0 1.4 multiply_reduce_fusion
  258.4 1.4 reshape.523
  259.7 1.3 multiply_multiply_fusion.6
  261.0 1.4 reshape.524
  262.4 3.1 fusion.95
  265.6 8.7 %fusion.100 = (f32[4,768]{1,0:T(4,128)S(1)}, bf16[2,2,128,4,768]{4,2,3,1,0:T(8,128)(2,1)S(1)}) fusion(f32[2,2,128,4,768]{4,2,3,1,0:T(8,128)} %get-tuple-element.155, bf16[4,768,768,1,1]{2,1,0,4,3:T(8,128)(2,1)} %bitcast.296, f32[2,2,128,768]{3,2,1,0:T(8,128)S(1)} %get-tuple-element.153, f32[2,2,128]{2,1,0:T(2,128)S(1)} %negate_multiply_fusion.2, ...), kind=kOutput, calls=%fused_computation.195 | convolution fusion | flops 2441868288 | bytes 22046720 | tf_op jit(solution)/shard_map/tsqd,jfd->tsqjf/dot_general | solution.py:686
  274.3 4.2 multiply_reduce_fusion.1
  278.5 1.1 add_reduce_fusion.1
  279.9 3.0 fusion.94
  283.1 1.1 copy-done.32
  284.3 2.1 convolution_convert_fusion.1
  286.4 1.2 copy.195
  287.6 5.0 %fusion.11 = f32[2,12,64,512,1]{3,2,1,0,4:T(8,128)S(1)} fusion(bf16[2,2,128,12,64]{2,4,3,1,0:T(8,128)(2,1)} %bitcast.302, bf16[2,2,12,128,512]{3,4,0,2,1:T(8,128)(2,1)} %copy-done.2), kind=kOutput, calls=%fused_computation.22 | convolution fusion | flops 402653184 | bytes 10223616 | tf_op jit(solution)/shard_map/tshqk,tsqhe->skhe/dot_general | solution.py:710
  292.6 17.6 %fusion.99 = (f32[2,12,128,512]{2,3,1,0:T(8,128)}, bf16[2,2,12,128,512]{3,4,0,2,1:T(8,128)(2,1)}) fusion(bf16[2,512,12,64,1]{1,3,4,2,0:T(8,128)(2,1)} %bitcast.286, bf16[2,2,128,12,64]{2,4,3,1,0:T(8,128)(2,1)} %bitcast.303, f32[2,2,12,128,512]{3,4,0,2,1:T(8,128)} %get-tuple-element.191, f32[2,2,12,128]{3,0,2,1:T(2,128)S(1)} %copy-done.43), kind=kOutput, calls=%fused_computation.194 | convolution fusion | flops 828905984 | bytes 27549696 | tf_op jit(solution)/shard_map/sub | solution.py:699
  310.3 13.5 %fusion.50 = f32[32,12]{1,0:T(8,128)S(1)} fusion(f32[2,12,128,512]{2,3,1,0:T(8,128)} %get-tuple-element.162, s32[2,128,512]{1,0,2:T(2,128)} %copy-done.17), kind=kOutput, calls=%fused_computation.106 | convolution fusion | flops 608174080 | bytes 6817280 | tf_op jit(solution)/shard_map/shqk,sqkn->nh/dot_general | solution.py:700
  324.1 1.4 copy.326
  325.6 1.7 copy.209
  327.3 5.0 %fusion.13 = bf16[2,12,64,512,1]{3,2,1,0,4:T(8,128)(2,1)S(1)} fusion(bf16[2,2,128,12,64]{2,4,3,1,0:T(8,128)(2,1)S(1)} %bitcast.301, bf16[2,2,12,128,512]{3,4,0,2,1:T(8,128)(2,1)} %get-tuple-element.163), kind=kOutput, calls=%fused_computation.24 | convolution fusion | flops 402653184 | bytes 8650752 | tf_op jit(solution)/shard_map/tshqk,tsqhe->skhe/dot_general | solution.py:707
  332.4 1.2 bitcast_convert_fusion.8
  333.6 0.9 copy-done.29
  334.5 2.1 convolution_add_fusion
  336.7 1.3 copy.204
  339.1 2.2 slice_bitcast_fusion.1
  341.3 1.3 slice_bitcast_fusion.3
  342.5 1.4 fusion.113
  344.0 1.5 add_convert_fusion
  345.5 1.3 copy.220
  347.4 1.8 fusion.41
  349.3 2.5 fusion.37
  351.7 2.5 fusion.39
  354.2 1.8 fusion.43
  356.8 4.7 fusion.26
  361.4 4.3 fusion.27
  365.7 101.9 %reduce_grads.1 = (f32[12,96,768]{2,1,0:T(8,128)}, f32[256,768]{1,0:T(8,128)}, f32[1,1536]{1,0:T(1,128)}) custom-call(bf16[96,96,768]{2,1,0:T(8,128)(2,1)} %bitcast.95.grads, bf16[4,256,768]{2,1,0:T(8,128)(2,1)} %bitcast.287, f32[8,1,1536]{2,1,0:T(1,128)} %concatenate.50.small), custom_call_target="tpu_custom_call" | custom-call | tf_op jit(solution)/shard_map/reduce_grads/pallas_call | solution.py:565
  467.6 2.5 fusion.53
  470.1 1.4 slice_bitcast_fusion.9
  471.5 1.3 slice_reduce_fusion.9
  473.5 1.4 copy.224
  474.9 2.3 slice_bitcast_fusion.5
  477.1 1.2 fusion.101
  478.3 1.1 copy.272
  (189 shorter events, 16.9 us)
Async XLA Ops:
  0.7 85.2 %copy-start = (bf16[32,12]{0,1:T(8,128)(2,1)S(1)}, bf16[32,12]{0,1:T(8,128)(2,1)}, u32[]{:S(2)}) copy-start(bf16[32,12]{0,1:T(8,128)(2,1)} %param.42) | copy-start | bytes 2308
  8.8 77.0 %copy-start.17 = (s32[2,128,512]{1,0,2:T(2,128)}, s32[2,128,512]{1,0,2:T(2,128)S(1)}, u32[]{:S(2)}) copy-start(s32[2,128,512]{1,0,2:T(2,128)S(1)} %copy.189) | copy-start | bytes 1572868
  174.6 1.5 copy-start.39
  176.1 27.6 %copy-start.20 = (bf16[2,4,128,768]{3,2,1,0:T(8,128)(2,1)}, bf16[2,4,128,768]{3,2,1,0:T(8,128)(2,1)S(1)}, u32[]{:S(2)}) copy-start(bf16[2,4,128,768]{3,2,1,0:T(8,128)(2,1)S(1)} %copy.184) | copy-start | bytes 4718596
  185.4 8.3 %copy-start.27 = (bf16[8,96,768]{2,1,0:T(8,128)(2,1)}, bf16[8,96,768]{2,1,0:T(8,128)(2,1)S(1)}, u32[]{:S(2)}) copy-start(bf16[8,96,768]{2,1,0:T(8,128)(2,1)S(1)} %get-tuple-element.159) | copy-start | bytes 3538948
  185.4 8.3 %copy-start.23 = (bf16[2,128,768]{2,1,0:T(8,128)(2,1)S(1)}, bf16[2,128,768]{2,1,0:T(8,128)(2,1)}, u32[]{:S(2)}) copy-start(bf16[2,128,768]{2,1,0:T(8,128)(2,1)} %xc.1) | copy-start | bytes 1179652
  185.4 8.3 %copy-start.35 = (bf16[2,128,768]{2,1,0:T(8,128)(2,1)S(1)}, bf16[2,128,768]{2,1,0:T(8,128)(2,1)}, u32[]{:S(2)}) copy-start(bf16[2,128,768]{2,1,0:T(8,128)(2,1)} %param.24) | copy-start | bytes 1179652
  185.4 8.3 %copy-start.60 = (f32[768]{0:T(1024)S(1)}, f32[768]{0:T(1024)}, u32[]{:S(2)}) copy-start(f32[768]{0:T(1024)} %add.190) | copy-start | bytes 9220
  197.0 12.4 %copy-start.13 = (bf16[2,2,128,768]{2,3,1,0:T(8,128)(2,1)}, bf16[2,2,128,768]{2,3,1,0:T(8,128)(2,1)S(1)}, u32[]{:S(2)}) copy-start(bf16[2,2,128,768]{2,3,1,0:T(8,128)(2,1)S(1)} %copy.187) | copy-start | bytes 2359300
  207.6 1.8 copy-start.38
  209.3 9.7 %copy-start.3 = (bf16[2,512,768]{1,2,0:T(8,128)(2,1)}, bf16[2,512,768]{1,2,0:T(8,128)(2,1)S(1)}, u32[]{:S(2)}) copy-start(bf16[2,512,768]{1,2,0:T(8,128)(2,1)S(1)} %copy.186) | copy-start | bytes 4718596
  219.1 6.3 %copy-start.42 = (f32[2,2,12,128]{3,0,2,1:T(2,128)}, f32[2,2,12,128]{3,0,2,1:T(2,128)S(1)}, u32[]{:S(2)}) copy-start(f32[2,2,12,128]{3,0,2,1:T(2,128)S(1)} %get-tuple-element.190) | copy-start | bytes 73732
  225.4 4.0 copy-start.2
  225.4 4.1 copy-start.9
  225.4 4.1 copy-start.36
  225.4 4.1 copy-start.40
  229.5 1.4 copy-start.53
  229.5 1.4 copy-start.55
  230.5 22.6 %copy-start.46 = (f32[2,2,128]{2,1,0:T(2,128)}, f32[2,2,128]{2,1,0:T(2,128)S(1)}, u32[]{:S(2)}) copy-start(f32[2,2,128]{2,1,0:T(2,128)S(1)} %broadcast_multiply_fusion.1) | copy-start | bytes 6148
  230.5 22.6 %slice-start.4 = ((s8[4718592]{0:T(1024)(128)(4,1)}), s8[4194304]{0:T(1024)(128)(4,1)S(1)}, s32[]{:S(2)}) async-start(s8[4718592]{0:T(1024)(128)(4,1)} %bitcast.297), calls=%async_computation.4 | async-start | bytes 8388608
  230.8 6.7 %copy-start.48 = (f32[2,2,128]{2,1,0:T(2,128)}, f32[2,2,128]{2,1,0:T(2,128)S(1)}, u32[]{:S(2)}) copy-start(f32[2,2,128]{2,1,0:T(2,128)S(1)} %multiply_reduce_fusion.5) | copy-start | bytes 6148
  230.9 22.2 %copy-start.57 = (f32[2,2,128]{2,1,0:T(2,128)}, f32[2,2,128]{2,1,0:T(2,128)S(1)}, u32[]{:S(2)}) copy-start(f32[2,2,128]{2,1,0:T(2,128)S(1)} %fusion.89) | copy-start | bytes 6148
  230.9 22.3 %slice-start.5 = ((s8[4718592]{0:T(1024)(128)(4,1)}), s8[524288]{0:T(1024)(128)(4,1)S(1)}, s32[]{:S(2)}) async-start(s8[4718592]{0:T(1024)(128)(4,1)} %bitcast.297), calls=%async_computation.5 | async-start | bytes 1048576
  237.5 15.6 %copy-start.5 = (f32[2,2,128,4,768]{4,2,3,1,0:T(8,128)}, f32[2,2,128,4,768]{4,2,3,1,0:T(8,128)S(1)}, u32[]{:S(2)}) copy-start(f32[2,2,128,4,768]{4,2,3,1,0:T(8,128)S(1)} %get-tuple-element.194) | copy-start | bytes 18874372
  237.5 15.7 %copy-start.59 = (f32[768]{0:T(1024)S(1)}, f32[768]{0:T(1024)}, u32[]{:S(2)}) copy-start(f32[768]{0:T(1024)} %add.214) | copy-start | bytes 9220
  253.1 3.0 copy-start.11
  253.2 3.8 copy-start.18
  253.2 3.8 copy-start.19
  253.2 3.8 copy-start.44
  256.1 2.3 copy-start.41
  257.0 1.4 copy-start.45
  262.4 11.9 %slice-start.2 = ((s8[4718592]{0:T(1024)(128)(4,1)}), s8[4194304]{0:T(1024)(128)(4,1)S(1)}, s32[]{:S(2)}) async-start(s8[4718592]{0:T(1024)(128)(4,1)} %bitcast.293), calls=%async_computation.2 | async-start | bytes 8388608
  265.5 8.7 %slice-start.3 = ((s8[4718592]{0:T(1024)(128)(4,1)}), s8[524288]{0:T(1024)(128)(4,1)S(1)}, s32[]{:S(2)}) async-start(s8[4718592]{0:T(1024)(128)(4,1)} %bitcast.293), calls=%async_computation.3 | async-start | bytes 1048576
  265.5 8.7 %copy-start.47 = (f32[2,2,128]{2,1,0:T(2,128)S(1)}, f32[2,2,128]{2,1,0:T(2,128)}, u32[]{:S(2)}) copy-start(f32[2,2,128]{2,1,0:T(2,128)} %copy-done.46) | copy-start | bytes 6148
  265.5 8.7 %copy-start.54 = (f32[768]{0:T(1024)S(1)}, f32[768]{0:T(1024)}, u32[]{:S(2)}) copy-start(f32[768]{0:T(1024)} %mul.182) | copy-start | bytes 9220
  265.5 8.7 %copy-start.58 = (f32[2,2,128]{2,1,0:T(2,128)S(1)}, f32[2,2,128]{2,1,0:T(2,128)}, u32[]{:S(2)}) copy-start(f32[2,2,128]{2,1,0:T(2,128)} %copy-done.57) | copy-start | bytes 6148
  274.2 4.3 copy-start.61
  274.3 5.5 %copy-start.49 = (f32[2,2,128]{2,1,0:T(2,128)S(1)}, f32[2,2,128]{2,1,0:T(2,128)}, u32[]{:S(2)}) copy-start(f32[2,2,128]{2,1,0:T(2,128)} %copy-done.48) | copy-start | bytes 6148
  274.3 5.5 %copy-start.56 = (f32[768]{0:T(1024)S(1)}, f32[768]{0:T(1024)}, u32[]{:S(2)}) copy-start(f32[768]{0:T(1024)} %add.208) | copy-start | bytes 9220
  282.8 4.7 copy-start.7
  287.6 5.1 %copy-start.43 = (f32[2,2,12,128]{3,0,2,1:T(2,128)S(1)}, f32[2,2,12,128]{3,0,2,1:T(2,128)}, u32[]{:S(2)}) copy-start(f32[2,2,12,128]{3,0,2,1:T(2,128)} %copy-done.42) | copy-start | bytes 73732
  325.5 1.8 copy-start.14
  325.6 6.8 %slice-start = ((s8[6291456]{0:T(1024)(128)(4,1)}), s8[4194304]{0:T(1024)(128)(4,1)S(1)}, s32[]{:S(2)}) async-start(s8[6291456]{0:T(1024)(128)(4,1)} %bitcast.281), calls=%async_computation | async-start | bytes 8388608
  327.3 5.1 %slice-start.1 = ((s8[6291456]{0:T(1024)(128)(4,1)}), s8[2097152]{0:T(1024)(128)(4,1)S(1)}, s32[]{:S(2)}) async-start(s8[6291456]{0:T(1024)(128)(4,1)} %bitcast.281), calls=%async_computation.1 | async-start | bytes 4194304
  327.3 5.1 %copy-start.4 = (bf16[2,512,768]{1,2,0:T(8,128)(2,1)S(1)}, bf16[2,512,768]{1,2,0:T(8,128)(2,1)}, u32[]{:S(2)}) copy-start(bf16[2,512,768]{1,2,0:T(8,128)(2,1)} %copy-done.3) | copy-start | bytes 4718596
  332.4 2.1 copy-start.8
  332.4 2.1 copy-start.28
  336.7 1.6 copy-start.51
  336.7 1.6 copy-start.52
  336.7 4.6 copy-start.6
  339.1 3.5 copy-start.22
  339.1 3.5 copy-start.26
  342.5 1.4 copy-start.25
  345.5 1.7 copy-start.30
  345.5 1.9 copy-start.37
  346.8 2.5 copy-start.21
  351.7 2.5 copy-start.16
  351.7 2.5 copy-start.33
  354.2 1.8 copy-start.34
  354.2 2.6 copy-start.62
  356.8 4.7 copy-start.12
  356.8 4.7 copy-start.31
  467.6 9.5 %copy-start.10 = (f32[12,96,768]{2,1,0:T(8,128)S(1)}, f32[12,96,768]{2,1,0:T(8,128)}, u32[]{:S(2)}) copy-start(f32[12,96,768]{2,1,0:T(8,128)} %get-tuple-element.30) | copy-start | bytes 10616836
  474.9 4.6 copy-start.1
  (5 other events, 5.3 us)

commit v2 on v1

--- a/solution.py
+++ b/solution.py
@@ -10,25 +10,6 @@
 H = 12
 HD = 64
 NB = 32
-
-bucket_marks = (12, 16, 23, 32, 46, 64, 91)
-
-
-def bucket_ids(pos_rows, pos_cols):
-    delta = pos_cols[..., None, :] - pos_rows[..., :, None]
-    dist = jnp.abs(delta)
-    far = jnp.full(dist.shape, 8, jnp.int32)
-    for mark in bucket_marks:
-        far = far + (dist >= mark).astype(jnp.int32)
-    near = jnp.where(dist < 8, dist, far)
-    return near + 16 * (delta > 0).astype(jnp.int32)
-
-
-def norm_apply(value, gain, shift):
-    center = value - jnp.mean(value, axis=-1, keepdims=True)
-    var = jnp.mean(center * center, axis=-1, keepdims=True)
-    return center * lax.rsqrt(var + 1e-05) * gain + shift
-
 
 MESH = pl.DeviceIdType.MESH
 UNITS = 12
@@ -617,6 +598,492 @@
         name="reduce_grads",
     )(grads, dxs, small)
 
+
+bucket_marks = (12, 16, 23, 32, 46, 64, 91)
+MASKED = NB
+TN = (((0,), (0,)), ((), ()))
+NT = (((1,), (1,)), ((), ()))
+
+
+def dot(left, right, dims=None):
+    if dims is None:
+        dims = (((1,), (0,)), ((), ()))
+    return lax.dot_general(left, right, dims, preferred_element_type=jnp.float32)
+
+
+def fill_buckets(buckets, pos_rows, pos_cols, lengths, base, seqs, block, span):
+    for s in range(seqs):
+        delta = pos_cols[s : s + 1, :] - pos_rows[s]
+        dist = jnp.abs(delta)
+        far = jnp.full(dist.shape, 8, jnp.int32)
+        for mark in bucket_marks:
+            far = far + (dist >= mark).astype(jnp.int32)
+        bucket = jnp.where(dist < 8, dist, far) + 16 * (delta > 0).astype(jnp.int32)
+        i = base + lax.broadcasted_iota(jnp.int32, (block, span), 0)
+        j = lax.broadcasted_iota(jnp.int32, (block, span), 1)
+        valid = j < lengths[s]
+        buckets[s, 0] = jnp.where(valid & (j <= i), bucket, MASKED)
+        buckets[s, 1] = jnp.where(valid & (j < jnp.maximum(i, 1)), bucket, MASKED)
+
+
+def head_lanes(rows, half):
+    lane = lax.broadcasted_iota(jnp.int32, (rows, 2 * HD), 1)
+    return (lane < HD) if half == 0 else (lane >= HD)
+
+
+def attend_kernel(
+    seqs, block, span, seqn,
+    lengths, xc, xq, xall, weights, vectors, table, pos_rows, pos_cols,
+    probs, attended, query, keys, values,
+    buckets,
+):
+    f32, bf16 = jnp.float32, jnp.bfloat16
+    step = pl.program_id(0)
+    pairs = H // 2
+    width = H * HD
+
+    @pl.when(step == 0)
+    def _():
+        base = lax.axis_index("seq") * block
+        fill_buckets(buckets, pos_rows, pos_cols, lengths, base, seqs, block, span)
+        for t, x in enumerate((xc, xq)):
+            rows = x[...].reshape(seqs * block, width)
+            query[t] = (dot(rows, weights[0]) + vectors[0:1, :]).astype(bf16).reshape(seqs, block, width)
+
+        def project(k, carry):
+            rows = xall[k].reshape(seqs * block, width)
+            at = pl.ds(pl.multiple_of(k * block, block), block)
+            keys[:, at, :] = dot(rows, weights[1]).astype(bf16).reshape(seqs, block, width)
+            values[:, at, :] = (dot(rows, weights[2]) + vectors[1:2, :]).astype(bf16).reshape(seqs, block, width)
+            return carry
+
+        lax.fori_loop(0, seqn, project, 0)
+
+    s, pair = step // pairs, lax.rem(step, pairs)
+    lanes = pl.ds(pl.multiple_of(pair * 128, 128), 128)
+    q = query[:, s, :, lanes].reshape(2 * block, 128)
+    k = keys[s, :, lanes]
+    v = values[s, :, lanes]
+    outs = []
+    for half in range(2):
+        entry = jnp.broadcast_to(table[pl.ds(pair * 2 + half, 1), :], (block, 128))
+        bias = jnp.concatenate(
+            [
+                jnp.concatenate(
+                    [
+                        jnp.take_along_axis(entry, buckets[s, t, :, pl.ds(c * 128, 128)], axis=1, mode="promise_in_bounds")
+                        for c in range(span // 128)
+                    ],
+                    axis=1,
+                )
+                for t in range(2)
+            ],
+            axis=0,
+        )
+        mine = head_lanes(2 * block, half)
+        one = jnp.where(mine, q * 0.125, 0).astype(bf16)
+        scores = dot(one, k, NT) + bias
+        top = jnp.max(scores, axis=-1, keepdims=True)
+        expo = jnp.exp(scores - top)
+        low = (expo * (1.0 / jnp.sum(expo, axis=-1, keepdims=True))).astype(bf16)
+        probs[0, half] = low
+        outs.append(dot(low, v))
+    mixed = jnp.where(head_lanes(2 * block, 0), outs[0], outs[1]).astype(bf16)
+    attended[:, s, :, lanes] = mixed.reshape(2, block, 128)
+
+
+def attend(lengths, xc, xq, xall, weights, vectors, table, pos_rows, pos_cols):
+    seqs, block, width = xc.shape
+    seqn = xall.shape[0]
+    span = pos_cols.shape[1]
+    bf16 = jnp.bfloat16
+    steps = seqs * H // 2
+    vmem = pl.BlockSpec(memory_space=pltpu.VMEM)
+    fixed = lambda shape: pl.BlockSpec(shape, lambda i: (0,) * len(shape))
+    return pl.pallas_call(
+        functools.partial(attend_kernel, seqs, block, span, seqn),
+        grid=(steps,),
+        out_shape=(
+            jax.ShapeDtypeStruct((steps, 2, 2 * block, span), bf16),
+            jax.ShapeDtypeStruct((2, seqs, block, width), bf16),
+            jax.ShapeDtypeStruct((2, seqs, block, width), bf16),
+            jax.ShapeDtypeStruct((seqs, span, width), bf16),
+            jax.ShapeDtypeStruct((seqs, span, width), bf16),
+        ),
+        in_specs=[pl.BlockSpec(memory_space=pltpu.SMEM), vmem, vmem, vmem]
+        + [pl.BlockSpec((3, width, width), lambda i: (0, 0, 0))]
+        + [vmem] * 4,
+        out_specs=(
+            pl.BlockSpec((1, 2, 2 * block, span), lambda i: (i, 0, 0, 0)),
+            fixed((2, seqs, block, width)),
+            fixed((2, seqs, block, width)),
+            fixed((seqs, span, width)),
+            fixed((seqs, span, width)),
+        ),
+        scratch_shapes=[pltpu.VMEM((seqs, 2, block, span), jnp.int32)],
+        compiler_params=pltpu.CompilerParams(vmem_limit_bytes=60 * 1024 * 1024),
+        name="attend",
+    )(lengths, xc, xq, xall, weights, vectors, table, pos_rows, pos_cols)
+
+
+def center_of(value):
+    center = value - jnp.mean(value, axis=-1, keepdims=True)
+    var = jnp.mean(center * center, axis=-1, keepdims=True)
+    inv = lax.rsqrt(var + 1e-05)
+    return center * inv, inv
+
+
+def norm_back(grad, gain, normed, inv):
+    scaled = grad * gain
+    return inv * (
+        scaled
+        - jnp.mean(scaled, axis=-1, keepdims=True)
+        - normed * jnp.mean(scaled * normed, axis=-1, keepdims=True)
+    )
+
+
+def middle_kernel(
+    seqs, block,
+    attended, xc, xq, cot_c, cot_q, keep, vectors, weights,
+    y_c, y_q, dr1_out, da_out, grads, dvec,
+    w, hidden, hidden_low, hidden_turn, normed1, inv1, active, slope, feed, dr2, dr2_low, du_low, dr1_low, y, stage,
+    w_sem, y_sem, stage_sem, dr1_sem,
+):
+    f32, bf16 = jnp.float32, jnp.bfloat16
+    width = H * HD
+    half = seqs * block
+    rows = 2 * half
+    chunk = 128
+    loads = [pltpu.make_async_copy(weights.at[3 + i], w.at[i], w_sem.at[i]) for i in range(9)]
+    for load in loads:
+        load.start()
+    dvec[...] = jnp.zeros_like(dvec)
+    vec = lambda i: vectors[i : i + 1, :]
+
+    loads[0].wait()
+
+    def phase_one(c, carry):
+        at = pl.ds(pl.multiple_of(c * chunk, chunk), chunk)
+        out = dot(attended[at, :], w[0]) + vec(2)
+
+        def from_x(x):
+            return x[pl.ds(pl.multiple_of(lax.rem(c, half // chunk) * chunk, chunk), chunk), :].astype(f32)
+
+        x = jnp.where(c < half // chunk, from_x(xc), from_x(xq))
+        normed, inv = center_of(x + out)
+        normed1[at, :] = normed
+        inv1[at, :] = inv
+        h = normed * vec(3) + vec(4)
+        hidden[at, :] = h
+        hidden_low[at, :] = h.astype(bf16)
+        return carry
+
+    lax.fori_loop(0, rows // chunk, phase_one, 0)
+    hidden_turn[...] = hidden_low[...].T
+
+    tile = 256
+    tiles = width // tile
+    for j in range(4):
+        loads[1 + j].wait()
+
+    def phase_two(step, carry):
+        j, n = step // tiles, lax.rem(step, tiles)
+        cols = pl.ds(pl.multiple_of(n * tile, tile), tile)
+        u = dot(hidden_low[...], w[1 + j, :, cols]) + vectors[pl.ds(8 + j, 1), cols]
+        cdf = 0.5 * (1.0 + lax.erf(u * (2.0**-0.5)))
+        active[j, :, cols] = (u * cdf).astype(bf16)
+        slope[j, :, cols] = cdf + u * (jnp.exp(-0.5 * u * u) * ((2.0 * jnp.pi) ** -0.5))
+        return carry
+
+    lax.fori_loop(0, 4 * tiles, phase_two, 0)
+    for j in range(4):
+        loads[5 + j].wait()
+
+    def phase_feed(n, carry):
+        cols = pl.ds(pl.multiple_of(n * tile, tile), tile)
+        feed[:, cols] = sum(dot(active[j], w[5 + j, :, cols]) for j in range(4))
+        return carry
+
+    lax.fori_loop(0, tiles, phase_feed, 0)
+
+    def phase_three(c, carry):
+        at = pl.ds(pl.multiple_of(c * chunk, chunk), chunk)
+        normed, inv = center_of(hidden[at, :] + feed[at, :] + vec(5))
+        kept = keep[at, :]
+        y[at, :] = (normed * vec(6) + vec(7)) * kept
+        inner = pl.ds(pl.multiple_of(lax.rem(c, half // chunk) * chunk, chunk), chunk)
+        cot = jnp.where(c < half // chunk, cot_c[inner, :].astype(f32), cot_q[inner, :].astype(f32)) * kept
+        d = norm_back(cot, vec(6), normed, inv)
+        dvec[6:7, :] += jnp.sum(cot * normed, axis=0, keepdims=True)
+        dvec[7:8, :] += jnp.sum(cot, axis=0, keepdims=True)
+        dvec[5:6, :] += jnp.sum(d, axis=0, keepdims=True)
+        dr2[at, :] = d
+        dr2_low[at, :] = d.astype(bf16)
+        return carry
+
+    lax.fori_loop(0, rows // chunk, phase_three, 0)
+    y_copies = [
+        pltpu.make_async_copy(y.at[pl.ds(0, half)], y_c, y_sem.at[0]),
+        pltpu.make_async_copy(y.at[pl.ds(half, half)], y_q, y_sem.at[1]),
+    ]
+    for copy in y_copies:
+        copy.start()
+
+    def phase_four(step, carry):
+        j, n = step // tiles, lax.rem(step, tiles)
+        cols = pl.ds(pl.multiple_of(n * tile, tile), tile)
+        du = slope[j, :, cols] * dot(dr2_low[...], w[5 + j, cols, :], NT)
+        dvec[pl.ds(8 + j, 1), cols] = jnp.sum(du, axis=0, keepdims=True)
+        low = du.astype(bf16)
+        du_low[j, :, cols] = low
+        stage[j, :, cols] = dot(hidden_turn[...], low).astype(bf16)
+        stage[4 + j, cols, :] = dot(active[j, :, cols], dr2_low[...], TN).astype(bf16)
+
+        @pl.when(n == tiles - 1)
+        def _():
+            pltpu.make_async_copy(stage.at[j], grads.at[4 + j], stage_sem.at[j]).start()
+            pltpu.make_async_copy(stage.at[4 + j], grads.at[8 + j], stage_sem.at[4 + j]).start()
+
+        return carry
+
+    lax.fori_loop(0, 4 * tiles, phase_four, 0)
+
+    def phase_hidden(n, carry):
+        cols = pl.ds(pl.multiple_of(n * tile, tile), tile)
+        dr2[:, cols] += sum(dot(du_low[j], w[1 + j, cols, :], NT) for j in range(4))
+        return carry
+
+    lax.fori_loop(0, tiles, phase_hidden, 0)
+    for copy in y_copies:
+        copy.wait()
+
+    def phase_five(c, carry):
+        at = pl.ds(pl.multiple_of(c * chunk, chunk), chunk)
+        dh = dr2[at, :]
+        normed = normed1[at, :]
+        d = norm_back(dh, vec(3), normed, inv1[at, :])
+        dvec[3:4, :] += jnp.sum(dh * normed, axis=0, keepdims=True)
+        dvec[4:5, :] += jnp.sum(dh, axis=0, keepdims=True)
+        dvec[2:3, :] += jnp.sum(d, axis=0, keepdims=True)
+        y[at, :] = d
+        low = d.astype(bf16)
+        dr1_low[at, :] = low
+        da_out[at, :] = dot(low, w[0], NT).astype(bf16)
+        return carry
+
+    lax.fori_loop(0, rows // chunk, phase_five, 0)
+    dr1_copy = pltpu.make_async_copy(y, dr1_out, dr1_sem)
+    dr1_copy.start()
+
+    def phase_out(n, carry):
+        cols = pl.ds(pl.multiple_of(n * tile, tile), tile)
+        stage[8, cols, :] = dot(attended[:, cols], dr1_low[...], TN).astype(bf16)
+        return carry
+
+    lax.fori_loop(0, tiles, phase_out, 0)
+    last = pltpu.make_async_copy(stage.at[8], grads.at[3], stage_sem.at[8])
+    last.start()
+    for j in range(8):
+        pltpu.make_async_copy(stage.at[j], grads.at[4 + j], stage_sem.at[j]).wait()
+    last.wait()
+    dr1_copy.wait()
+
+
+def middle(attended, xc, xq, cot_c, cot_q, keep, vectors, weights):
+    seqs, block, width = xc.shape
+    f32, bf16 = jnp.float32, jnp.bfloat16
+    half = seqs * block
+    rows = 2 * half
+    vmem = pl.BlockSpec(memory_space=pltpu.VMEM)
+    anywhere = pl.BlockSpec(memory_space=pl.ANY)
+    flat = lambda a: a.reshape(half, width)
+    return pl.pallas_call(
+        functools.partial(middle_kernel, seqs, block),
+        out_shape=(
+            jax.ShapeDtypeStruct((half, width), f32),
+            jax.ShapeDtypeStruct((half, width), f32),
+            jax.ShapeDtypeStruct((rows, width), f32),
+            jax.ShapeDtypeStruct((rows, width), bf16),
+            jax.ShapeDtypeStruct((UNITS, width, width), bf16),
+            jax.ShapeDtypeStruct((UNITS, width), f32),
+        ),
+        in_specs=[vmem] * 7 + [anywhere],
+        out_specs=(anywhere, anywhere, anywhere, vmem, anywhere, vmem),
+        scratch_shapes=[
+            pltpu.VMEM((9, width, width), bf16),
+            pltpu.VMEM((rows, width), f32),
+            pltpu.VMEM((rows, width), bf16),
+            pltpu.VMEM((width, rows), bf16),
+            pltpu.VMEM((rows, width), f32),
+            pltpu.VMEM((rows, 1), f32),
+            pltpu.VMEM((4, rows, width), bf16),
+            pltpu.VMEM((4, rows, width), f32),
+            pltpu.VMEM((rows, width), f32),
+            pltpu.VMEM((rows, width), f32),
+            pltpu.VMEM((rows, width), bf16),
+            pltpu.VMEM((4, rows, width), bf16),
+            pltpu.VMEM((rows, width), bf16),
+            pltpu.VMEM((rows, width), f32),
+            pltpu.VMEM((9, width, width), bf16),
+            pltpu.SemaphoreType.DMA((9,)),
+            pltpu.SemaphoreType.DMA((2,)),
+            pltpu.SemaphoreType.DMA((9,)),
+            pltpu.SemaphoreType.DMA(()),
+        ],
+        compiler_params=pltpu.CompilerParams(vmem_limit_bytes=63 * 1024 * 1024),
+        name="middle",
+    )(attended, flat(xc), flat(xq), flat(cot_c), flat(cot_q), keep, vectors, weights)
+
+
+def attend_back_kernel(
+    seqs, block, span, seqn,
+    lengths, xc, xq, xall, weights, pos_rows, pos_cols, probs, attended, d_attended, query, keys, values, dr1, grads_in,
+    grads, d_content, d_query_x, dxs, dvec, counts,
+    buckets, dq, dk, dv, ds_sum, stage, grads_low, stage_sem,
+):
+    f32, bf16 = jnp.float32, jnp.bfloat16
+    step = pl.program_id(0)
+    pairs = H // 2
+    width = H * HD
+    rows = 2 * block
+
+    @pl.when(step == 0)
+    def _():
+        base = lax.axis_index("seq") * block
+        fill_buckets(buckets, pos_rows, pos_cols, lengths, base, seqs, block, span)
+        counts[...] = jnp.zeros_like(counts)
+
+    s, pair = step // pairs, lax.rem(step, pairs)
+    lanes = pl.ds(pl.multiple_of(pair * 128, 128), 128)
+    q = query[:, s, :, lanes].reshape(rows, 128)
+    k = keys[s, :, lanes]
+    v = values[s, :, lanes]
+    da = d_attended[:, s, :, lanes].reshape(rows, 128)
+    product = da.astype(f32) * attended[:, s, :, lanes].reshape(rows, 128).astype(f32)
+    d_queries, dk_turn, dv_turn = [], 0.0, 0.0
+    for half in range(2):
+        mine = head_lanes(rows, half)
+        one = jnp.where(mine, da, 0).astype(bf16)
+        inner = jnp.sum(jnp.where(mine, product, 0.0), axis=-1, keepdims=True)
+        low = probs[0, half]
+        ds = low.astype(f32) * (dot(one, v, NT) - inner)
+        ds_sum[pair * 2 + half] = (ds[:block] + ds[block:]).astype(bf16)
+        ds_low = ds.astype(bf16)
+        d_queries.append(dot(ds_low, k))
+        dk_turn += dot(jnp.where(mine, q, 0).astype(bf16), ds_low, TN)
+        dv_turn += dot(one, low, TN)
+    d_query = jnp.where(head_lanes(rows, 0), d_queries[0], d_queries[1]) * 0.125
+    dq[:, s, :, lanes] = d_query.reshape(2, block, 128)
+    dk[s, :, lanes] = (dk_turn * 0.125).T.astype(bf16)
+    dv[s, :, lanes] = dv_turn.T
+
+    @pl.when(pair == pairs - 1)
+    def _():
+        def count(g, carry):
+            at = pl.ds(pl.multiple_of(g * 16, 16), 16)
+            bucket = buckets[s, 0, at, :]
+            hot = jnp.concatenate(
+                [jnp.where(bucket == n, 1.0, 0.0).astype(bf16) for n in range(NB)], axis=0
+            )
+            counts[...] += dot(hot, ds_sum[:, at, :].reshape(H * 16, span), NT)
+            return carry
+
+        lax.fori_loop(0, block // 16, count, 0)
+
+    @pl.when(step == seqs * pairs - 1)
+    def _():
+        all_rows = 2 * seqs * block
+        dvec[...] = jnp.zeros_like(dvec)
+        dvec[0:1, :] = jnp.sum(dq[...].reshape(all_rows, width), axis=0, keepdims=True)
+        dvec[1:2, :] = jnp.sum(dv[...].reshape(seqs * span, width), axis=0, keepdims=True)
+        for t, (x, out) in enumerate(((xc, d_content), (xq, d_query_x))):
+            low = dq[t].reshape(seqs * block, width).astype(bf16)
+            out[...] = dr1[pl.ds(t * seqs * block, seqs * block), :] + dot(low, weights[0], NT)
+            piece = dot(x[...].reshape(seqs * block, width), low, TN)
+            stage[t] = piece
+        low_q = (stage[0] + stage[1]).astype(bf16)
+
+        def every(k, carry):
+            at = pl.ds(pl.multiple_of(k * block, block), block)
+            x = xall[k].reshape(seqs * block, width)
+            low_k = dk[:, at, :].reshape(seqs * block, width)
+            low_v = dv[:, at, :].reshape(seqs * block, width).astype(bf16)
+            dxs[k] = (dot(low_k, weights[1], NT) + dot(low_v, weights[2], NT)).astype(bf16)
+            turned = x.T
+
+            @pl.when(k == 0)
+            def _():
+                stage[0] = dot(turned, low_k)
+                stage[1] = dot(turned, low_v)
+
+            @pl.when(k > 0)
+            def _():
+                stage[0] += dot(turned, low_k)
+                stage[1] += dot(turned, low_v)
+
+            return carry
+
+        grads_low[0] = low_q
+        lax.fori_loop(0, seqn, every, 0)
+        grads_low[1] = stage[0].astype(bf16)
+        grads_low[2] = stage[1].astype(bf16)
+        for i in range(3):
+            pltpu.make_async_copy(grads_low.at[i], grads.at[i], stage_sem.at[i]).start()
+        for i in range(3):
+            pltpu.make_async_copy(grads_low.at[i], grads.at[i], stage_sem.at[i]).wait()
+
+
+def attend_back(lengths, xc, xq, xall, weights, pos_rows, pos_cols, probs, attended, d_attended, query, keys, values, dr1, grads):
+    seqs, block, width = xc.shape
+    seqn = xall.shape[0]
+    span = pos_cols.shape[1]
+    f32, bf16 = jnp.float32, jnp.bfloat16
+    steps = seqs * H // 2
+    vmem = pl.BlockSpec(memory_space=pltpu.VMEM)
+    anywhere = pl.BlockSpec(memory_space=pl.ANY)
+    fixed = lambda shape: pl.BlockSpec(shape, lambda i: (0,) * len(shape))
+    own = (seqs * block, width)
+    return pl.pallas_call(
+        functools.partial(attend_back_kernel, seqs, block, span, seqn),
+        grid=(steps,),
+        out_shape=(
+            jax.ShapeDtypeStruct(grads.shape, bf16),
+            jax.ShapeDtypeStruct(own, f32),
+            jax.ShapeDtypeStruct(own, f32),
+            jax.ShapeDtypeStruct((seqn,) + own, bf16),
+            jax.ShapeDtypeStruct((8, width), f32),
+            jax.ShapeDtypeStruct((NB * 16, H * 16), f32),
+        ),
+        in_specs=[pl.BlockSpec(memory_space=pltpu.SMEM), vmem, vmem, vmem]
+        + [pl.BlockSpec((3, width, width), lambda i: (0, 0, 0))]
+        + [vmem] * 2
+        + [pl.BlockSpec((1, 2, 2 * block, span), lambda i: (i, 0, 0, 0))]
+        + [vmem] * 6
+        + [anywhere],
+        out_specs=(
+            anywhere,
+            fixed(own),
+            fixed(own),
+            fixed((seqn,) + own),
+            fixed((8, width)),
+            fixed((NB * 16, H * 16)),
+        ),
+        scratch_shapes=[
+            pltpu.VMEM((seqs, 2, block, span), jnp.int32),
+            pltpu.VMEM((2, seqs, block, width), f32),
+            pltpu.VMEM((seqs, span, width), bf16),
+            pltpu.VMEM((seqs, span, width), f32),
+            pltpu.VMEM((H, block, span), bf16),
+            pltpu.VMEM((2, width, width), f32),
+            pltpu.VMEM((3, width, width), bf16),
+            pltpu.SemaphoreType.DMA((3,)),
+        ],
+        input_output_aliases={14: 0},
+        compiler_params=pltpu.CompilerParams(vmem_limit_bytes=62 * 1024 * 1024),
+        name="attend_back",
+    )(lengths, xc, xq, xall, weights, pos_rows, pos_cols, probs, attended, d_attended, query, keys, values, dr1, grads)
+
+
 def per_device(
     x_content, x_query, cot_content, cot_query,
     w_query, b_query, w_key, w_value, b_value, w_out, b_out, gain_attn, shift_attn,
@@ -624,127 +1091,57 @@
     *, shards, seqn,
 ):
     f32 = jnp.float32
-    bf16 = jnp.bfloat16
-    scale = HD ** (-0.5)
     seqs, block, width = x_content.shape
-    span = positions.shape[1]
     r = w_query.shape[0]
     vec = jnp.concatenate(
         [b_query, b_value, b_out, gain_attn, shift_attn, b_down, gain_ffn, shift_ffn, b_up]
     ).astype(f32)[None]
     full, xall, vall = gather(w_query, w_key, w_value, w_out, w_up, w_down, x_content, vec, shards, seqn)
     weights = full.reshape(UNITS, width, width)
-    wq, wk, wv, wo = (weights[i] for i in range(4))
-    w1, w2 = weights[4:8], weights[8:12]
-    bq, bv, bo, g1, b1, c2, g2, b2 = (vall[:, 0, i * r : (i + 1) * r].reshape(width) for i in range(8))
-    c1 = vall[:, 0, 8 * r :].reshape(4, width)
-    x_every = jnp.transpose(xall, (1, 0, 2, 3)).reshape(seqs, span, width)
-
+    eight = jnp.transpose(vall[:, 0, : 8 * r].reshape(shards, 8, r), (1, 0, 2)).reshape(8, width)
+    vectors = jnp.concatenate([eight, vall[:, 0, 8 * r :].reshape(4, width)])
     base = lax.axis_index("seq") * block
-    slot_q = base + jnp.arange(block)
-    slot_k = jnp.arange(span)
-    valid_k = slot_k[None, :] < lengths[:, None]
-    valid_q = slot_q[None, :] < lengths[:, None]
-    allow_c = valid_k[:, None, :] & (slot_k[None, :] <= slot_q[:, None])[None]
-    allow_q = valid_k[:, None, :] & (slot_k[None, :] < jnp.maximum(slot_q[:, None], 1))[None]
-    allowed = jnp.stack([allow_c, allow_q])
-    pos_q = lax.dynamic_slice_in_dim(positions, base, block, 1)
-    onehot = (bucket_ids(pos_q, positions)[..., None] == jnp.arange(NB)).astype(f32)
-    table = rel_table.astype(f32)
-    bias = jnp.einsum("sqkn,nh->shqk", onehot, table, precision=lax.Precision.HIGHEST)
-    xs = jnp.stack([x_content, x_query])
-    keys = jnp.einsum("sqd,de->sqe", x_every, wk, preferred_element_type=f32).astype(bf16)
-    values = (jnp.einsum("sqd,de->sqe", x_every, wv, preferred_element_type=f32) + bv).astype(bf16)
-    query = (jnp.einsum("tsqd,de->tsqe", xs, wq, preferred_element_type=f32) + bq).astype(bf16)
-    query4 = query.reshape(2, seqs, block, H, HD)
-    keys4 = keys.reshape(seqs, span, H, HD)
-    values4 = values.reshape(seqs, span, H, HD)
-
-    raw = jnp.einsum("tsqhe,skhe->tshqk", query4, keys4, preferred_element_type=f32)
-    scores = jnp.where(allowed[:, :, None], raw * scale + bias[None], -1e30)
-    top = jnp.max(scores, axis=-1, keepdims=True)
-    expo = jnp.exp(scores - top)
-    probs = expo / jnp.sum(expo, axis=-1, keepdims=True)
-    mixed = jnp.einsum("tshqk,skhe->tsqhe", probs.astype(bf16), values4, preferred_element_type=f32)
-    attended = mixed.reshape(2, seqs, block, width).astype(bf16)
-    out = jnp.einsum("tsqd,de->tsqe", attended, wo, preferred_element_type=f32) + bo
-    resid_one = xs.astype(f32) + out
-    hidden, pull_one = jax.vjp(norm_apply, resid_one, g1, b1)
-    hidden_low = hidden.astype(bf16)
-    upper = jnp.einsum("tsqd,jdf->tsqjf", hidden_low, w1, preferred_element_type=f32) + c1
-    active_full, pull_gelu = jax.vjp(lambda value: jax.nn.gelu(value, approximate=False), upper)
-    active = active_full.astype(bf16)
-    feed = jnp.einsum("tsqjf,jfd->tsqd", active, w2, preferred_element_type=f32) + c2
-    result, pull_two = jax.vjp(norm_apply, hidden + feed, g2, b2)
-    keep = jnp.stack([valid_q, valid_q & (predicted > 0)])[..., None].astype(f32)
-    outputs = result * keep
-    cotangent = jnp.stack([cot_content, cot_query]).astype(f32) * keep
-    d_resid_two, d_g2, d_b2 = pull_two(cotangent)
-    d_c2 = jnp.sum(d_resid_two, axis=(0, 1, 2))
-    d_feed_low = d_resid_two.astype(bf16)
-    d_w2 = jnp.einsum("tsqjf,tsqd->jfd", active, d_feed_low, preferred_element_type=f32)
-    d_active = jnp.einsum("tsqd,jfd->tsqjf", d_feed_low, w2, preferred_element_type=f32)
-    (d_upper,) = pull_gelu(d_active)
-    d_c1 = jnp.sum(d_upper, axis=(0, 1, 2)).reshape(4 * width)
-    d_upper_low = d_upper.astype(bf16)
-    d_w1 = jnp.einsum("tsqd,tsqjf->jdf", hidden_low, d_upper_low, preferred_element_type=f32)
-    d_hidden = d_resid_two + jnp.einsum("tsqjf,jdf->tsqd", d_upper_low, w1, preferred_element_type=f32)
-    d_resid_one, d_g1, d_b1 = pull_one(d_hidden)
-    d_bo = jnp.sum(d_resid_one, axis=(0, 1, 2))
-    d_out_low = d_resid_one.astype(bf16)
-    d_wo = jnp.einsum("tsqd,tsqe->de", attended, d_out_low, preferred_element_type=f32)
-    d_attended = jnp.einsum("tsqe,de->tsqd", d_out_low, wo, preferred_element_type=f32).astype(bf16)
-    d_mixed = d_attended.reshape(2, seqs, block, H, HD)
-    d_probs = jnp.einsum("tsqhe,skhe->tshqk", d_mixed, values4, preferred_element_type=f32)
-    d_scores = probs * (d_probs - jnp.sum(d_probs * probs, axis=-1, keepdims=True))
-    d_table = jnp.einsum(
-        "shqk,sqkn->nh", jnp.sum(d_scores, axis=0), onehot, precision=lax.Precision.HIGHEST
+    pos_rows = lax.dynamic_slice_in_dim(positions, base, block, 1)[..., None]
+    table = jnp.full((H, 128), -1e30, f32).at[:, :NB].set(rel_table.astype(f32).T)
+    valid = (base + jnp.arange(block))[None, :] < lengths[:, None]
+    keep = jnp.stack([valid, valid & (predicted > 0)]).astype(f32).reshape(2 * seqs * block, 1)
+
+    probs, attended, query, keys, values = attend(
+        lengths, x_content, x_query, xall, weights, vectors, table, pos_rows, positions
     )
-    d_raw = (d_scores * scale).astype(bf16)
-    d_query = jnp.einsum("tshqk,skhe->tsqhe", d_raw, keys4, preferred_element_type=f32).reshape(
-        2, seqs, block, width
+    y_c, y_q, dr1, d_attended, grads, dvec = middle(
+        attended.reshape(2 * seqs * block, width), x_content, x_query, cot_content, cot_query, keep, vectors, weights
     )
-    d_keys = jnp.einsum("tshqk,tsqhe->skhe", d_raw, query4, preferred_element_type=f32).reshape(
-        seqs, span, width
+    grads, d_content, d_query_x, dxs, dvec_qv, counts = attend_back(
+        lengths, x_content, x_query, xall, weights, pos_rows, positions, probs,
+        attended, d_attended.reshape(attended.shape), query, keys, values, dr1, grads,
     )
-    d_values = jnp.einsum(
-        "tshqk,tsqhe->skhe", probs.astype(bf16), d_mixed, preferred_element_type=f32
-    ).reshape(seqs, span, width)
-    d_bq = jnp.sum(d_query, axis=(0, 1, 2))
-    d_bv = jnp.sum(d_values, axis=(0, 1))
-    d_query_low = d_query.astype(bf16)
-    d_key_low = d_keys.astype(bf16)
-    d_value_low = d_values.astype(bf16)
-    d_wq = jnp.einsum("tsqd,tsqe->de", xs, d_query_low, preferred_element_type=f32)
-    d_wk = jnp.einsum("sqd,sqe->de", x_every, d_key_low, preferred_element_type=f32)
-    d_wv = jnp.einsum("sqd,sqe->de", x_every, d_value_low, preferred_element_type=f32)
-    d_inputs = d_resid_one + jnp.einsum("tsqe,de->tsqd", d_query_low, wq, preferred_element_type=f32)
-    d_every = jnp.einsum("sqe,de->sqd", d_key_low, wk, preferred_element_type=f32) + jnp.einsum(
-        "sqe,de->sqd", d_value_low, wv, preferred_element_type=f32
-    )
-    dxs = jnp.transpose(d_every.astype(bf16).reshape(seqs, seqn, block, width), (1, 0, 2, 3))
-    grads = jnp.concatenate(
-        [jnp.stack([d_wq, d_wk, d_wv, d_wo]).astype(bf16), d_w1.astype(bf16), d_w2.astype(bf16)]
-    ).reshape(UNITS * shards, r, width)
+    same = jnp.arange(16)[:, None] == jnp.arange(16)[None, :]
+    d_table = jnp.sum(jnp.where(same[None, :, None, :], counts.reshape(NB, 16, H, 16), 0.0), axis=(1, 3))
+    eight = jnp.concatenate([dvec_qv[:2], dvec[2:8]])
     small = jnp.concatenate(
-        [d.reshape(shards, 1, r) for d in (d_bq, d_bv, d_bo, d_g1, d_b1, d_c2, d_g2, d_b2)]
-        + [d_c1.reshape(shards, 1, 4 * r), jnp.broadcast_to(d_table.reshape(1, 1, NB * H), (shards, 1, NB * H))],
+        [
+            jnp.transpose(eight.reshape(8, shards, r), (1, 0, 2)).reshape(shards, 8 * r),
+            dvec[8:].reshape(shards, 4 * r),
+            jnp.broadcast_to(d_table.reshape(1, NB * H), (shards, NB * H)),
+        ],
         axis=-1,
-    )
-    sums, dx, tiny = reduce_grads(grads, dxs.reshape(seqn, seqs * block, width), small, shards, seqn)
-    grad_content = d_inputs[0] + dx.reshape(seqs, block, width)
+    )[:, None]
+    sums, dx, tiny = reduce_grads(grads.reshape(UNITS * shards, r, width), dxs, small, shards, seqn)
+    shape = (seqs, block, width)
+    grad_content = (d_content + dx).reshape(shape)
     tiny = tiny[0]
-    pieces = [tiny[i * r : (i + 1) * r] for i in range(8)]
-    g_bq, g_bv, g_bo, g_g1, g_b1, g_c2, g_g2, g_b2 = pieces
+    g_bq, g_bv, g_bo, g_g1, g_b1, g_c2, g_g2, g_b2 = (tiny[i * r : (i + 1) * r] for i in range(8))
     g_c1 = tiny[8 * r : 12 * r]
     g_table = tiny[12 * r :].reshape(NB, H)
     g_w1 = jnp.transpose(sums[4:8], (1, 0, 2)).reshape(r, 4 * width)
     g_w2 = sums[8:12].reshape(4 * r, width)
     return (
-        outputs[0], outputs[1], grad_content, d_inputs[1],
+        y_c.reshape(shape), y_q.reshape(shape), grad_content, d_query_x.reshape(shape),
         sums[0], g_bq, sums[1], sums[2], g_bv, sums[3], g_bo, g_g1, g_b1,
         g_w1, g_c1, g_w2, g_c2, g_g2, g_b2, g_table,
     )
+
 
 def solution(mesh):
     in_specs = (

time: 484 us -> 307 us (0.63)
  local copies, waits for them, and re-layouts: 139 us -> 18.5 us
  matrix products: 119 us -> 0 us
  Pallas kernels: 176 us -> 283 us
  other arithmetic: 43.5 us -> 4.16 us
    pallas_call x0 -> x3, Pallas kernels: none -> 106 us  [the longest x1 40.5 us: middle(): pl.pallas_call(functools.partial(middle_kernel, seqs, block), out_shape=(...]
    dot_general x24 -> x0, matrix products: 91.3 us -> none  [the longest x1 13.5 us: per_device(): jnp.einsum('shqk,sqkn->nh', jnp.sum(d_scores, axis=0), onehot, precision=...]
    eq x1 -> x0, local copies, waits for them, and re-layouts: 74.6 us -> none  [per_device(): bucket_ids(pos_q, positions)[..., None] == jnp.arange(NB)]
    sub x2 -> x0, matrix products: 27.4 us -> none  [the longest x1 17.6 us: per_device(): d_probs - jnp.sum(d_probs * probs, axis=-1, keepdims=True)]
    convert_element_type x3 -> x1, other arithmetic: 22.4 us -> 0.01 us  [per_device(): jnp.stack([valid, valid & (predicted > 0)]).astype(f32)]
    slice x5 -> x6, local copies, waits for them, and re-layouts: 14.1 us -> 2.9 us  [the longest x1 0.8 us: per_device(): vall[:, 0, :8 * r].reshape(shards, 8, r)]
    transpose x2 -> x0, local copies, waits for them, and re-layouts: 10.7 us -> none  [the longest x1 9.15 us: per_device(): jnp.einsum('sqkn,nh->shqk', onehot, table, precision=lax.Precision.HIGHEST)]
    reduce_sum x9 -> x1, other arithmetic: 9.83 us -> 0.43 us  [per_device(): jnp.sum(jnp.where(same[None, :, None, :], counts.reshape(NB, 16, H, 16),...]
where the time goes in v2:
time: 307 us; the launch traced here: 306 us
  Pallas kernels  283 us (92%)
  local copies, waits for them, and re-layouts  18.5 us (6%)
  other arithmetic  4.16 us (1%)
    pallas_call x1, Pallas kernels, reduce_grads(): pl.pallas_call(functools.partial(reduce_kernel, shards, seqn), out_shape=...  102 us
    pallas_call x1, Pallas kernels, gather(): pl.pallas_call(functools.partial(gather_kernel, shards, seqn), out_shape=...  74.4 us
    pallas_call x1, Pallas kernels, middle(): pl.pallas_call(functools.partial(middle_kernel, seqs, block), out_shape=(...  40.5 us
    pallas_call x1, Pallas kernels, attend_back(): pl.pallas_call(functools.partial(attend_back_kernel, seqs, block, span, s...  34.8 us
    pallas_call x1, Pallas kernels, attend(): pl.pallas_call(functools.partial(attend_kernel, seqs, block, span, seqn),...  31.1 us

profile of v2, /device:TPU:1, one launch (start us, length us, event | category | flops | bytes accessed | tf_op | source)
XLA Modules:
  0.0 306.2 jit_solution(8239244008038286936)
XLA Ops:
  0.7 0.7 dynamic-slice_bitcast_fusion
  1.3 0.8 copy.56.pos_rows
  2.1 0.7 concatenate.47
  2.8 0.9 concatenate.48
  3.7 0.6 convert_element_type.26.vec
  4.3 74.4 %gather_weights.1 = (bf16[96,96,768]{2,1,0:T(8,128)(2,1)}, bf16[4,2,128,768]{3,2,1,0:T(8,128)(2,1)}, f32[8,1,1152]{2,1,0:T(1,128)}) custom-call(bf16[96,768]{1,0:T(8,128)(2,1)} %wq.1, bf16[96,768]{1,0:T(8,128)(2,1)} %wk.1, bf16[96,768]{1,0:T(8,128)(2,1)} %wv.1, bf16[96,768]{1,0:T(8,128)(2,1)} %wo.1, bf16[96,3072]{1,0:T(8,128)(2,1)} %wu.1, ...), custom_call_target="tpu_custom_call" | custom-call | tf_op jit(solution)/shard_map/gather_weights/pallas_call | solution.py:250
  78.7 0.8 slice_reduce_fusion
  79.5 0.1 reshape_squeeze.6
  79.6 0.1 reshape.335
  79.7 0.7 slice_reduce_fusion.1
  80.5 0.0 copy-start.2
  80.5 0.6 compare_reduce_fusion
  81.1 1.3 select_bitcast_fusion
  82.5 0.6 scatter.4.table
  83.1 0.0 copy-done.2
  83.1 0.0 copy-start.5
  83.1 0.0 copy-start.6
  83.1 31.1 %attend.1 = (bf16[12,2,256,512]{3,2,1,0:T(8,128)(2,1)}, bf16[2,2,128,768]{3,2,1,0:T(8,128)(2,1)}, bf16[2,2,128,768]{3,2,1,0:T(8,128)(2,1)}, bf16[2,512,768]{2,1,0:T(8,128)(2,1)}, bf16[2,512,768]{2,1,0:T(8,128)(2,1)}) custom-call(s32[2]{0:T(128)} %lengths.3, bf16[2,128,768]{2,1,0:T(8,128)(2,1)} %xc.5, bf16[2,128,768]{2,1,0:T(8,128)(2,1)} %xq.3, ...), custom_call_target="tpu_custom_call" | custom-call | tf_op jit(solution)/shard_map/attend/pallas_call | solution.py:703
  114.1 0.0 copy-done.5
  114.1 0.0 copy-done.6
  114.2 0.1 and_bitcast_fusion
  114.2 0.1 broadcast_compare_fusion
  114.3 0.9 copy.57.keep
  115.2 40.5 %middle.1 = (f32[256,768]{1,0:T(8,128)}, f32[256,768]{1,0:T(8,128)}, f32[512,768]{1,0:T(8,128)}, bf16[512,768]{1,0:T(8,128)(2,1)}, bf16[12,768,768]{2,1,0:T(8,128)(2,1)}, /*index=5*/f32[12,768]{1,0:T(8,128)}) custom-call(bf16[512,768]{1,0:T(8,128)(2,1)} %bitcast.71, bf16[256,768]{1,0:T(8,128)(2,1)} %bitcast.69, bf16[256,768]{1,0:T(8,128)(2,1)} %bitcast.70, ...), custom_call_target="tpu_custom_call" | custom-call | tf_op jit(solution)/shard_map/middle/pallas_call | solution.py:900
  155.7 34.8 %attend_back.1 = (bf16[12,768,768]{2,1,0:T(8,128)(2,1)}, f32[256,768]{1,0:T(8,128)}, f32[256,768]{1,0:T(8,128)}, bf16[4,256,768]{2,1,0:T(8,128)(2,1)}, f32[8,768]{1,0:T(8,128)}, /*index=5*/f32[512,192]{1,0:T(8,128)}) custom-call(s32[2]{0:T(128)} %lengths.3, bf16[2,128,768]{2,1,0:T(8,128)(2,1)} %xc.5, ...), custom_call_target="tpu_custom_call", output_to_operand_aliasing={{0}: (14, {})} | custom-call | tf_op jit(solution)/shard_map/attend_back/pallas_call | solution.py:1046
  190.6 1.2 copy.60
  191.8 1.1 reshape.348
  192.9 0.0 copy-start.3
  192.9 0.4 select_reduce_fusion
  193.3 0.1 copy.61
  193.4 0.1 reshape.359
  193.5 0.7 slice.109
  194.3 0.0 copy-done.3
  194.3 0.1 reshape.345
  194.4 0.1 reshape.346
  194.5 0.7 broadcast_in_dim.37.small
  195.2 101.9 %reduce_grads.1 = (f32[12,96,768]{2,1,0:T(8,128)}, f32[256,768]{1,0:T(8,128)}, f32[1,1536]{1,0:T(1,128)}) custom-call(bf16[96,96,768]{2,1,0:T(8,128)(2,1)} %bitcast.68, bf16[4,256,768]{2,1,0:T(8,128)(2,1)} %get-tuple-element.70.dxs, f32[8,1,1536]{2,1,0:T(1,128)} %broadcast_in_dim.37.small), custom_call_target="tpu_custom_call" | custom-call | tf_op jit(solution)/shard_map/reduce_grads/pallas_call | solution.py:546
  297.0 2.8 fusion
  299.8 0.0 copy-start
  299.8 0.0 copy-start.1
  299.8 0.0 copy-start.4
  299.8 1.1 copy.64
  301.0 2.3 slice_bitcast_fusion.1
  303.2 0.0 copy-done
  303.2 0.0 copy-done.1
  303.2 1.0 add.23
  304.2 0.0 copy-done.4
  304.2 0.6 slice_reduce_fusion.2
  304.8 0.1 reshape.353
  304.9 0.7 copy.63
  305.6 0.6 slice_bitcast_fusion.5
  (14 shorter events, 0.1 us)
Async XLA Ops:
  80.5 2.6 copy-start.2
  83.1 31.1 %copy-start.5 = (s32[2]{0:T(128)S(1)}, s32[2]{0:T(128)}, u32[]{:S(2)}) copy-start(s32[2]{0:T(128)} %lengths.3) | copy-start | bytes 28
  83.1 31.1 %copy-start.6 = (s32[2,128]{1,0:T(2,128)S(1)}, s32[2,128]{1,0:T(2,128)}, u32[]{:S(2)}) copy-start(s32[2,128]{1,0:T(2,128)} %param.47) | copy-start | bytes 3076
  192.9 1.4 copy-start.3
  299.8 3.4 %copy-start = (f32[256,768]{1,0:T(8,128)S(1)}, f32[256,768]{1,0:T(8,128)}, u32[]{:S(2)}) copy-start(f32[256,768]{1,0:T(8,128)} %get-tuple-element.68) | copy-start | bytes 2359300
  299.8 3.4 %copy-start.1 = (f32[256,768]{1,0:T(8,128)S(1)}, f32[256,768]{1,0:T(8,128)}, u32[]{:S(2)}) copy-start(f32[256,768]{1,0:T(8,128)} %get-tuple-element.74) | copy-start | bytes 2359300
  299.8 4.4 %copy-start.4 = (f32[1,1536]{1,0:T(1,128)S(1)}, f32[1,1536]{1,0:T(1,128)}, u32[]{:S(2)}) copy-start(f32[1,1536]{1,0:T(1,128)} %get-tuple-element.77) | copy-start | bytes 18436

commit v3 on v0

v3 whole, which is shorter than its diff:
```python
import functools

import jax
import jax.numpy as jnp
from jax import lax
from jax.experimental import pallas as pl
from jax.experimental.pallas import tpu as pltpu
from jax.sharding import PartitionSpec as P

H = 12
HD = 64
NB = 32

MESH = pl.DeviceIdType.MESH
UNITS = 12


def cutter(rows_of):
    by_rows = rows_of % 96 == 0
    piece = rows_of // 6 if by_rows else 128

    def cut(start, size):
        if not isinstance(start, int):
            start = pl.multiple_of(start * piece, 16 if by_rows else 128)
        else:
            start = start * piece
        inner = pl.ds(start, size * piece)
        return (inner, slice(None)) if by_rows else (slice(None), inner)

    def shape(size):
        return (size * piece, 768) if by_rows else (rows_of, size * piece)

    return cut, shape


def place():
    dp, sq = lax.axis_index("dp"), lax.axis_index("seq")
    row, side = dp // 2, dp % 2
    deck, core = sq // 2, sq % 2
    return dp, sq, row, side, deck, core


def tile_of(unit, shard, shards):
    down = unit // 8
    return (1 - down) * (unit * shards + shard) + down * (8 * shards + shard * 4 + unit - 8)


def remote(src, dst, send, recv, device):
    return pltpu.make_async_remote_copy(
        src_ref=src, dst_ref=dst, send_sem=send, recv_sem=recv, device_id=device, device_id_type=MESH
    )


def greet_all(dp, sq, shards, seqn):
    barrier = pltpu.get_barrier_semaphore()

    def greet(step, carry):
        pl.semaphore_signal(barrier, inc=1, device_id=(lax.rem(dp + step, shards), sq), device_id_type=MESH)
        return carry

    def greet_seq(step, carry):
        pl.semaphore_signal(barrier, inc=1, device_id=(dp, lax.rem(sq + step, seqn)), device_id_type=MESH)
        return carry

    lax.fori_loop(1, shards, greet, 0)
    lax.fori_loop(1, seqn, greet_seq, 0)
    return barrier, shards + seqn - 2


AHEAD = 2


def gather_steps(shards, seqn, ins, outs, scratch):
    wk, wv, wq, wo, wu, wd, xc, vec = ins
    full, xall, vall = outs
    (own, xown, load_sem, keep_sem, zu_sem, zd_sem, xs_sem, ys_sem, cp_sem, cy_sem,
     zr_sem, xr_sem, yr_sem, cpr_sem, cyr_sem, xc_send, xc_recv, vec_send, vec_recv) = scratch
    dp, sq, row, side, deck, core = place()
    rows = shards // 2
    across = (row * 2 + 1 - side, sq)
    other_deck = (dp, (1 - deck) * 2 + core)
    sibling = (dp, deck * 2 + 1 - core)
    cut, _ = cutter(own.shape[1])
    plane = cut(core * 3 + deck, 2)
    solo = cut(core * 3 + deck * 2, 1)
    theirs = cut(core * 3 + (1 - deck) * 2, 1)

    def many(count, size):
        return full.at[(pl.ds(0, count),) + cut(0, size)]

    def part(unit, shard, piece):
        return full.at[(tile_of(unit, shard, shards),) + piece]

    pieces = [wk, wv, wq, wo] + [wu.at[:, pl.ds(j * 768, 768)] for j in range(4)] + [wd.at[j] for j in range(4)]
    loads = [pltpu.make_async_copy(piece, own.at[u], load_sem.at[u]) for u, piece in enumerate(pieces)]
    xload = pltpu.make_async_copy(xc, xown, load_sem.at[UNITS])
    keep_x = pltpu.make_async_copy(xown, xall.at[sq], keep_sem.at[UNITS])
    keep_vec = pltpu.make_async_copy(vec, vall.at[dp], keep_sem.at[UNITS + 1])
    x_deck = remote(xown, xall.at[sq], xc_send.at[0], xc_recv.at[0], other_deck)
    x_core = remote(xown, xall.at[sq], xc_send.at[1], xc_recv.at[1], sibling)
    x_theirs = xall.at[(1 - deck) * 2 + core]
    x_forward = remote(x_theirs, x_theirs, xc_send.at[2], xc_recv.at[2], sibling)

    def keep_copy(u):
        return pltpu.make_async_copy(own.at[u], full.at[tile_of(u, dp, shards)], keep_sem.at[u])

    up = ((row + 1) * 2 + side, sq)
    down = ((row - 1) * 2 + side, sq)

    def along(u, s, src):
        dst = part(u, s * 2 + side, plane)

        @pl.when((s <= row) & (row < rows - 1))
        def _():
            remote(src, dst, zu_sem.at[s], zr_sem.at[u, s], up).start()

        @pl.when((s >= row) & (row > 0))
        def _():
            remote(src, dst, zd_sem.at[s], zr_sem.at[u, s], down).start()

    def send_own(u):
        along(u, row, own.at[(u,) + plane])
        across_own(u)

    def across_own(u):
        remote(own.at[(u,) + plane], part(u, dp, plane), xs_sem, xr_sem.at[u], across).start()

    def to_deck(u, shard):
        ref = part(u, shard, solo)
        remote(ref, ref, ys_sem, yr_sem.at[u], other_deck).start()

    def to_core(u, shard):
        ref = part(u, shard, plane)
        remote(ref, ref, cp_sem, cpr_sem.at[u], sibling).start()

    def begin():
        barrier, count = greet_all(dp, sq, shards, seqn)
        for load in loads:
            load.start()
        xload.start()
        pl.semaphore_wait(barrier, count)

        def send_vec(step, carry):
            to = (lax.rem(dp + step, shards), sq)
            remote(vec, vall.at[dp], vec_send, vec_recv, to).start()
            return carry

        lax.fori_loop(1, shards, send_vec, 0)
        keep_vec.start()
        for load in loads:
            load.wait()

        def first(u, carry):
            send_own(u)
            return carry

        lax.fori_loop(0, AHEAD, first, 0)

        def keep(u, carry):
            keep_copy(u).start()
            return carry

        lax.fori_loop(0, UNITS, keep, 0)
        xload.wait()
        keep_x.start()
        x_deck.start()
        x_core.start()

    def step(n):
        @pl.when(n + AHEAD < UNITS)
        def _():
            send_own(n + AHEAD)

        def hop(t, carry):
            u = n - (t - 1)

            def arrived(s):
                ref = part(u, s * 2 + side, plane)
                remote(ref, ref, xs_sem, zr_sem.at[u, s], across).wait_recv()
                along(u, s, ref)
                remote(ref, ref, xs_sem, xr_sem.at[u], across).start()
                to_deck(u, s * 2 + side)
                to_core(u, s * 2 + side)

            @pl.when((u >= 0) & (u < UNITS))
            def _():
                pl.when(row - t >= 0)(lambda: arrived(row - t))
                pl.when(row + t < rows)(lambda: arrived(row + t))

            return carry

        lax.fori_loop(1, rows, hop, 0)
        ux = n - (rows - 1)

        @pl.when((ux >= 0) & (ux < UNITS))
        def _():
            remote(many(rows, 2), many(rows, 2), xs_sem, xr_sem.at[ux], across).wait_recv()

            def pass_on(s, carry):
                to_deck(ux, s * 2 + 1 - side)
                to_core(ux, s * 2 + 1 - side)
                return carry

            lax.fori_loop(0, rows, pass_on, 0)

        uy = n - rows

        @pl.when((uy >= 0) & (uy < UNITS))
        def _():
            remote(many(shards - 1, 1), many(shards - 1, 1), ys_sem, yr_sem.at[uy], other_deck).wait_recv()

            def pass_on(k, carry):
                ref = part(uy, lax.rem(dp + k, shards), theirs)
                remote(ref, ref, cy_sem, cyr_sem.at[uy], sibling).start()
                return carry

            lax.fori_loop(1, shards, pass_on, 0)

    def pass_x():
        x_deck.wait_recv()
        x_forward.start()

    def wait_x():
        x_core.wait_recv()
        x_forward.wait_recv()
        keep_x.wait()

    def wait_vec():
        keep_vec.wait()
        rest = vall.at[pl.ds(0, shards - 1)]
        remote(rest, rest, vec_send, vec_recv, sibling).wait_recv()

    def whole(u):
        remote(many(shards - 1, 2), many(shards - 1, 2), cp_sem, cpr_sem.at[u], sibling).wait_recv()
        remote(many(shards - 1, 1), many(shards - 1, 1), cy_sem, cyr_sem.at[u], sibling).wait_recv()
        keep_copy(u).wait()

    def finish():
        x_deck.wait_send()
        x_core.wait_send()
        x_forward.wait_send()
        rest = vall.at[pl.ds(0, shards - 1)]
        remote(rest, rest, vec_send, vec_recv, sibling).wait_send()
        for count, size, sem in (
            (UNITS * rows, 2, xs_sem),
            (UNITS * (shards - 1), 1, ys_sem),
            (UNITS * (shards - 1), 1, cy_sem),
            (UNITS * (shards - 1), 2, cp_sem),
        ):
            ref = many(count, size)
            remote(ref, ref, sem, xr_sem.at[0], sibling).wait_send()

        def sent(s, carry):
            ref = many(UNITS, 2)

            @pl.when((s <= row) & (row < rows - 1))
            def _():
                remote(ref, ref, zu_sem.at[s], xr_sem.at[0], sibling).wait_send()

            @pl.when((s >= row) & (row > 0))
            def _():
                remote(ref, ref, zd_sem.at[s], xr_sem.at[0], sibling).wait_send()

            return carry

        lax.fori_loop(0, rows, sent, 0)

    return begin, step, whole, pass_x, wait_x, wait_vec, finish


def gather_scratch(shards, rows_of, width, xshape):
    bf16 = jnp.bfloat16
    dma = pltpu.SemaphoreType.DMA
    return [
        pltpu.VMEM((UNITS, rows_of, width), bf16),
        pltpu.VMEM(xshape, bf16),
        dma((UNITS + 1,)),
        dma((UNITS + 2,)),
    ] + [dma((shards // 2,))] * 2 + [dma(())] * 4 + [dma((UNITS, shards // 2))] + [dma((UNITS,))] * 4 + [dma((3,)), dma((3,)), dma(()), dma(())]


GATHER_SCRATCH = 19


def reduce_steps(shards, seqn, rows_of, small, out, scratch):
    f32, bf16 = jnp.float32, jnp.bfloat16
    (acc, got_core, got_deck, got_across, line, got_line, final, got_final, half, got_half,
     got_small, mid_small, got_mid, got_all,
     load_sem, core_send, core_recv, deck_send, deck_recv, across_send, across_recv,
     line_send, line_recv, final_send, final_recv, half_send, half_recv,
     small_send, small_recv) = scratch
    dp, sq, row, side, deck, core = place()
    rows = shards // 2
    across = (row * 2 + 1 - side, sq)
    other_deck = (dp, (1 - deck) * 2 + core)
    sibling = (dp, deck * 2 + 1 - core)
    cut, _ = cutter(rows_of)
    mine = cut(core * 3, 3)
    siblings = cut((1 - core) * 3, 3)
    plane = cut(deck, 2)
    solo = cut(deck * 2, 1)
    other_solo = cut((1 - deck) * 2, 1)
    every = (slice(None), slice(None))

    def total(left, right):
        return (left.astype(f32) + right.astype(f32)).astype(bf16)

    def begin():
        barrier, count = greet_all(dp, sq, shards, seqn)
        pl.semaphore_wait(barrier, count)

    def send_unit(u, tiles):
        def one(s, carry):
            for b in range(2):
                tile = tiles(s * 2 + b)
                remote(
                    tile.at[siblings], got_core.at[u, s, b], core_send.at[u], core_recv.at[u], sibling
                ).start()
                pltpu.make_async_copy(tile.at[mine], acc.at[u, s, b], load_sem.at[u]).start()
            return carry

        lax.fori_loop(0, rows, one, 0)

    def copy_of(kind, u):
        if kind == "core":
            return remote(got_core.at[u], got_core.at[u], core_send.at[u], core_recv.at[u], sibling)
        if kind == "deck":
            src = acc.at[(u,) + every + other_solo]
            return remote(src, got_deck.at[u], deck_send.at[u], deck_recv.at[u], other_deck)
        if kind == "across":
            src = acc.at[(u, slice(None), 1 - side) + plane]
            return remote(src, got_across.at[u], across_send.at[u], across_recv.at[u], across)
        if kind == "line":
            ref = got_line.at[u, pl.ds(0, rows - 1)]
            return remote(ref, ref, line_send.at[u], line_recv.at[u], across)
        if kind == "final":
            return remote(final.at[u], got_final.at[u], final_send.at[u], final_recv.at[u], other_deck)
        return remote(half.at[u], got_half.at[u], half_send.at[u], half_recv.at[u], sibling)

    def stage_core(u):
        pltpu.make_async_copy(acc.at[u], acc.at[u], load_sem.at[u]).wait()
        copy_of("core", u).wait_recv()

        def add(s, carry):
            for b in range(2):
                acc[u, s, b] = total(acc[u, s, b], got_core[u, s, b])
            return carry

        lax.fori_loop(0, rows, add, 0)
        copy_of("deck", u).start()

    def stage_deck(u):
        copy_of("deck", u).wait_recv()

        def add(s, carry):
            for b in range(2):
                at = (u, s, b) + solo
                acc[at] = total(acc[at], got_deck[u, s, b])
            return carry

        lax.fori_loop(0, rows, add, 0)
        copy_of("across", u).start()

    def stage_across(u):
        copy_of("across", u).wait_recv()

        def add(k, carry):
            s = lax.rem(row + k, rows)
            line[u, s] = total(acc[(u, s, side) + plane], got_across[u, s])

            @pl.when(k < rows)
            def _():
                remote(
                    line.at[u, s], got_line.at[u, rows - 1 - k], line_send.at[u], line_recv.at[u], (s * 2 + side, sq)
                ).start()

            return carry

        lax.fori_loop(1, rows + 1, add, 0)

    def stage_line(u):
        copy_of("line", u).wait_recv()
        summed = line[u, row].astype(f32)
        if rows <= 4:
            for k in range(rows - 1):
                summed = summed + got_line[u, k].astype(f32)
        else:
            summed = lax.fori_loop(0, rows - 1, lambda k, t: t + got_line[u, k].astype(f32), summed)
        final[u] = summed.astype(bf16)
        copy_of("final", u).start()

    def stage_final(u):
        copy_of("final", u).wait_recv()
        half[(u,) + plane] = final[u]
        half[(u,) + other_solo] = got_final[(u,) + cut(1 - deck, 1)]
        both = (u,) + cut(1, 1)
        half[both] = total(half[both], got_final[(u,) + cut(deck, 1)])
        copy_of("half", u).start()

    def stage_half(u):
        copy_of("half", u).wait_recv()
        out[(u,) + mine] = half[u].astype(f32)
        out[(u,) + siblings] = got_half[u].astype(f32)

    stages = (stage_core, stage_deck, stage_across, stage_line, stage_final, stage_half)

    def step(n, order):
        for i, stage in enumerate(stages):

            @pl.when((n - i >= 0) & (n - i < UNITS))
            def _(i=i, stage=stage):
                stage(order(n - i))

    def small_first():
        got_small[dp] = small[dp]

        def send(k, carry):
            to = lax.rem(dp + k, shards)
            remote(small.at[to], got_small.at[dp], small_send.at[0], small_recv.at[0], (to, sq)).start()
            return carry

        lax.fori_loop(1, shards, send, 0)

    def sum_of(ref, count):
        summed = ref[0]
        for i in range(1, count):
            summed = summed + ref[i]
        return summed

    def small_second():
        rest = got_small.at[pl.ds(0, shards - 1)]
        remote(rest, rest, small_send.at[0], small_recv.at[0], sibling).wait()
        summed = sum_of(got_small, shards)
        mid_small[0] = summed
        got_mid[sq] = summed

        def send(k, carry):
            to = (dp, lax.rem(sq + k, seqn))
            remote(mid_small.at[0], got_mid.at[sq], small_send.at[1], small_recv.at[1], to).start()
            return carry

        lax.fori_loop(1, seqn, send, 0)

    def small_third():
        rest = got_mid.at[pl.ds(0, seqn - 1)]
        remote(rest, rest, small_send.at[1], small_recv.at[1], sibling).wait()
        summed = sum_of(got_mid, seqn)
        mid_small[1] = summed
        got_all[dp] = summed

        def send(k, carry):
            to = (lax.rem(dp + k, shards), sq)
            remote(mid_small.at[1], got_all.at[dp], small_send.at[2], small_recv.at[2], to).start()
            return carry

        lax.fori_loop(1, shards, send, 0)

    def small_last(small_out):
        rest = got_all.at[pl.ds(0, shards - 1)]
        remote(rest, rest, small_send.at[2], small_recv.at[2], sibling).wait()
        small_out[...] = got_all[...]

    def finish():
        def sent(u, carry):
            for kind in ("core", "deck", "across", "line", "final", "half"):
                copy_of(kind, u).wait_send()
            return carry

        lax.fori_loop(0, UNITS, sent, 0)

    return begin, send_unit, step, (small_first, small_second, small_third, small_last), finish


REDUCE_STAGES = 6
REDUCE_SCRATCH = 29


def reduce_scratch(shards, seqn, rows_of, small_shape):
    f32, bf16 = jnp.float32, jnp.bfloat16
    rows = shards // 2
    _, shape = cutter(rows_of)
    dma = pltpu.SemaphoreType.DMA
    return (
        [
            pltpu.VMEM((UNITS, rows, 2) + shape(3), bf16),
            pltpu.VMEM((UNITS, rows, 2) + shape(3), bf16),
            pltpu.VMEM((UNITS, rows, 2) + shape(1), bf16),
            pltpu.VMEM((UNITS, rows) + shape(2), bf16),
            pltpu.VMEM((UNITS, rows) + shape(2), bf16),
            pltpu.VMEM((UNITS, rows) + shape(2), bf16),
            pltpu.VMEM((UNITS,) + shape(2), bf16),
            pltpu.VMEM((UNITS,) + shape(2), bf16),
            pltpu.VMEM((UNITS,) + shape(3), bf16),
            pltpu.VMEM((UNITS,) + shape(3), bf16),
            pltpu.VMEM(small_shape, f32),
            pltpu.VMEM((2,) + small_shape[1:], f32),
            pltpu.VMEM((seqn,) + small_shape[1:], f32),
            pltpu.VMEM(small_shape, f32),
        ]
        + [dma((UNITS,))] * 13
        + [dma((3,))] * 2
    )


def dx_steps(dxs, scratch):
    f32, bf16 = jnp.float32, jnp.bfloat16
    dx_own, dx_core, dx_deck, load, send, recv = scratch
    dp, sq, row, side, deck, core = place()
    other_deck = (dp, (1 - deck) * 2 + core)
    sibling = (dp, deck * 2 + 1 - core)
    deck_dx = remote(dx_own.at[1 - deck], dx_deck, send.at[2], recv.at[2], other_deck)

    def first():
        for k in range(2):
            pltpu.make_async_copy(dxs.at[k * 2 + core], dx_own.at[k], load.at[k]).start()
            remote(dxs.at[k * 2 + 1 - core], dx_core.at[k], send.at[k], recv.at[k], sibling).start()

    def second():
        for k in range(2):
            pltpu.make_async_copy(dx_own.at[k], dx_own.at[k], load.at[k]).wait()
            remote(dx_core.at[k], dx_core.at[k], send.at[k], recv.at[k], sibling).wait()
            dx_own[k] = (dx_own[k].astype(f32) + dx_core[k].astype(f32)).astype(bf16)
        deck_dx.start()

    def third(dx_out):
        deck_dx.wait()
        dx_out[...] = dx_own[deck].astype(f32) + dx_deck[...].astype(f32)

    return first, second, third


def dx_scratch(own):
    bf16 = jnp.bfloat16
    dma = pltpu.SemaphoreType.DMA
    return [pltpu.VMEM((2,) + own, bf16), pltpu.VMEM((2,) + own, bf16), pltpu.VMEM(own, bf16), dma((2,)), dma((3,)), dma((3,))]


bucket_marks = (12, 16, 23, 32, 46, 64, 91)
MASKED = NB
TN = (((0,), (0,)), ((), ()))
NT = (((1,), (1,)), ((), ()))


def dot(left, right, dims=None):
    if dims is None:
        dims = (((1,), (0,)), ((), ()))
    return lax.dot_general(left, right, dims, preferred_element_type=jnp.float32)


def fill_buckets(buckets, pos_rows, pos_cols, lengths, base, seqs, block, span):
    for s in range(seqs):
        delta = pos_cols[s : s + 1, :] - pos_rows[s]
        dist = jnp.abs(delta)
        far = jnp.full(dist.shape, 8, jnp.int32)
        for mark in bucket_marks:
            far = far + (dist >= mark).astype(jnp.int32)
        bucket = jnp.where(dist < 8, dist, far) + 16 * (delta > 0).astype(jnp.int32)
        i = base + lax.broadcasted_iota(jnp.int32, (block, span), 0)
        j = lax.broadcasted_iota(jnp.int32, (block, span), 1)
        valid = j < lengths[s]
        buckets[s, 0] = jnp.where(valid & (j <= i), bucket, MASKED)
        buckets[s, 1] = jnp.where(valid & (j < jnp.maximum(i, 1)), bucket, MASKED)


def head_lanes(rows, half):
    lane = lax.broadcasted_iota(jnp.int32, (rows, 2 * HD), 1)
    return (lane < HD) if half == 0 else (lane >= HD)


def attend_pair(i, refs, block, span, low_out):
    attended, query, keys, values, buckets, table = refs
    f32, bf16 = jnp.float32, jnp.bfloat16
    pairs = H // 2
    s, pair = i // pairs, lax.rem(i, pairs)
    lanes = pl.ds(pl.multiple_of(pair * 128, 128), 128)
    q = query[:, s, :, lanes].reshape(2 * block, 128)
    k = keys[s, :, lanes]
    v = values[s, :, lanes]
    outs = []
    for half in range(2):
        entry = jnp.broadcast_to(table[pl.ds(pair * 2 + half, 1), :], (block, 128))
        bias = jnp.concatenate(
            [
                jnp.concatenate(
                    [
                        jnp.take_along_axis(entry, buckets[s, t, :, pl.ds(c * 128, 128)], axis=1, mode="promise_in_bounds")
                        for c in range(span // 128)
                    ],
                    axis=1,
                )
                for t in range(2)
            ],
            axis=0,
        )
        mine = head_lanes(2 * block, half)
        one = jnp.where(mine, q * 0.125, 0).astype(bf16)
        scores = dot(one, k, NT) + bias
        top = jnp.max(scores, axis=-1, keepdims=True)
        expo = jnp.exp(scores - top)
        low = (expo * (1.0 / jnp.sum(expo, axis=-1, keepdims=True))).astype(bf16)
        low_out[half] = low
        outs.append(dot(low, v))
    mixed = jnp.where(head_lanes(2 * block, 0), outs[0], outs[1]).astype(bf16)
    attended[:, s, :, lanes] = mixed.reshape(2, block, 128)


EARLY = 8


def forward_kernel(
    shards, seqn, seqs, block, span,
    lengths, wk, wv, wq, wo, wu, wd, xc, xc_rows, xq_rows, table, pos_rows, pos_cols,
    bq, bv, bo, g1, b1, c2, g2, b2, c1,
    full, xall, vall, probs, attended, query, keys, values,
    buckets, w, x_every, v_every, low_two, vec, io_sem, low_sem, *scratch,
):
    f32, bf16 = jnp.float32, jnp.bfloat16
    width = H * HD
    r = vec.shape[1]
    for i, piece in enumerate((bq, bv, bo, g1, b1, c2, g2, b2)):
        vec[i : i + 1, :] = piece[...].astype(f32)
    vec[8:12, :] = c1[...].astype(f32)
    begin, step, whole, pass_x, wait_x, wait_vec, finish = gather_steps(
        shards, seqn, (wk, wv, wq, wo, wu, wd, xc, vec), (full, xall, vall), scratch
    )
    begin()
    fill_buckets(buckets, pos_rows, pos_cols, lengths, lax.axis_index("seq") * block, seqs, block, span)

    def one(n, carry):
        step(n)
        return carry

    lax.fori_loop(0, EARLY - 2, one, 0)
    pass_x()
    lax.fori_loop(EARLY - 2, EARLY, one, 0)
    wait_x()
    wait_vec()
    take_x = pltpu.make_async_copy(xall, x_every, io_sem.at[3])
    take_v = pltpu.make_async_copy(vall, v_every, io_sem.at[4])
    take_x.start()
    take_v.start()

    def take(u):
        return pltpu.make_async_copy(full.at[pl.ds(u * shards, shards)], w.at[u], io_sem.at[u])

    for u in range(3):
        whole(u)
        take(u).start()
    take_v.wait()

    def spread(i, carry):
        row = lax.broadcasted_iota(jnp.int32, (r, width), 0)
        col = lax.broadcasted_iota(jnp.int32, (r, width), 1)
        at = jnp.where(col == row + i * r, 1.0, 0.0).astype(bf16)
        return carry + dot(v_every[i].astype(bf16), at)

    biases = lax.fori_loop(0, shards, spread, jnp.zeros((UNITS, width), f32))
    take_x.wait()

    def matrix(u):
        return w[u].reshape(width, width)

    def project(k, carry):
        rows = x_every[k].reshape(seqs * block, width)
        at = pl.ds(pl.multiple_of(k * block, block), block)
        keys[:, at, :] = dot(rows, matrix(0)).astype(bf16).reshape(seqs, block, width)
        values[:, at, :] = (dot(rows, matrix(1)) + biases[1:2, :]).astype(bf16).reshape(seqs, block, width)
        return carry

    for u in range(3):
        take(u).wait()
    lax.fori_loop(0, seqn, project, 0)
    for t, x in enumerate((xc_rows, xq_rows)):
        rows = x[...].reshape(seqs * block, width)
        query[t] = (dot(rows, matrix(2)) + biases[0:1, :]).astype(bf16).reshape(seqs, block, width)

    total = seqs * H // 2

    def put(i, slot):
        return pltpu.make_async_copy(low_two.at[slot], probs.at[i], low_sem.at[slot])

    def attend_one(i, carry):
        slot = lax.rem(i, 2)

        @pl.when(EARLY + i < UNITS + shards // 2)
        def _():
            step(EARLY + i)

        @pl.when(i >= 2)
        def _():
            put(i - 2, slot).wait()

        attend_pair(i, (attended, query, keys, values, buckets, table), block, span, low_two.at[slot])
        put(i, slot).start()
        return carry

    lax.fori_loop(0, total, attend_one, 0)
    lax.fori_loop(EARLY + total, UNITS + shards // 2, one, 0)
    put(total - 2, lax.rem(total - 2, 2)).wait()
    put(total - 1, lax.rem(total - 1, 2)).wait()

    def last(u, carry):
        whole(u)
        return carry

    lax.fori_loop(3, UNITS, last, 0)
    finish()


def forward(wk, wv, wq, wo, wu, wd, xc, xq, vecs, lengths, table, pos_rows, pos_cols, shards, seqn):
    rows_of, width = wq.shape
    seqs, block, _ = xc.shape
    span = pos_cols.shape[1]
    f32, bf16 = jnp.float32, jnp.bfloat16
    steps = seqs * H // 2
    anywhere = pl.BlockSpec(memory_space=pl.ANY)
    vmem = pl.BlockSpec(memory_space=pltpu.VMEM)
    rows = shards // 2
    dma = pltpu.SemaphoreType.DMA
    return pl.pallas_call(
        functools.partial(forward_kernel, shards, seqn, seqs, block, span),
        out_shape=(
            jax.ShapeDtypeStruct((UNITS * shards, rows_of, width), bf16),
            jax.ShapeDtypeStruct((seqn,) + xc.shape, bf16),
            jax.ShapeDtypeStruct((shards, UNITS, rows_of), f32),
            jax.ShapeDtypeStruct((steps, 2, 2 * block, span), bf16),
            jax.ShapeDtypeStruct((2, seqs, block, width), bf16),
            jax.ShapeDtypeStruct((2, seqs, block, width), bf16),
            jax.ShapeDtypeStruct((seqs, span, width), bf16),
            jax.ShapeDtypeStruct((seqs, span, width), bf16),
        ),
        in_specs=[pl.BlockSpec(memory_space=pltpu.SMEM)] + [anywhere] * 7 + [vmem] * 14,
        out_specs=(anywhere,) * 4 + (vmem,) * 4,
        scratch_shapes=[
            pltpu.VMEM((seqs, 2, block, span), jnp.int32),
            pltpu.VMEM((3, shards, rows_of, width), bf16),
            pltpu.VMEM((seqn,) + xc.shape, bf16),
            pltpu.VMEM((shards, UNITS, rows_of), f32),
            pltpu.VMEM((2, 2, 2 * block, span), bf16),
            pltpu.VMEM((UNITS, rows_of), f32),
            dma((5,)),
            dma((2,)),
        ]
        + gather_scratch(shards, rows_of, width, xc.shape),
        compiler_params=pltpu.CompilerParams(
            collective_id=0, has_side_effects=True, vmem_limit_bytes=60 * 1024 * 1024
        ),
        name="gather_attend",
    )(lengths, wk, wv, wq, wo, wu, wd.reshape(4, rows_of, width), xc, xc, xq, table, pos_rows, pos_cols, *vecs)


def center_of(value):
    center = value - jnp.mean(value, axis=-1, keepdims=True)
    var = jnp.mean(center * center, axis=-1, keepdims=True)
    inv = lax.rsqrt(var + 1e-05)
    return center * inv, inv


def norm_back(grad, gain, normed, inv):
    scaled = grad * gain
    return inv * (
        scaled
        - jnp.mean(scaled, axis=-1, keepdims=True)
        - normed * jnp.mean(scaled * normed, axis=-1, keepdims=True)
    )


def middle_kernel(
    seqs, block,
    attended, xc, xq, cot_c, cot_q, keep, vectors, weights,
    y_c, y_q, dr1_out, da_out, grads, dvec,
    w, hidden, hidden_low, hidden_turn, normed1, inv1, active, slope, feed, dr2, dr2_low, du_low, dr1_low, y, stage,
    w_sem, y_sem, stage_sem, dr1_sem,
):
    f32, bf16 = jnp.float32, jnp.bfloat16
    width = H * HD
    half = seqs * block
    rows = 2 * half
    chunk = 128
    loads = [pltpu.make_async_copy(weights.at[3 + i], w.at[i], w_sem.at[i]) for i in range(9)]
    for load in loads:
        load.start()
    dvec[...] = jnp.zeros_like(dvec)
    vec = lambda i: vectors[i : i + 1, :]

    loads[0].wait()

    def phase_one(c, carry):
        at = pl.ds(pl.multiple_of(c * chunk, chunk), chunk)
        out = dot(attended[at, :], w[0]) + vec(2)

        def from_x(x):
            return x[pl.ds(pl.multiple_of(lax.rem(c, half // chunk) * chunk, chunk), chunk), :].astype(f32)

        x = jnp.where(c < half // chunk, from_x(xc), from_x(xq))
        normed, inv = center_of(x + out)
        normed1[at, :] = normed
        inv1[at, :] = inv
        h = normed * vec(3) + vec(4)
        hidden[at, :] = h
        hidden_low[at, :] = h.astype(bf16)
        return carry

    lax.fori_loop(0, rows // chunk, phase_one, 0)
    hidden_turn[...] = hidden_low[...].T

    tile = 256
    tiles = width // tile
    for j in range(4):
        loads[1 + j].wait()

    def phase_two(step, carry):
        j, n = step // tiles, lax.rem(step, tiles)
        cols = pl.ds(pl.multiple_of(n * tile, tile), tile)
        u = dot(hidden_low[...], w[1 + j, :, cols]) + vectors[pl.ds(8 + j, 1), cols]
        cdf = 0.5 * (1.0 + lax.erf(u * (2.0**-0.5)))
        active[j, :, cols] = (u * cdf).astype(bf16)
        slope[j, :, cols] = cdf + u * (jnp.exp(-0.5 * u * u) * ((2.0 * jnp.pi) ** -0.5))
        return carry

    lax.fori_loop(0, 4 * tiles, phase_two, 0)
    for j in range(4):
        loads[5 + j].wait()

    def phase_feed(n, carry):
        cols = pl.ds(pl.multiple_of(n * tile, tile), tile)
        feed[:, cols] = sum(dot(active[j], w[5 + j, :, cols]) for j in range(4))
        return carry

    lax.fori_loop(0, tiles, phase_feed, 0)

    def phase_three(c, carry):
        at = pl.ds(pl.multiple_of(c * chunk, chunk), chunk)
        normed, inv = center_of(hidden[at, :] + feed[at, :] + vec(5))
        kept = keep[at, :]
        y[at, :] = (normed * vec(6) + vec(7)) * kept
        inner = pl.ds(pl.multiple_of(lax.rem(c, half // chunk) * chunk, chunk), chunk)
        cot = jnp.where(c < half // chunk, cot_c[inner, :].astype(f32), cot_q[inner, :].astype(f32)) * kept
        d = norm_back(cot, vec(6), normed, inv)
        dvec[6:7, :] += jnp.sum(cot * normed, axis=0, keepdims=True)
        dvec[7:8, :] += jnp.sum(cot, axis=0, keepdims=True)
        dvec[5:6, :] += jnp.sum(d, axis=0, keepdims=True)
        dr2[at, :] = d
        dr2_low[at, :] = d.astype(bf16)
        return carry

    lax.fori_loop(0, rows // chunk, phase_three, 0)
    y_copies = [
        pltpu.make_async_copy(y.at[pl.ds(0, half)], y_c, y_sem.at[0]),
        pltpu.make_async_copy(y.at[pl.ds(half, half)], y_q, y_sem.at[1]),
    ]
    for copy in y_copies:
        copy.start()

    def phase_four(step, carry):
        j, n = step // tiles, lax.rem(step, tiles)
        cols = pl.ds(pl.multiple_of(n * tile, tile), tile)
        du = slope[j, :, cols] * dot(dr2_low[...], w[5 + j, cols, :], NT)
        dvec[pl.ds(8 + j, 1), cols] = jnp.sum(du, axis=0, keepdims=True)
        low = du.astype(bf16)
        du_low[j, :, cols] = low
        stage[j, :, cols] = dot(hidden_turn[...], low).astype(bf16)
        stage[4 + j, cols, :] = dot(active[j, :, cols], dr2_low[...], TN).astype(bf16)

        @pl.when(n == tiles - 1)
        def _():
            pltpu.make_async_copy(stage.at[j], grads.at[4 + j], stage_sem.at[j]).start()
            pltpu.make_async_copy(stage.at[4 + j], grads.at[8 + j], stage_sem.at[4 + j]).start()

        return carry

    lax.fori_loop(0, 4 * tiles, phase_four, 0)

    def phase_hidden(n, carry):
        cols = pl.ds(pl.multiple_of(n * tile, tile), tile)
        dr2[:, cols] += sum(dot(du_low[j], w[1 + j, cols, :], NT) for j in range(4))
        return carry

    lax.fori_loop(0, tiles, phase_hidden, 0)
    for copy in y_copies:
        copy.wait()

    def phase_five(c, carry):
        at = pl.ds(pl.multiple_of(c * chunk, chunk), chunk)
        dh = dr2[at, :]
        normed = normed1[at, :]
        d = norm_back(dh, vec(3), normed, inv1[at, :])
        dvec[3:4, :] += jnp.sum(dh * normed, axis=0, keepdims=True)
        dvec[4:5, :] += jnp.sum(dh, axis=0, keepdims=True)
        dvec[2:3, :] += jnp.sum(d, axis=0, keepdims=True)
        y[at, :] = d
        low = d.astype(bf16)
        dr1_low[at, :] = low
        da_out[at, :] = dot(low, w[0], NT).astype(bf16)
        return carry

    lax.fori_loop(0, rows // chunk, phase_five, 0)
    dr1_copy = pltpu.make_async_copy(y, dr1_out, dr1_sem)
    dr1_copy.start()

    def phase_out(n, carry):
        cols = pl.ds(pl.multiple_of(n * tile, tile), tile)
        stage[8, cols, :] = dot(attended[:, cols], dr1_low[...], TN).astype(bf16)
        return carry

    lax.fori_loop(0, tiles, phase_out, 0)
    last = pltpu.make_async_copy(stage.at[8], grads.at[3], stage_sem.at[8])
    last.start()
    for j in range(8):
        pltpu.make_async_copy(stage.at[j], grads.at[4 + j], stage_sem.at[j]).wait()
    last.wait()
    dr1_copy.wait()


def middle(attended, xc, xq, cot_c, cot_q, keep, vectors, weights):
    seqs, block, width = xc.shape
    f32, bf16 = jnp.float32, jnp.bfloat16
    half = seqs * block
    rows = 2 * half
    vmem = pl.BlockSpec(memory_space=pltpu.VMEM)
    anywhere = pl.BlockSpec(memory_space=pl.ANY)
    flat = lambda a: a.reshape(half, width)
    return pl.pallas_call(
        functools.partial(middle_kernel, seqs, block),
        out_shape=(
            jax.ShapeDtypeStruct((half, width), f32),
            jax.ShapeDtypeStruct((half, width), f32),
            jax.ShapeDtypeStruct((rows, width), f32),
            jax.ShapeDtypeStruct((rows, width), bf16),
            jax.ShapeDtypeStruct((UNITS, width, width), bf16),
            jax.ShapeDtypeStruct((UNITS, width), f32),
        ),
        in_specs=[vmem] * 7 + [anywhere],
        out_specs=(anywhere, anywhere, anywhere, vmem, anywhere, vmem),
        scratch_shapes=[
            pltpu.VMEM((9, width, width), bf16),
            pltpu.VMEM((rows, width), f32),
            pltpu.VMEM((rows, width), bf16),
            pltpu.VMEM((width, rows), bf16),
            pltpu.VMEM((rows, width), f32),
            pltpu.VMEM((rows, 1), f32),
            pltpu.VMEM((4, rows, width), bf16),
            pltpu.VMEM((4, rows, width), f32),
            pltpu.VMEM((rows, width), f32),
            pltpu.VMEM((rows, width), f32),
            pltpu.VMEM((rows, width), bf16),
            pltpu.VMEM((4, rows, width), bf16),
            pltpu.VMEM((rows, width), bf16),
            pltpu.VMEM((rows, width), f32),
            pltpu.VMEM((9, width, width), bf16),
            pltpu.SemaphoreType.DMA((9,)),
            pltpu.SemaphoreType.DMA((2,)),
            pltpu.SemaphoreType.DMA((9,)),
            pltpu.SemaphoreType.DMA(()),
        ],
        compiler_params=pltpu.CompilerParams(vmem_limit_bytes=63 * 1024 * 1024),
        name="middle",
    )(attended, flat(xc), flat(xq), flat(cot_c), flat(cot_q), keep, vectors, weights)


def attend_back_pair(i, refs, low, seqs, block, span):
    attended, d_attended, query, keys, values, buckets, dq, dk, dv, ds_sum, sums, counts = refs
    f32, bf16 = jnp.float32, jnp.bfloat16
    pairs = H // 2
    rows = 2 * block
    s, pair = i // pairs, lax.rem(i, pairs)
    lanes = pl.ds(pl.multiple_of(pair * 128, 128), 128)
    q = query[:, s, :, lanes].reshape(rows, 128)
    k = keys[s, :, lanes]
    v = values[s, :, lanes]
    da = d_attended[:, s, :, lanes].reshape(rows, 128)
    product = da.astype(f32) * attended[:, s, :, lanes].reshape(rows, 128).astype(f32)
    d_queries, dk_turn, dv_turn = [], 0.0, 0.0
    for half in range(2):
        mine = head_lanes(rows, half)
        one = jnp.where(mine, da, 0).astype(bf16)
        inner = jnp.sum(jnp.where(mine, product, 0.0), axis=-1, keepdims=True)
        ds = low[half].astype(f32) * (dot(one, v, NT) - inner)
        ds_sum[pair * 2 + half] = (ds[:block] + ds[block:]).astype(bf16)
        ds_low = ds.astype(bf16)
        d_queries.append(dot(ds_low, k))
        dk_turn += dot(jnp.where(mine, q, 0).astype(bf16), ds_low, TN)
        dv_turn += dot(one, low[half], TN)
    d_query = jnp.where(head_lanes(rows, 0), d_queries[0], d_queries[1]) * 0.125
    sums[0:1, lanes] += jnp.sum(d_query, axis=0, keepdims=True)
    dq[:, s, :, lanes] = d_query.reshape(2, block, 128).astype(bf16)
    dk[s, :, lanes] = (dk_turn * 0.125).T.astype(bf16)
    d_value = dv_turn.T
    sums[1:2, lanes] += jnp.sum(d_value, axis=0, keepdims=True)
    dv[s, :, lanes] = d_value.astype(bf16)

    @pl.when(pair == pairs - 1)
    def _():
        def count(g, carry):
            at = pl.ds(pl.multiple_of(g * 16, 16), 16)
            bucket = buckets[s, 0, at, :]
            hot = jnp.concatenate([jnp.where(bucket == n, 1.0, 0.0).astype(bf16) for n in range(NB)], axis=0)
            counts[...] += dot(hot, ds_sum[:, at, :].reshape(H * 16, span), NT)
            return carry

        lax.fori_loop(0, block // 16, count, 0)


def table_of(counts):
    row = lax.broadcasted_iota(jnp.int32, counts.shape, 0)
    col = lax.broadcasted_iota(jnp.int32, counts.shape, 1)
    kept = jnp.where(lax.rem(row, 16) == lax.rem(col, 16), counts, 0.0)
    folded = jnp.sum(kept.reshape(NB, 16, H * 16), axis=1)
    lane = lax.broadcasted_iota(jnp.int32, (H * 16, 128), 1)
    head = lax.broadcasted_iota(jnp.int32, (H * 16, 128), 0) // 16
    return jnp.dot(folded, jnp.where(lane == head, 1.0, 0.0), precision=lax.Precision.HIGHEST)


READY = 9


def backward_kernel(
    shards, seqn, seqs, block, span, rows_of,
    lengths, grads, full, xall, probs, attended_in, da_in, query_in, keys_in, values_in, dr1_in,
    xc, xq, dvec, pos_rows, pos_cols,
    out, dx_out, d_content, d_query_x, small_out,
    dq, dk, dv, late, w, x_every, dxs, sums, counts, small, io_sem, low_sem, *scratch,
):
    f32, bf16 = jnp.float32, jnp.bfloat16
    width = H * HD
    half = seqs * block
    total = seqs * H // 2
    begin, send_unit, step, (small_first, small_second, small_third, small_last), finish = reduce_steps(
        shards, seqn, rows_of, small, out, scratch[:REDUCE_SCRATCH]
    )
    dx_first, dx_second, dx_third = dx_steps(dxs, scratch[REDUCE_SCRATCH:])
    order = lambda k: UNITS - 1 - k
    weights = [pltpu.make_async_copy(full.at[pl.ds(u * shards, shards)], w.at[u], io_sem.at[5 + u]) for u in range(3)]
    slots = [
        pltpu.make_async_copy(xall.at[k], x_every.at[:, pl.ds(k * block, block)], io_sem.at[8 + k]) for k in range(seqn)
    ]

    def one(n, carry):
        step(n, order)
        return carry

    def attention(attended, d_attended, query, keys, values, buckets, low_two, ds_sum):
        loads = [
            pltpu.make_async_copy(src, dst, io_sem.at[i])
            for i, (src, dst) in enumerate(
                ((attended_in, attended), (da_in, d_attended), (query_in, query), (keys_in, keys), (values_in, values))
            )
        ]

        def take(i, slot):
            return pltpu.make_async_copy(probs.at[i], low_two.at[slot], low_sem.at[slot])

        for load in loads:
            load.start()
        take(0, 0).start()
        for load in weights + slots:
            load.start()
        begin()

        def send(k, carry):
            u = order(k)
            send_unit(u, lambda shard: grads.at[tile_of(u, shard, shards)])
            return carry

        lax.fori_loop(0, READY, send, 0)
        fill_buckets(buckets, pos_rows, pos_cols, lengths, lax.axis_index("seq") * block, seqs, block, span)
        counts[...] = jnp.zeros_like(counts)
        sums[...] = jnp.zeros_like(sums)
        for load in loads:
            load.wait()
        refs = (attended, d_attended, query, keys, values, buckets, dq, dk, dv, ds_sum, sums, counts)

        def pair(i, carry):
            slot = lax.rem(i, 2)

            @pl.when(lax.rem(i, 2) == 0)
            def _():
                step(i // 2, order)

            take(i, slot).wait()

            @pl.when(i + 1 < total)
            def _():
                take(i + 1, 1 - slot).start()

            attend_back_pair(i, refs, low_two.at[slot], seqs, block, span)
            return carry

        lax.fori_loop(0, total, pair, 0)

    pl.run_scoped(
        attention,
        pltpu.VMEM((2, seqs, block, width), bf16),
        pltpu.VMEM((2, seqs, block, width), bf16),
        pltpu.VMEM((2, seqs, block, width), bf16),
        pltpu.VMEM((seqs, span, width), bf16),
        pltpu.VMEM((seqs, span, width), bf16),
        pltpu.VMEM((seqs, 2, block, span), jnp.int32),
        pltpu.VMEM((2, 2, 2 * block, span), bf16),
        pltpu.VMEM((H, block, span), bf16),
    )

    tile = 256

    def send_late(u):
        send_unit(u, lambda shard: late.at[u, shard])

    def weight_grads(dr1, turned, x_two):
        load = pltpu.make_async_copy(dr1_in, dr1, io_sem.at[0])
        load.start()
        loads = [pltpu.make_async_copy(x, x_two.at[t], io_sem.at[1 + t]) for t, x in enumerate((xc, xq))]
        for copy in loads:
            copy.start()
        for copy in weights + slots:
            copy.wait()
        matrix = lambda u: w[u].reshape(width, width)
        turned[...] = x_every[...].reshape(seqs * span, width).T

        def late_from(u, ref):
            def tiles(n, carry):
                cols = pl.ds(pl.multiple_of(n * tile, tile), tile)
                grad = dot(turned[...], ref[:, :, cols].reshape(seqs * span, tile))
                late[u, :, :, cols] = grad.astype(bf16).reshape(shards, rows_of, tile)
                return carry

            lax.fori_loop(0, width // tile, tiles, 0)
            send_late(u)

        late_from(0, dk)
        step(6, order)
        late_from(1, dv)

        def every(n, carry):
            s, k = n // seqn, lax.rem(n, seqn)
            at = pl.ds(pl.multiple_of(k * block, block), block)
            part = dot(dk[s, at, :], matrix(0), NT) + dot(dv[s, at, :], matrix(1), NT)
            dxs[k, pl.ds(pl.multiple_of(s * block, block), block), :] = part.astype(bf16)
            return carry

        lax.fori_loop(0, seqs * seqn, every, 0)
        dx_first()
        step(7, order)
        for copy in loads:
            copy.wait()

        def tiles(n, carry):
            cols = pl.ds(pl.multiple_of(n * tile, tile), tile)
            grad = sum(
                dot(x_two[t].reshape(half, width), dq[t, :, :, cols].reshape(half, tile), TN) for t in range(2)
            )
            late[2, :, :, cols] = grad.astype(bf16).reshape(shards, rows_of, tile)
            return carry

        lax.fori_loop(0, width // tile, tiles, 0)
        send_late(2)
        load.wait()
        for t, d_x in enumerate((d_content, d_query_x)):
            d_x[...] = dr1[pl.ds(t * half, half), :] + dot(dq[t].reshape(half, width), matrix(2), NT)

    pl.run_scoped(
        weight_grads,
        pltpu.VMEM((2 * half, width), f32),
        pltpu.VMEM((width, seqs * span), bf16),
        pltpu.VMEM((2, seqs, block, width), bf16),
    )
    step(8, order)
    table = table_of(counts[...])
    vectors = jnp.concatenate([sums[0:2, :], dvec[2:, :], jnp.zeros((4, width), f32)], axis=0)
    pieces = [vectors[:, c * 128 : (c + 1) * 128] for c in range(width // 128)] + [table[:16], table[16:]]
    each = shards // 8
    size = 16 // each
    for p, piece in enumerate(pieces):
        for k in range(each):
            small[p * each + k] = piece[k * size : (k + 1) * size]
    small_first()
    dx_second()
    step(9, order)
    small_second()
    step(10, order)
    small_third()
    lax.fori_loop(11, UNITS + REDUCE_STAGES - 1, one, 0)
    dx_third(dx_out)
    small_last(small_out)
    finish()


def backward(lengths, grads, full, xall, probs, attended, d_attended, query, keys, values, dr1, xc, xq, dvec, pos_rows, pos_cols, shards, seqn):
    rows_of, width = full.shape[1:]
    seqs, block, _ = xc.shape
    span = pos_cols.shape[1]
    f32, bf16 = jnp.float32, jnp.bfloat16
    anywhere = pl.BlockSpec(memory_space=pl.ANY)
    vmem = pl.BlockSpec(memory_space=pltpu.VMEM)
    own = (seqs * block, width)
    small_shape = (shards, 128 // shards, 128)
    dma = pltpu.SemaphoreType.DMA
    return pl.pallas_call(
        functools.partial(backward_kernel, shards, seqn, seqs, block, span, rows_of),
        out_shape=(
            jax.ShapeDtypeStruct((UNITS, rows_of, width), f32),
            jax.ShapeDtypeStruct(own, f32),
            jax.ShapeDtypeStruct(own, f32),
            jax.ShapeDtypeStruct(own, f32),
            jax.ShapeDtypeStruct(small_shape, f32),
        ),
        in_specs=[pl.BlockSpec(memory_space=pltpu.SMEM)] + [anywhere] * 12 + [vmem] * 3,
        out_specs=(vmem,) * 5,
        scratch_shapes=[
            pltpu.VMEM((2, seqs, block, width), bf16),
            pltpu.VMEM((seqs, span, width), bf16),
            pltpu.VMEM((seqs, span, width), bf16),
            pltpu.VMEM((3, shards, rows_of, width), bf16),
            pltpu.VMEM((3, shards, rows_of, width), bf16),
            pltpu.VMEM((seqs, span, width), bf16),
            pltpu.VMEM((seqn,) + own, bf16),
            pltpu.VMEM((8, width), f32),
            pltpu.VMEM((NB * 16, H * 16), f32),
            pltpu.VMEM(small_shape, f32),
            dma((8 + seqn,)),
            dma((2,)),
        ]
        + reduce_scratch(shards, seqn, rows_of, small_shape)
        + dx_scratch(own),
        compiler_params=pltpu.CompilerParams(
            collective_id=1, has_side_effects=True, vmem_limit_bytes=67043328
        ),
        name="attend_back_reduce",
    )(lengths, grads, full, xall, probs, attended, d_attended, query, keys, values, dr1, xc, xq, dvec, pos_rows, pos_cols)


def per_device(
    x_content, x_query, cot_content, cot_query,
    w_query, b_query, w_key, w_value, b_value, w_out, b_out, gain_attn, shift_attn,
    w_up, b_up, w_down, b_down, gain_ffn, shift_ffn, rel_table, lengths, positions, predicted,
    *, shards, seqn,
):
    f32 = jnp.float32
    seqs, block, width = x_content.shape
    r = w_query.shape[0]
    vecs = [
        v.reshape(1, r) for v in (b_query, b_value, b_out, gain_attn, shift_attn, b_down, gain_ffn, shift_ffn)
    ] + [b_up.reshape(4, r)]
    base = lax.axis_index("seq") * block
    pos_rows = lax.dynamic_slice_in_dim(positions, base, block, 1)[..., None]
    table = jnp.full((H, 128), -1e30, f32).at[:, :NB].set(rel_table.astype(f32).T)
    valid = (base + jnp.arange(block))[None, :] < lengths[:, None]
    keep = jnp.stack([valid, valid & (predicted > 0)]).astype(f32).reshape(2 * seqs * block, 1)

    full, xall, vall, probs, attended, query, keys, values = forward(
        w_key, w_value, w_query, w_out, w_up, w_down, x_content, x_query, vecs,
        lengths, table, pos_rows, positions, shards, seqn,
    )
    weights = full.reshape(UNITS, width, width)
    vectors = jnp.concatenate(
        [jnp.transpose(vall[:, :8], (1, 0, 2)).reshape(8, width), vall[:, 8:].reshape(4, width)]
    )
    y_c, y_q, dr1, d_attended, grads, dvec = middle(
        attended.reshape(2 * seqs * block, width), x_content, x_query, cot_content, cot_query, keep, vectors, weights
    )
    sums, dx, d_content, d_query_x, small = backward(
        lengths, grads.reshape(UNITS * shards, r, width), full, xall, probs, attended,
        d_attended.reshape(attended.shape), query, keys, values, dr1, x_content, x_query, dvec,
        pos_rows, positions, shards, seqn,
    )
    small = small.reshape(8, 16, 128)
    summed = jnp.transpose(small[:6, :12], (1, 0, 2)).reshape(UNITS, width)
    mine = lax.axis_index("dp")
    tiny = lax.dynamic_slice_in_dim(summed[:8], mine * r, r, 1)
    g_c1 = lax.dynamic_slice_in_dim(summed[8:].reshape(4 * width), mine * 4 * r, 4 * r, 0)
    g_table = small[6:].reshape(NB, 128)[:, :H]
    shape = (seqs, block, width)
    grad_content = (d_content + dx).reshape(shape)
    g_bq, g_bv, g_bo, g_g1, g_b1, g_c2, g_g2, g_b2 = (tiny[i] for i in range(8))
    g_w1 = jnp.transpose(sums[4:8], (1, 0, 2)).reshape(r, 4 * width)
    g_w2 = sums[8:12].reshape(4 * r, width)
    return (
        y_c.reshape(shape), y_q.reshape(shape), grad_content, d_query_x.reshape(shape),
        sums[2], g_bq, sums[0], sums[1], g_bv, sums[3], g_bo, g_g1, g_b1,
        g_w1, g_c1, g_w2, g_c2, g_g2, g_b2, g_table,
    )


def solution(mesh):
    in_specs = (
        P("dp", "seq", None),
        P("dp", "seq", None),
        P("dp", "seq", None),
        P("dp", "seq", None),
        P("dp", None),
        P("dp"),
        P("dp", None),
        P("dp", None),
        P("dp"),
        P("dp", None),
        P("dp"),
        P("dp"),
        P("dp"),
        P("dp", None),
        P("dp"),
        P("dp", None),
        P("dp"),
        P("dp"),
        P("dp"),
        P(),
        P("dp"),
        P("dp", None),
        P("dp", "seq"),
    )
    out_specs = (
        P("dp", "seq", None),
        P("dp", "seq", None),
        P("dp", "seq", None),
        P("dp", "seq", None),
        P("dp", None),
        P("dp"),
        P("dp", None),
        P("dp", None),
        P("dp"),
        P("dp", None),
        P("dp"),
        P("dp"),
        P("dp"),
        P("dp", None),
        P("dp"),
        P("dp", None),
        P("dp"),
        P("dp"),
        P("dp"),
        P(),
    )
    return jax.shard_map(
        functools.partial(per_device, shards=mesh.shape["dp"], seqn=mesh.shape["seq"]),
        mesh=mesh, in_specs=in_specs, out_specs=out_specs, check_vma=False
    )
```

time: 1210 us -> 259 us (0.21)
  waiting for transfers between devices: 709 us -> 0 us
  Pallas kernels: 0 us -> 236 us
  matrix products: 136 us -> 0 us
  local copies, waits for them, and re-layouts: 151 us -> 16.8 us
  blocking collectives: 131 us -> 0 us
  other arithmetic: 52.6 us -> 5.25 us
  between operations: 17.3 us -> 0.74 us
    reduce_scatter x4 -> x0, waiting for transfers between devices: 389 us -> none  [the longest x1 165 us: per_device(): lax.psum_scatter(d_w1, 'dp', scatter_dimension=0, tiled=True)]
    pallas_call x0 -> x3, Pallas kernels: none -> 236 us  [the longest x1 113 us: backward(): pl.pallas_call(functools.partial(backward_kernel, shards, seqn, seqs, blo...]
    unnamed x21 -> x0, waiting for transfers between devices: 168 us -> none
    all_gather x8 -> x0, waiting for transfers between devices: 152 us -> none  [the longest x1 54.7 us: per_device(): lax.all_gather(w_down, 'dp', axis=0, tiled=True)]
    dot_general x25 -> x0, matrix products: 117 us -> none  [the longest x1 13.1 us: per_device(): jnp.einsum('shqk,sqkn->nh', jnp.sum(d_scores, axis=0), onehot, precision=...]
    eq x1 -> x0, local copies, waits for them, and re-layouts: 74.6 us -> none  [per_device(): bucket_ids(pos_q, positions)[..., None] == jnp.arange(NB)]
    unnamed x2 -> x0, blocking collectives: 57.2 us -> none
    psum x2 -> x0, blocking collectives: 52.3 us -> none  [the longest x1 39.4 us: per_device(): table_total = lax.psum(d_table, ('dp', 'seq'))]
  transfers between devices with their start and end apart: 17 -> 0, of which waited for: 11 -> 0; matrix products, arithmetic and copies ran while one was open for 21% -> 0% of each run, Pallas kernels for 0% -> 0%
where the time goes in v3:
time: 259 us; the launch traced here: 258 us
  Pallas kernels  236 us (91%)
  local copies, waits for them, and re-layouts  16.8 us (6%)
  other arithmetic  5.25 us (2%)
    pallas_call x1, Pallas kernels, backward(): pl.pallas_call(functools.partial(backward_kernel, shards, seqn, seqs, blo...  113 us
    pallas_call x1, Pallas kernels, forward(): pl.pallas_call(functools.partial(forward_kernel, shards, seqn, seqs, bloc...  82.4 us
    pallas_call x1, Pallas kernels, middle(): pl.pallas_call(functools.partial(middle_kernel, seqs, block), out_shape=(...  40.5 us

profile of v3, /device:TPU:1, one launch (start us, length us, event | category | flops | bytes accessed | tf_op | source)
XLA Modules:
  0.0 258.4 jit_solution(17215850202564441600)
XLA Ops:
  0.7 0.6 compare_reduce_fusion
  1.3 1.3 select_bitcast_fusion
  2.6 0.6 scatter.4.table
  3.2 0.7 dynamic-slice_bitcast_fusion
  3.9 0.8 copy.45.pos_rows
  4.7 0.0 copy-start.4
  4.7 0.0 copy-start.5
  4.7 1.4 reshape.222.c1
  6.1 82.4 %gather_attend.1 = (bf16[96,96,768]{2,1,0:T(8,128)(2,1)}, bf16[4,2,128,768]{3,2,1,0:T(8,128)(2,1)}, f32[8,12,96]{2,1,0:T(8,128)}, bf16[12,2,256,512]{3,2,1,0:T(8...) custom-call(s32[2]{0:T(128)} %lengths.3, ...), custom_call_target="tpu_custom_call" | custom-call | tf_op jit(solution)/shard_map/gather_attend/pallas_call | solution.py:720
  88.5 0.0 copy-done.4
  88.5 0.0 copy-done.5
  88.5 0.1 and_bitcast_fusion
  88.5 0.1 broadcast_compare_fusion
  88.6 0.9 copy.47.keep
  89.5 0.8 slice.84
  90.3 0.1 reshape.229
  90.3 0.8 slice_bitcast_fusion.6
  91.1 0.1 reshape.228
  91.2 0.6 pad_maximum_fusion.vectors
  91.8 40.5 %middle.1 = (f32[256,768]{1,0:T(8,128)}, f32[256,768]{1,0:T(8,128)}, f32[512,768]{1,0:T(8,128)}, bf16[512,768]{1,0:T(8,128)(2,1)}, bf16[12,768,768]{2,1,0:T(8,128)(2,1)}, /*index=5*/f32[12,768]{1,0:T(8,128)}) custom-call(bf16[512,768]{1,0:T(8,128)(2,1)} %bitcast.69, bf16[256,768]{1,0:T(8,128)(2,1)} %bitcast.67, bf16[256,768]{1,0:T(8,128)(2,1)} %bitcast.68, ...), custom_call_target="tpu_custom_call" | custom-call | tf_op jit(solution)/shard_map/middle/pallas_call | solution.py:923
  132.4 112.7 %attend_back_reduce.1 = (f32[12,96,768]{2,1,0:T(8,128)}, f32[256,768]{1,0:T(8,128)}, f32[256,768]{1,0:T(8,128)}, f32[256,768]{1,0:T(8,128)}, f32[8,16,128]{2,1,0:T(8,128)}) custom-call(s32[2]{0:T(128)} %lengths.3, bf16[96,96,768]{2,1,0:T(8,128)(2,1)} %bitcast.66, bf16[96,96,768]{2,1,0:T(8,128)(2,1)} %get-tuple-element.53.full, ...), custom_call_target="tpu_custom_call" | custom-call | tf_op jit(solution)/shard_map/attend_back_reduce/pallas_call | solution.py:1197
  245.1 0.0 copy-start
  245.1 2.5 add.29
  247.5 0.0 copy-start.3
  247.6 2.3 slice_bitcast_fusion.1
  249.8 0.0 copy-done.3
  249.8 0.0 copy-start.2
  249.9 0.6 copy-done.2
  250.5 0.6 slice_bitcast_fusion.7
  251.1 0.8 constant_dynamic-slice_fusion
  251.8 0.5 slice_bitcast_fusion.8
  252.4 0.0 copy-done
  252.4 1.2 fusion
  253.6 0.0 copy-start.1
  253.6 1.1 copy.53
  254.7 0.7 slice.106
  255.4 0.7 dynamic_slice.11
  256.1 0.7 slice.103
  256.8 0.7 copy.52
  257.5 0.0 copy-done.1
  257.5 0.9 copy.55
  (6 shorter events, 0.0 us)
Async XLA Ops:
  4.7 83.7 %copy-start.4 = (s32[2]{0:T(128)S(1)}, s32[2]{0:T(128)}, u32[]{:S(2)}) copy-start(s32[2]{0:T(128)} %lengths.3) | copy-start | bytes 28
  4.7 83.7 %copy-start.5 = (s32[2,128]{1,0:T(2,128)S(1)}, s32[2,128]{1,0:T(2,128)}, u32[]{:S(2)}) copy-start(s32[2,128]{1,0:T(2,128)} %param.47) | copy-start | bytes 3076
  245.1 7.3 %copy-start = (f32[12,96,768]{2,1,0:T(8,128)S(1)}, f32[12,96,768]{2,1,0:T(8,128)}, u32[]{:S(2)}) copy-start(f32[12,96,768]{2,1,0:T(8,128)} %get-tuple-element.68) | copy-start | bytes 10616836
  247.5 2.3 copy-start.3
  249.8 0.6 copy-start.2
  253.6 3.9 %copy-start.1 = (f32[256,768]{1,0:T(8,128)S(1)}, f32[256,768]{1,0:T(8,128)}, u32[]{:S(2)}) copy-start(f32[256,768]{1,0:T(8,128)} %get-tuple-element.67) | copy-start | bytes 2359300

commit v4 on v3

v4 whole, which is shorter than its diff:
```python
import functools

import jax
import jax.numpy as jnp
from jax import lax
from jax.experimental import pallas as pl
from jax.experimental.pallas import tpu as pltpu
from jax.sharding import PartitionSpec as P

H = 12
HD = 64
NB = 32

MESH = pl.DeviceIdType.MESH
UNITS = 12


def cutter(rows_of):
    by_rows = rows_of % 96 == 0
    piece = rows_of // 6 if by_rows else 128

    def cut(start, size):
        if not isinstance(start, int):
            start = pl.multiple_of(start * piece, 16 if by_rows else 128)
        else:
            start = start * piece
        inner = pl.ds(start, size * piece)
        return (inner, slice(None)) if by_rows else (slice(None), inner)

    def shape(size):
        return (size * piece, 768) if by_rows else (rows_of, size * piece)

    return cut, shape


def place():
    dp, sq = lax.axis_index("dp"), lax.axis_index("seq")
    row, side = dp // 2, dp % 2
    deck, core = sq // 2, sq % 2
    return dp, sq, row, side, deck, core


def tile_of(unit, shard, shards):
    down = unit // 8
    return (1 - down) * (unit * shards + shard) + down * (8 * shards + shard * 4 + unit - 8)


def remote(src, dst, send, recv, device):
    return pltpu.make_async_remote_copy(
        src_ref=src, dst_ref=dst, send_sem=send, recv_sem=recv, device_id=device, device_id_type=MESH
    )


def greet_all(dp, sq, shards, seqn):
    barrier = pltpu.get_barrier_semaphore()

    def greet(step, carry):
        pl.semaphore_signal(barrier, inc=1, device_id=(lax.rem(dp + step, shards), sq), device_id_type=MESH)
        return carry

    def greet_seq(step, carry):
        pl.semaphore_signal(barrier, inc=1, device_id=(dp, lax.rem(sq + step, seqn)), device_id_type=MESH)
        return carry

    lax.fori_loop(1, shards, greet, 0)
    lax.fori_loop(1, seqn, greet_seq, 0)
    return barrier, shards + seqn - 2


AHEAD = 2


def gather_steps(shards, seqn, ins, outs, scratch):
    wk, wv, wq, wo, wu, wd, xc = ins
    full, xall, vall = outs
    (load_sem, zu_sem, zd_sem, xs_sem, ys_sem, cp_sem, cy_sem,
     zr_sem, xr_sem, yr_sem, cpr_sem, cyr_sem, xc_send, xc_recv, vec_send, vec_recv) = scratch
    dp, sq, row, side, deck, core = place()
    rows = shards // 2
    across = (row * 2 + 1 - side, sq)
    other_deck = (dp, (1 - deck) * 2 + core)
    sibling = (dp, deck * 2 + 1 - core)
    cut, _ = cutter(full.shape[1])
    plane = cut(core * 3 + deck, 2)
    solo = cut(core * 3 + deck * 2, 1)
    theirs = cut(core * 3 + (1 - deck) * 2, 1)

    def many(count, size):
        return full.at[(pl.ds(0, count),) + cut(0, size)]

    def part(unit, shard, piece):
        return full.at[(tile_of(unit, shard, shards),) + piece]

    pieces = [wk, wv, wq, wo] + [wu.at[:, pl.ds(j * 768, 768)] for j in range(4)] + [wd.at[j] for j in range(4)]
    loads = [
        pltpu.make_async_copy(piece, full.at[tile_of(u, dp, shards)], load_sem.at[u]) for u, piece in enumerate(pieces)
    ]
    x_mine = xall.at[sq]
    xload = pltpu.make_async_copy(xc, x_mine, load_sem.at[UNITS])
    x_deck = remote(x_mine, x_mine, xc_send.at[0], xc_recv.at[0], other_deck)
    x_core = remote(x_mine, x_mine, xc_send.at[1], xc_recv.at[1], sibling)
    x_theirs = xall.at[(1 - deck) * 2 + core]
    x_forward = remote(x_theirs, x_theirs, xc_send.at[2], xc_recv.at[2], sibling)

    up = ((row + 1) * 2 + side, sq)
    down = ((row - 1) * 2 + side, sq)

    def along(u, s, src):
        dst = part(u, s * 2 + side, plane)

        @pl.when((s <= row) & (row < rows - 1))
        def _():
            remote(src, dst, zu_sem.at[s], zr_sem.at[u, s], up).start()

        @pl.when((s >= row) & (row > 0))
        def _():
            remote(src, dst, zd_sem.at[s], zr_sem.at[u, s], down).start()

    def send_own(u):
        tile = full.at[tile_of(u, dp, shards)]
        pltpu.make_async_copy(tile, tile, load_sem.at[u]).wait()
        along(u, row, part(u, dp, plane))
        across_own(u)

    def across_own(u):
        ref = part(u, dp, plane)
        remote(ref, ref, xs_sem, xr_sem.at[u], across).start()

    def to_deck(u, shard):
        ref = part(u, shard, solo)
        remote(ref, ref, ys_sem, yr_sem.at[u], other_deck).start()

    def to_core(u, shard):
        ref = part(u, shard, plane)
        remote(ref, ref, cp_sem, cpr_sem.at[u], sibling).start()

    def begin():
        barrier, count = greet_all(dp, sq, shards, seqn)
        for load in loads:
            load.start()
        xload.start()
        pl.semaphore_wait(barrier, count)

        def send_vec(step, carry):
            to = (lax.rem(dp + step, shards), sq)
            remote(vall.at[dp], vall.at[dp], vec_send, vec_recv, to).start()
            return carry

        lax.fori_loop(1, shards, send_vec, 0)

        def first(u, carry):
            send_own(u)
            return carry

        lax.fori_loop(0, AHEAD, first, 0)

        xload.wait()
        x_deck.start()
        x_core.start()

    def step(n):
        @pl.when(n + AHEAD < UNITS)
        def _():
            send_own(n + AHEAD)

        def hop(t, carry):
            u = n - (t - 1)

            def arrived(s):
                ref = part(u, s * 2 + side, plane)
                remote(ref, ref, xs_sem, zr_sem.at[u, s], across).wait_recv()
                along(u, s, ref)
                remote(ref, ref, xs_sem, xr_sem.at[u], across).start()
                to_deck(u, s * 2 + side)
                to_core(u, s * 2 + side)

            @pl.when((u >= 0) & (u < UNITS))
            def _():
                pl.when(row - t >= 0)(lambda: arrived(row - t))
                pl.when(row + t < rows)(lambda: arrived(row + t))

            return carry

        lax.fori_loop(1, rows, hop, 0)
        ux = n - (rows - 1)

        @pl.when((ux >= 0) & (ux < UNITS))
        def _():
            remote(many(rows, 2), many(rows, 2), xs_sem, xr_sem.at[ux], across).wait_recv()

            def pass_on(s, carry):
                to_deck(ux, s * 2 + 1 - side)
                to_core(ux, s * 2 + 1 - side)
                return carry

            lax.fori_loop(0, rows, pass_on, 0)

        uy = n - rows

        @pl.when((uy >= 0) & (uy < UNITS))
        def _():
            remote(many(shards - 1, 1), many(shards - 1, 1), ys_sem, yr_sem.at[uy], other_deck).wait_recv()

            def pass_on(k, carry):
                ref = part(uy, lax.rem(dp + k, shards), theirs)
                remote(ref, ref, cy_sem, cyr_sem.at[uy], sibling).start()
                return carry

            lax.fori_loop(1, shards, pass_on, 0)

    def pass_x():
        x_deck.wait_recv()
        x_forward.start()

    def wait_x():
        x_core.wait_recv()
        x_forward.wait_recv()

    def wait_vec():
        rest = vall.at[pl.ds(0, shards - 1)]
        remote(rest, rest, vec_send, vec_recv, sibling).wait_recv()

    def whole(u):
        remote(many(shards - 1, 2), many(shards - 1, 2), cp_sem, cpr_sem.at[u], sibling).wait_recv()
        remote(many(shards - 1, 1), many(shards - 1, 1), cy_sem, cyr_sem.at[u], sibling).wait_recv()

    def finish():
        x_deck.wait_send()
        x_core.wait_send()
        x_forward.wait_send()
        rest = vall.at[pl.ds(0, shards - 1)]
        remote(rest, rest, vec_send, vec_recv, sibling).wait_send()
        for count, size, sem in (
            (UNITS * rows, 2, xs_sem),
            (UNITS * (shards - 1), 1, ys_sem),
            (UNITS * (shards - 1), 1, cy_sem),
            (UNITS * (shards - 1), 2, cp_sem),
        ):
            ref = many(count, size)
            remote(ref, ref, sem, xr_sem.at[0], sibling).wait_send()

        def sent(s, carry):
            ref = many(UNITS, 2)

            @pl.when((s <= row) & (row < rows - 1))
            def _():
                remote(ref, ref, zu_sem.at[s], xr_sem.at[0], sibling).wait_send()

            @pl.when((s >= row) & (row > 0))
            def _():
                remote(ref, ref, zd_sem.at[s], xr_sem.at[0], sibling).wait_send()

            return carry

        lax.fori_loop(0, rows, sent, 0)

    return begin, step, whole, pass_x, wait_x, wait_vec, finish


def gather_scratch(shards):
    dma = pltpu.SemaphoreType.DMA
    return [dma((UNITS + 1,))] + [dma((shards // 2,))] * 2 + [dma(())] * 4 + [dma((UNITS, shards // 2))] + [dma((UNITS,))] * 4 + [dma((3,)), dma((3,)), dma(()), dma(())]


GATHER_SCRATCH = 16


def reduce_front(shards, rows_of, count, scratch):
    f32, bf16 = jnp.float32, jnp.bfloat16
    acc, got_core, got_deck, load_sem, core_send, core_recv, deck_send, deck_recv = scratch
    dp, sq, row, side, deck, core = place()
    rows = shards // 2
    other_deck = (dp, (1 - deck) * 2 + core)
    sibling = (dp, deck * 2 + 1 - core)
    cut, _ = cutter(rows_of)
    mine = cut(core * 3, 3)
    siblings = cut((1 - core) * 3, 3)
    solo = cut(deck * 2, 1)
    other_solo = cut((1 - deck) * 2, 1)

    def send(u, tiles):
        def one(s, carry):
            for b in range(2):
                tile = tiles(s * 2 + b)
                remote(tile.at[siblings], got_core.at[u, s, b], core_send.at[u], core_recv.at[u], sibling).start()
                pltpu.make_async_copy(tile.at[mine], acc.at[u, s, b], load_sem.at[u]).start()
            return carry

        lax.fori_loop(0, rows, one, 0)

    def core_copy(u):
        return remote(got_core.at[u], got_core.at[u], core_send.at[u], core_recv.at[u], sibling)

    def deck_copy(u):
        src = acc.at[(u, slice(None), slice(None)) + other_solo]
        return remote(src, got_deck.at[u], deck_send.at[u], deck_recv.at[u], other_deck)

    def stage_core(u):
        pltpu.make_async_copy(acc.at[u], acc.at[u], load_sem.at[u]).wait()
        core_copy(u).wait_recv()

        def add(s, carry):
            for b in range(2):
                acc[u, s, b] = total(acc[u, s, b], got_core[u, s, b])
            return carry

        lax.fori_loop(0, rows, add, 0)
        deck_copy(u).start()

    def stage_deck(u):
        deck_copy(u).wait_recv()

        def add(s, carry):
            for b in range(2):
                at = (u, s, b) + solo
                acc[at] = total(acc[at], got_deck[u, s, b])
            return carry

        lax.fori_loop(0, rows, add, 0)

    def sent():
        def one(u, carry):
            core_copy(u).wait_send()
            deck_copy(u).wait_send()
            return carry

        lax.fori_loop(0, count, one, 0)

    return send, stage_core, stage_deck, sent


def total(left, right):
    return left + right


def front_scratch(shards, rows_of, count):
    bf16 = jnp.bfloat16
    rows = shards // 2
    _, shape = cutter(rows_of)
    return [
        pltpu.VMEM((count, rows, 2) + shape(3), bf16),
        pltpu.VMEM((count, rows, 2) + shape(3), bf16),
        pltpu.VMEM((count, rows, 2) + shape(1), bf16),
    ] + [pltpu.SemaphoreType.DMA((count,))] * 5


FRONT_SCRATCH = 8


def reduce_back(shards, rows_of, out, scratch):
    f32, bf16 = jnp.float32, jnp.bfloat16
    (own_side, got_across, line, got_line, final, got_final, half, got_half,
     side_sem, across_send, across_recv, line_send, line_recv, final_send, final_recv, half_send, half_recv) = scratch
    dp, sq, row, side, deck, core = place()
    rows = shards // 2
    across = (row * 2 + 1 - side, sq)
    other_deck = (dp, (1 - deck) * 2 + core)
    sibling = (dp, deck * 2 + 1 - core)
    cut, _ = cutter(rows_of)
    mine = cut(core * 3, 3)
    siblings = cut((1 - core) * 3, 3)
    plane = cut(deck, 2)
    other_solo = cut((1 - deck) * 2, 1)

    def send_across(u, planes):
        remote(
            planes.at[(slice(None), 1 - side) + plane], got_across.at[u], across_send.at[u], across_recv.at[u], across
        ).start()
        pltpu.make_async_copy(planes.at[(slice(None), side) + plane], own_side.at[u], side_sem.at[u]).start()

    def across_copy(u):
        return remote(got_across.at[u], got_across.at[u], across_send.at[u], across_recv.at[u], across)

    def line_copy(u):
        ref = got_line.at[u, pl.ds(0, rows - 1)]
        return remote(ref, ref, line_send.at[u], line_recv.at[u], across)

    def final_copy(u):
        return remote(final.at[u], got_final.at[u], final_send.at[u], final_recv.at[u], other_deck)

    def half_copy(u):
        return remote(half.at[u], got_half.at[u], half_send.at[u], half_recv.at[u], sibling)

    def stage_across(u):
        pltpu.make_async_copy(own_side.at[u], own_side.at[u], side_sem.at[u]).wait()
        across_copy(u).wait_recv()

        def add(k, carry):
            s = lax.rem(row + k, rows)
            line[u, s] = total(own_side[u, s], got_across[u, s])

            @pl.when(k < rows)
            def _():
                remote(
                    line.at[u, s], got_line.at[u, rows - 1 - k], line_send.at[u], line_recv.at[u], (s * 2 + side, sq)
                ).start()

            return carry

        lax.fori_loop(1, rows + 1, add, 0)

    def stage_line(u):
        line_copy(u).wait_recv()
        summed = line[u, row].astype(f32)
        if rows <= 4:
            for k in range(rows - 1):
                summed = summed + got_line[u, k].astype(f32)
        else:
            summed = lax.fori_loop(0, rows - 1, lambda k, t: t + got_line[u, k].astype(f32), summed)
        final[u] = summed.astype(bf16)
        final_copy(u).start()

    def stage_final(u):
        final_copy(u).wait_recv()
        half[(u,) + plane] = final[u]
        half[(u,) + other_solo] = got_final[(u,) + cut(1 - deck, 1)]
        both = (u,) + cut(1, 1)
        half[both] = total(half[both], got_final[(u,) + cut(deck, 1)])
        half_copy(u).start()

    def stage_half(u):
        half_copy(u).wait_recv()
        out[(u,) + mine] = half[u].astype(f32)
        out[(u,) + siblings] = got_half[u].astype(f32)

    def sent():
        def one(u, carry):
            for copy in (across_copy, line_copy, final_copy, half_copy):
                copy(u).wait_send()
            return carry

        lax.fori_loop(0, UNITS, one, 0)

    return send_across, (stage_across, stage_line, stage_final, stage_half), sent


def back_scratch(shards, rows_of):
    bf16 = jnp.bfloat16
    rows = shards // 2
    _, shape = cutter(rows_of)
    return [pltpu.VMEM((UNITS, rows) + shape(2), bf16)] * 4 + [
        pltpu.VMEM((UNITS,) + shape(2), bf16),
        pltpu.VMEM((UNITS,) + shape(2), bf16),
        pltpu.VMEM((UNITS,) + shape(3), bf16),
        pltpu.VMEM((UNITS,) + shape(3), bf16),
    ] + [pltpu.SemaphoreType.DMA((UNITS,))] * 9


BACK_SCRATCH = 17


def small_steps(shards, seqn, small, scratch):
    got_small, mid_small, got_mid, got_all, small_send, small_recv = scratch
    dp, sq, row, side, deck, core = place()
    sibling = (dp, deck * 2 + 1 - core)

    def small_first():
        got_small[dp] = small[dp]

        def send(k, carry):
            to = lax.rem(dp + k, shards)
            remote(small.at[to], got_small.at[dp], small_send.at[0], small_recv.at[0], (to, sq)).start()
            return carry

        lax.fori_loop(1, shards, send, 0)

    def sum_of(ref, count):
        summed = ref[0]
        for i in range(1, count):
            summed = summed + ref[i]
        return summed

    def small_second():
        rest = got_small.at[pl.ds(0, shards - 1)]
        remote(rest, rest, small_send.at[0], small_recv.at[0], sibling).wait()
        summed = sum_of(got_small, shards)
        mid_small[0] = summed
        got_mid[sq] = summed

        def send(k, carry):
            to = (dp, lax.rem(sq + k, seqn))
            remote(mid_small.at[0], got_mid.at[sq], small_send.at[1], small_recv.at[1], to).start()
            return carry

        lax.fori_loop(1, seqn, send, 0)

    def small_third():
        rest = got_mid.at[pl.ds(0, seqn - 1)]
        remote(rest, rest, small_send.at[1], small_recv.at[1], sibling).wait()
        summed = sum_of(got_mid, seqn)
        mid_small[1] = summed
        got_all[dp] = summed

        def send(k, carry):
            to = (lax.rem(dp + k, shards), sq)
            remote(mid_small.at[1], got_all.at[dp], small_send.at[2], small_recv.at[2], to).start()
            return carry

        lax.fori_loop(1, shards, send, 0)

    def small_last(small_out):
        rest = got_all.at[pl.ds(0, shards - 1)]
        remote(rest, rest, small_send.at[2], small_recv.at[2], sibling).wait()
        small_out[...] = got_all[...]

    return small_first, small_second, small_third, small_last


def small_scratch(shards, seqn, small_shape):
    f32 = jnp.float32
    return [
        pltpu.VMEM(small_shape, f32),
        pltpu.VMEM((2,) + small_shape[1:], f32),
        pltpu.VMEM((seqn,) + small_shape[1:], f32),
        pltpu.VMEM(small_shape, f32),
    ] + [pltpu.SemaphoreType.DMA((3,))] * 2


SMALL_SCRATCH = 6


def dx_steps(dxs, scratch):
    f32, bf16 = jnp.float32, jnp.bfloat16
    dx_own, dx_core, dx_deck, load, send, recv = scratch
    dp, sq, row, side, deck, core = place()
    other_deck = (dp, (1 - deck) * 2 + core)
    sibling = (dp, deck * 2 + 1 - core)
    deck_dx = remote(dx_own.at[1 - deck], dx_deck, send.at[2], recv.at[2], other_deck)

    def first():
        for k in range(2):
            pltpu.make_async_copy(dxs.at[k * 2 + core], dx_own.at[k], load.at[k]).start()
            remote(dxs.at[k * 2 + 1 - core], dx_core.at[k], send.at[k], recv.at[k], sibling).start()

    def second():
        for k in range(2):
            pltpu.make_async_copy(dx_own.at[k], dx_own.at[k], load.at[k]).wait()
            remote(dx_core.at[k], dx_core.at[k], send.at[k], recv.at[k], sibling).wait()
            dx_own[k] = (dx_own[k].astype(f32) + dx_core[k].astype(f32)).astype(bf16)
        deck_dx.start()

    def third(dx_out):
        deck_dx.wait()
        dx_out[...] = dx_own[deck].astype(f32) + dx_deck[...].astype(f32)

    return first, second, third


def dx_scratch(own):
    bf16 = jnp.bfloat16
    dma = pltpu.SemaphoreType.DMA
    return [pltpu.VMEM((2,) + own, bf16), pltpu.VMEM((2,) + own, bf16), pltpu.VMEM(own, bf16), dma((2,)), dma((3,)), dma((3,))]


bucket_marks = (12, 16, 23, 32, 46, 64, 91)
MASKED = NB
TN = (((0,), (0,)), ((), ()))
NT = (((1,), (1,)), ((), ()))


def dot(left, right, dims=None):
    if dims is None:
        dims = (((1,), (0,)), ((), ()))
    return lax.dot_general(left, right, dims, preferred_element_type=jnp.float32)


def column_of(row):
    return jnp.broadcast_to(row.astype(jnp.float32), (row.shape[1], row.shape[1])).T


def fill_buckets(buckets, positions, lengths, base, seqs, block, span):
    for s in range(seqs):
        mine = column_of(positions[s : s + 1, pl.ds(pl.multiple_of(base, block), block)]).astype(jnp.int32)
        for c in range(span // block):
            cols = slice(c * block, (c + 1) * block)
            delta = positions[s : s + 1, cols] - mine
            dist = jnp.abs(delta)
            far = jnp.full(dist.shape, 8, jnp.int32)
            for mark in bucket_marks:
                far = far + (dist >= mark).astype(jnp.int32)
            bucket = jnp.where(dist < 8, dist, far) + 16 * (delta > 0).astype(jnp.int32)
            i = base + lax.broadcasted_iota(jnp.int32, (block, block), 0)
            j = c * block + lax.broadcasted_iota(jnp.int32, (block, block), 1)
            valid = j < lengths[s]
            buckets[s, 0, :, cols] = jnp.where(valid & (j <= i), bucket, MASKED)
            buckets[s, 1, :, cols] = jnp.where(valid & (j < jnp.maximum(i, 1)), bucket, MASKED)


def head_lanes(rows, half):
    lane = lax.broadcasted_iota(jnp.int32, (rows, 2 * HD), 1)
    return (lane < HD) if half == 0 else (lane >= HD)


def fill_bias(i, biases, buckets, table, block, span):
    s, head = i // H, lax.rem(i, H)
    entry = jnp.broadcast_to(table[pl.ds(head, 1), :], (block, 128))
    for c in range(span // 128):
        cols = slice(c * 128, (c + 1) * 128)
        value = jnp.take_along_axis(entry, buckets[s, 0, :, cols], axis=1, mode="promise_in_bounds")
        biases[i, 0, :, cols] = value
        biases[i, 1, :, cols] = jnp.where(buckets[s, 1, :, cols] == MASKED, -1e30, value)


def attend_pair(i, refs, block, span, low_out):
    attended, query, keys, values, biases = refs
    f32, bf16 = jnp.float32, jnp.bfloat16
    pairs = H // 2
    s, pair = i // pairs, lax.rem(i, pairs)
    lanes = pl.ds(pl.multiple_of(pair * 128, 128), 128)
    q = query[:, s, :, lanes].reshape(2 * block, 128)
    k = keys[s, :, lanes]
    v = values[s, :, lanes]
    outs = []
    for half in range(2):
        mine = head_lanes(2 * block, half)
        one = jnp.where(mine, q * 0.125, 0).astype(bf16)
        scores = dot(one, k, NT) + biases[i * 2 + half].reshape(2 * block, span)
        top = jnp.max(scores, axis=-1, keepdims=True)
        expo = jnp.exp(scores - top)
        low = (expo * (1.0 / jnp.sum(expo, axis=-1, keepdims=True))).astype(bf16)
        low_out[half] = low
        outs.append(dot(low, v))
    mixed = jnp.where(head_lanes(2 * block, 0), outs[0], outs[1]).astype(bf16)
    attended[:, s, :, lanes] = mixed.reshape(2, block, 128)


def center_of(value):
    center = value - jnp.mean(value, axis=-1, keepdims=True)
    var = jnp.mean(center * center, axis=-1, keepdims=True)
    inv = lax.rsqrt(var + 1e-05)
    return center * inv, inv


def norm_back(grad, gain, normed, inv):
    scaled = grad * gain
    return inv * (
        scaled
        - jnp.mean(scaled, axis=-1, keepdims=True)
        - normed * jnp.mean(scaled * normed, axis=-1, keepdims=True)
    )


EARLY = 8
TILE = 256
LONG = 384
DOWNS = 4


def forward_kernel(
    shards, seqn, seqs, block, span, rows_of,
    lengths, wk, wv, wq, wo, wu, wd, xc, xc_rows, xq_rows, cot_c, cot_q, positions, predicted, rel_table,
    bq, bv, bo, g1, b1, c2, g2, b2, c1,
    squares, x_out, probs, attended_out, query_out, keys_out, values_out, y_c, y_q, dr1_out, da_out, grads, downs, dvec,
    full, xall, vall, vectors, keep, attended, table, io_sem, low_sem, *scratch,
):
    f32, bf16 = jnp.float32, jnp.bfloat16
    width = H * HD
    half = seqs * block
    rows = 2 * half
    r = rows_of
    wide = 4 * r
    base = lax.axis_index("seq") * block
    me = lax.axis_index("dp")
    begin, step, whole, pass_x, wait_x, wait_vec, finish = gather_steps(
        shards, seqn, (wk, wv, wq, wo, wu, wd, xc), (full, xall, vall), scratch[: -FRONT_SCRATCH]
    )
    send_front, stage_core, stage_deck, front_sent = reduce_front(shards, r, DOWNS, scratch[-FRONT_SCRATCH:])
    acc = scratch[-FRONT_SCRATCH]
    vall[me] = jnp.zeros(vall.shape[1:], f32)
    for i, piece in enumerate((bq, bv, bo, g1, b1, c2, g2, b2)):
        vall[me, i : i + 1, 0:r] = piece[...].astype(f32)
    vall[me, 8:9, :] = c1[...].astype(f32)
    begin()

    def one(n, carry):
        step(n)
        return carry

    def matrix(u):
        return full[pl.ds(u * shards, shards)].reshape(width, width)

    def columns(u, cols):
        size = cols.size
        return full[pl.ds(u * shards, shards), :, cols].reshape(width, size)

    def row_block(u, n):
        per = LONG // r
        return full[pl.ds(u * shards + n * per, per)].reshape(LONG, width)

    def attention(query, keys, values, buckets, low_two, biases):
        fill_buckets(buckets, positions, lengths, base, seqs, block, span)
        eye = (
            lax.broadcasted_iota(jnp.int32, (NB, 128), 0) == lax.broadcasted_iota(jnp.int32, (NB, 128), 1)
        )
        by_head = dot(rel_table[...], jnp.where(eye, 1.0, 0.0).astype(bf16), TN)
        lane = lax.broadcasted_iota(jnp.int32, by_head.shape, 1)
        table[...] = jnp.where(lane < NB, by_head, -1e30)
        for s in range(seqs):
            live = base + lax.broadcasted_iota(jnp.int32, (block, 1), 0) < lengths[s]
            chosen = column_of(predicted[s : s + 1, :])[:, 0:1] > 0
            keep[s * block : (s + 1) * block, :] = jnp.where(live, 1.0, 0.0)
            keep[half + s * block : half + (s + 1) * block, :] = jnp.where(live & chosen, 1.0, 0.0)
        share = seqs * H // EARLY

        def one_and_bias(n, carry):
            step(n)

            def bias(k, inner):
                fill_bias(n * share + k, biases, buckets, table, block, span)
                return inner

            return lax.fori_loop(0, share, bias, carry)

        lax.fori_loop(0, EARLY - 2, one_and_bias, 0)
        pass_x()
        lax.fori_loop(EARLY - 2, EARLY, one_and_bias, 0)
        wait_x()
        wait_vec()
        vectors[...] = jnp.zeros_like(vectors)

        def spread(i, carry):
            row = lax.broadcasted_iota(jnp.int32, (r, width), 0)
            col = lax.broadcasted_iota(jnp.int32, (r, width), 1)
            at = jnp.where(col == row + i * r, 1.0, 0.0).astype(bf16)
            vectors[0:8, :] += dot(vall[i, 0:8, 0:r].astype(bf16), at)
            per = width // wide
            row = lax.broadcasted_iota(jnp.int32, (wide, width), 0)
            col = lax.broadcasted_iota(jnp.int32, (wide, width), 1)
            at = jnp.where(col == row + lax.rem(i, per) * wide, 1.0, 0.0).astype(bf16)
            vectors[pl.ds(8 + i // per, 1), :] += dot(vall[i, 8:9, :].astype(bf16), at)
            return carry

        lax.fori_loop(0, shards, spread, 0)
        for u in range(3):
            whole(u)

        def project(k, carry):
            x = xall[k].reshape(half, width)
            at = pl.ds(pl.multiple_of(k * block, block), block)
            keys[:, at, :] = dot(x, matrix(0)).astype(bf16).reshape(seqs, block, width)
            values[:, at, :] = (dot(x, matrix(1)) + vectors[1:2, :]).astype(bf16).reshape(seqs, block, width)
            return carry

        lax.fori_loop(0, seqn, project, 0)
        for t, x in enumerate((xc_rows, xq_rows)):
            query[t] = (dot(x[...], matrix(2)) + vectors[0:1, :]).astype(bf16).reshape(seqs, block, width)
        puts = [
            pltpu.make_async_copy(src, dst, io_sem.at[i])
            for i, (src, dst) in enumerate(((query, query_out), (keys, keys_out), (values, values_out)))
        ]
        for copy in puts:
            copy.start()
        total = seqs * H // 2

        def put(i, slot):
            return pltpu.make_async_copy(low_two.at[slot], probs.at[i], low_sem.at[slot])

        def attend_one(i, carry):
            slot = lax.rem(i, 2)

            @pl.when(lax.rem(i, 4) == 0)
            def _():
                step(EARLY + i // 4)

            @pl.when(i >= 2)
            def _():
                put(i - 2, slot).wait()

            attend_pair(i, (attended, query, keys, values, biases), block, span, low_two.at[slot])
            put(i, slot).start()
            return carry

        lax.fori_loop(0, total, attend_one, 0)
        put(total - 2, (total - 2) % 2).wait()
        put(total - 1, (total - 1) % 2).wait()
        for copy in puts:
            copy.wait()

    pl.run_scoped(
        attention,
        pltpu.VMEM((2, seqs, block, width), bf16),
        pltpu.VMEM((seqs, span, width), bf16),
        pltpu.VMEM((seqs, span, width), bf16),
        pltpu.VMEM((seqs, 2, block, span), jnp.int32),
        pltpu.VMEM((2, 2, 2 * block, span), bf16),
        pltpu.VMEM((seqs * H, 2, block, span), f32),
    )
    done = EARLY + seqs * H // 8
    more = [
        pltpu.make_async_copy(full.at[pl.ds(0, 3 * shards)], squares, io_sem.at[3]),
        pltpu.make_async_copy(xall, x_out, io_sem.at[4]),
        pltpu.make_async_copy(attended, attended_out, io_sem.at[5]),
    ]
    for copy in more:
        copy.start()
    dvec[...] = jnp.zeros_like(dvec)
    vec = lambda i: vectors[i : i + 1, :]
    chunk = 128
    chunks = half // chunk

    def ffn(hidden, hidden_low, hidden_turn, normed1, inv1, active, slope, feed, dr2, dr2_low, dr1_low, da, stage, stage_down):
        step(done)
        whole(3)

        def phase_one(c, carry):
            t, s = c // seqs, lax.rem(c, seqs)
            at = pl.ds(pl.multiple_of(c * chunk, chunk), chunk)
            out = dot(attended[t, s], matrix(3)) + vec(2)
            inner = pl.ds(pl.multiple_of(s * chunk, chunk), chunk)
            x = jnp.where(t == 0, xc_rows[inner, :].astype(f32), xq_rows[inner, :].astype(f32))
            normed, inv = center_of(x + out)
            normed1[at, :] = normed
            inv1[at, :] = inv
            h = normed * vec(3) + vec(4)
            hidden[at, :] = h
            hidden_low[at, :] = h.astype(bf16)
            return carry

        lax.fori_loop(0, rows // chunk, phase_one, 0)
        hidden_turn[...] = hidden_low[...].T
        tiles = width // TILE

        def phase_two(j, carry):
            step(done + 1 + j)
            whole(4 + j)

            def tile(n, inner):
                cols = pl.ds(pl.multiple_of(n * TILE, TILE), TILE)
                u = dot(hidden_low[...], columns(4 + j, cols)) + vectors[pl.ds(8 + j, 1), cols]
                cdf = 0.5 * (1.0 + lax.erf(u * (2.0**-0.5)))
                active[j, :, cols] = (u * cdf).astype(bf16)
                slope[j, :, cols] = (cdf + u * (jnp.exp(-0.5 * u * u) * ((2.0 * jnp.pi) ** -0.5))).astype(bf16)
                return inner

            return lax.fori_loop(0, tiles, tile, carry)

        lax.fori_loop(0, 4, phase_two, 0)

        def last(u, carry):
            whole(u)
            return carry

        lax.fori_loop(done + 5, UNITS + shards // 2, one, 0)
        lax.fori_loop(8, UNITS, last, 0)

        def phase_feed(n, carry):
            cols = pl.ds(pl.multiple_of(n * TILE, TILE), TILE)
            feed[:, cols] = sum(dot(active[j], columns(8 + j, cols)) for j in range(4))
            return carry

        lax.fori_loop(0, tiles, phase_feed, 0)

        def phase_three(c, carry):
            t, s = c // seqs, lax.rem(c, seqs)
            at = pl.ds(pl.multiple_of(c * chunk, chunk), chunk)
            normed, inv = center_of(hidden[at, :] + feed[at, :] + vec(5))
            kept = keep[at, :]
            feed[at, :] = (normed * vec(6) + vec(7)) * kept
            inner = pl.ds(pl.multiple_of(s * chunk, chunk), chunk)
            cot = jnp.where(t == 0, cot_c[inner, :].astype(f32), cot_q[inner, :].astype(f32)) * kept
            d = norm_back(cot, vec(6), normed, inv)
            dvec[6:7, :] += jnp.sum(cot * normed, axis=0, keepdims=True)
            dvec[7:8, :] += jnp.sum(cot, axis=0, keepdims=True)
            dvec[5:6, :] += jnp.sum(d, axis=0, keepdims=True)
            dr2[at, :] = d
            dr2_low[at, :] = d.astype(bf16)
            return carry

        lax.fori_loop(0, rows // chunk, phase_three, 0)
        y_copies = [
            pltpu.make_async_copy(feed.at[pl.ds(0, half)], y_c, io_sem.at[6]),
            pltpu.make_async_copy(feed.at[pl.ds(half, half)], y_q, io_sem.at[7]),
        ]
        for copy in y_copies:
            copy.start()
        longs = width // LONG

        def phase_down(step_, carry):
            j, n = step_ // longs, lax.rem(step_, longs)
            cols = pl.ds(pl.multiple_of(n * LONG, 128), LONG)
            grad = dot(active[j, :, cols], dr2_low[...], TN).astype(bf16)
            per = LONG // r
            stage_down[pl.ds(step_ * per, per)] = grad.reshape(per, r, width)
            return carry

        lax.fori_loop(0, 4 * longs, phase_down, 0)

        def start_down(k, carry):
            send_front(k, lambda shard: stage_down.at[shard * 4 + k])
            return carry

        lax.fori_loop(0, DOWNS, start_down, 0)

        def phase_slope(step_, carry):
            j, n = step_ // longs, lax.rem(step_, longs)
            cols = pl.ds(pl.multiple_of(n * LONG, 128), LONG)
            du = slope[j, :, cols].astype(f32) * dot(dr2_low[...], row_block(8 + j, n), NT)
            dvec[pl.ds(8 + j, 1), cols] = jnp.sum(du, axis=0, keepdims=True)
            active[j, :, cols] = du.astype(bf16)

            @pl.when(n == longs - 1)
            def _():
                stage_core(j)

            return carry

        lax.fori_loop(0, 4 * longs, phase_slope, 0)

        def phase_up(j, carry):
            def tile(n, inner):
                cols = pl.ds(pl.multiple_of(n * TILE, TILE), TILE)
                grad = dot(hidden_turn[...], active[j, :, cols]).astype(bf16)
                stage[1 + j, :, :, cols] = grad.reshape(shards, r, TILE)
                return inner

            lax.fori_loop(0, tiles, tile, 0)
            pltpu.make_async_copy(
                stage.at[1 + j], grads.at[pl.ds((1 + j) * shards, shards)], io_sem.at[10 + j]
            ).start()
            return carry

        lax.fori_loop(0, 4, phase_up, 0)

        def put_down(k):
            return pltpu.make_async_copy(acc.at[k], downs.at[k], io_sem.at[14 + k])

        def finish_down(k):
            stage_deck(k)
            put_down(k).start()

        finish_down(0)

        def phase_hidden(n, carry):
            cols = pl.ds(pl.multiple_of(n * LONG, 128), LONG)
            dr2[:, cols] += sum(dot(active[j], row_block(4 + j, n), NT) for j in range(4))
            return carry

        lax.fori_loop(0, longs, phase_hidden, 0)
        for copy in y_copies:
            copy.wait()
        finish_down(1)

        def phase_five(c, carry):
            at = pl.ds(pl.multiple_of(c * chunk, chunk), chunk)
            dh = dr2[at, :]
            normed = normed1[at, :]
            d = norm_back(dh, vec(3), normed, inv1[at, :])
            dvec[3:4, :] += jnp.sum(dh * normed, axis=0, keepdims=True)
            dvec[4:5, :] += jnp.sum(dh, axis=0, keepdims=True)
            dvec[2:3, :] += jnp.sum(d, axis=0, keepdims=True)
            feed[at, :] = d
            low = d.astype(bf16)
            dr1_low[at, :] = low
            da[at, :] = dot(low, matrix(3), NT).astype(bf16)
            return carry

        lax.fori_loop(0, rows // chunk, phase_five, 0)
        finals = [
            pltpu.make_async_copy(feed, dr1_out, io_sem.at[6]),
            pltpu.make_async_copy(da, da_out, io_sem.at[7]),
        ]
        for copy in finals:
            copy.start()
        finish_down(2)
        turned = attended[...].reshape(rows, width).T

        def phase_out(n, carry):
            cols = pl.ds(pl.multiple_of(n * TILE, TILE), TILE)
            grad = dot(hidden_turn[...], dr1_low[:, cols]).astype(bf16)
            stage[0, :, :, cols] = grad.reshape(shards, r, TILE)
            return carry

        hidden_turn[...] = turned
        lax.fori_loop(0, tiles, phase_out, 0)
        out_copy = pltpu.make_async_copy(stage.at[0], grads.at[pl.ds(0, shards)], io_sem.at[9])
        out_copy.start()
        finish_down(3)
        for j in range(4):
            pltpu.make_async_copy(
                stage.at[1 + j], grads.at[pl.ds((1 + j) * shards, shards)], io_sem.at[10 + j]
            ).wait()
            put_down(j).wait()
        out_copy.wait()
        for copy in finals + more:
            copy.wait()
        front_sent()
        finish()

    pl.run_scoped(
        ffn,
        pltpu.VMEM((rows, width), f32),
        pltpu.VMEM((rows, width), bf16),
        pltpu.VMEM((width, rows), bf16),
        pltpu.VMEM((rows, width), f32),
        pltpu.VMEM((rows, 1), f32),
        pltpu.VMEM((4, rows, width), bf16),
        pltpu.VMEM((4, rows, width), bf16),
        pltpu.VMEM((rows, width), f32),
        pltpu.VMEM((rows, width), f32),
        pltpu.VMEM((rows, width), bf16),
        pltpu.VMEM((rows, width), bf16),
        pltpu.VMEM((rows, width), bf16),
        pltpu.VMEM((5, shards, r, width), bf16),
        pltpu.VMEM((4 * shards, r, width), bf16),
    )


def forward(wk, wv, wq, wo, wu, wd, xc, xq, cot_c, cot_q, vecs, lengths, positions, predicted, rel_table, shards, seqn):
    rows_of, width = wq.shape
    seqs, block, _ = xc.shape
    span = positions.shape[1]
    f32, bf16 = jnp.float32, jnp.bfloat16
    steps = seqs * H // 2
    half = seqs * block
    anywhere = pl.BlockSpec(memory_space=pl.ANY)
    vmem = pl.BlockSpec(memory_space=pltpu.VMEM)
    rows = shards // 2
    _, shape = cutter(rows_of)
    dma = pltpu.SemaphoreType.DMA
    flat = lambda a: a.reshape(half, width)
    stream = (2, seqs, block, width)
    return pl.pallas_call(
        functools.partial(forward_kernel, shards, seqn, seqs, block, span, rows_of),
        out_shape=(
            jax.ShapeDtypeStruct((3 * shards, rows_of, width), bf16),
            jax.ShapeDtypeStruct((seqn,) + xc.shape, bf16),
            jax.ShapeDtypeStruct((steps, 2, 2 * block, span), bf16),
            jax.ShapeDtypeStruct(stream, bf16),
            jax.ShapeDtypeStruct(stream, bf16),
            jax.ShapeDtypeStruct((seqs, span, width), bf16),
            jax.ShapeDtypeStruct((seqs, span, width), bf16),
            jax.ShapeDtypeStruct((half, width), f32),
            jax.ShapeDtypeStruct((half, width), f32),
            jax.ShapeDtypeStruct((2 * half, width), f32),
            jax.ShapeDtypeStruct((2 * half, width), bf16),
            jax.ShapeDtypeStruct((5 * shards, rows_of, width), bf16),
            jax.ShapeDtypeStruct((DOWNS, rows, 2) + shape(3), bf16),
            jax.ShapeDtypeStruct((UNITS, width), f32),
        ),
        in_specs=[pl.BlockSpec(memory_space=pltpu.SMEM)] + [anywhere] * 7 + [vmem] * 16,
        out_specs=(anywhere,) * 13 + (vmem,),
        scratch_shapes=[
            pltpu.VMEM((UNITS * shards, rows_of, width), bf16),
            pltpu.VMEM((seqn,) + xc.shape, bf16),
            pltpu.VMEM((shards, 9, 4 * rows_of), f32),
            pltpu.VMEM((UNITS, width), f32),
            pltpu.VMEM((2 * half, 1), f32),
            pltpu.VMEM(stream, bf16),
            pltpu.VMEM((H, 128), f32),
            dma((18,)),
            dma((2,)),
        ]
        + gather_scratch(shards)
        + front_scratch(shards, rows_of, DOWNS),
        compiler_params=pltpu.CompilerParams(collective_id=0, has_side_effects=True, vmem_limit_bytes=67043328),
        name="gather_attend_ffn",
    )(
        lengths, wk, wv, wq, wo, wu, wd.reshape(4, rows_of, width), xc, flat(xc), flat(xq), flat(cot_c), flat(cot_q),
        positions, predicted, rel_table, *vecs,
    )


def attend_back_pair(i, refs, low, seqs, block, span):
    attended, d_attended, query, keys, values, buckets, dq, dk, dv, ds_sum, sums, counts = refs
    f32, bf16 = jnp.float32, jnp.bfloat16
    pairs = H // 2
    rows = 2 * block
    s, pair = i // pairs, lax.rem(i, pairs)
    lanes = pl.ds(pl.multiple_of(pair * 128, 128), 128)
    q = query[:, s, :, lanes].reshape(rows, 128)
    k = keys[s, :, lanes]
    v = values[s, :, lanes]
    da = d_attended[:, s, :, lanes].reshape(rows, 128)
    product = da.astype(f32) * attended[:, s, :, lanes].reshape(rows, 128).astype(f32)
    d_queries, dk_turn, dv_turn = [], 0.0, 0.0
    for half in range(2):
        mine = head_lanes(rows, half)
        one = jnp.where(mine, da, 0).astype(bf16)
        inner = jnp.sum(jnp.where(mine, product, 0.0), axis=-1, keepdims=True)
        ds = low[half].astype(f32) * (dot(one, v, NT) - inner)
        ds_sum[pair * 2 + half] = (ds[:block] + ds[block:]).astype(bf16)
        ds_low = ds.astype(bf16)
        d_queries.append(dot(ds_low, k))
        dk_turn += dot(jnp.where(mine, q, 0).astype(bf16), ds_low, TN)
        dv_turn += dot(one, low[half], TN)
    d_query = jnp.where(head_lanes(rows, 0), d_queries[0], d_queries[1]) * 0.125
    sums[0:1, lanes] += jnp.sum(d_query, axis=0, keepdims=True)
    dq[:, s, :, lanes] = d_query.reshape(2, block, 128).astype(bf16)
    dk[s, :, lanes] = (dk_turn * 0.125).T.astype(bf16)
    d_value = dv_turn.T
    sums[1:2, lanes] += jnp.sum(d_value, axis=0, keepdims=True)
    dv[s, :, lanes] = d_value.astype(bf16)

    @pl.when(pair == pairs - 1)
    def _():
        def count(g, carry):
            at = pl.ds(pl.multiple_of(g * 16, 16), 16)
            bucket = buckets[s, 0, at, :]
            hot = jnp.concatenate([jnp.where(bucket == n, 1.0, 0.0).astype(bf16) for n in range(NB)], axis=0)
            counts[...] += dot(hot, ds_sum[:, at, :].reshape(H * 16, span), NT)
            return carry

        lax.fori_loop(0, block // 16, count, 0)


def table_of(counts):
    row = lax.broadcasted_iota(jnp.int32, counts.shape, 0)
    col = lax.broadcasted_iota(jnp.int32, counts.shape, 1)
    kept = jnp.where(lax.rem(row, 16) == lax.rem(col, 16), counts, 0.0)
    folded = jnp.sum(kept.reshape(NB, 16, H * 16), axis=1)
    lane = lax.broadcasted_iota(jnp.int32, (H * 16, 128), 1)
    head = lax.broadcasted_iota(jnp.int32, (H * 16, 128), 0) // 16
    return jnp.dot(folded, jnp.where(lane == head, 1.0, 0.0), precision=lax.Precision.HIGHEST)


def backward_kernel(
    shards, seqn, seqs, block, span, rows_of,
    lengths, grads, downs, squares, xall, probs, attended_in, da_in, query_in, keys_in, values_in, dr1_in,
    xc, xq, dvec, positions,
    out, dx_out, d_content, d_query_x, small_out,
    dq, dk, dv, late, w, x_every, dxs, sums, counts, small, io_sem, low_sem, *scratch,
):
    f32, bf16 = jnp.float32, jnp.bfloat16
    width = H * HD
    half = seqs * block
    total_pairs = seqs * H // 2
    front, scratch = scratch[:FRONT_SCRATCH], scratch[FRONT_SCRATCH:]
    back, scratch = scratch[:BACK_SCRATCH], scratch[BACK_SCRATCH:]
    send_front, stage_core, stage_deck, front_sent = reduce_front(shards, rows_of, UNITS - DOWNS, front)
    send_across, later, back_sent = reduce_back(shards, rows_of, out, back)
    small_first, small_second, small_third, small_last = small_steps(shards, seqn, small, scratch[:SMALL_SCRATCH])
    dx_first, dx_second, dx_third = dx_steps(dxs, scratch[SMALL_SCRATCH:])
    dp, sq = lax.axis_index("dp"), lax.axis_index("seq")
    acc = front[0]
    early = UNITS - DOWNS - 3
    order = lambda k: UNITS - 1 - k
    weights = [pltpu.make_async_copy(squares.at[pl.ds(u * shards, shards)], w.at[u], io_sem.at[5 + u]) for u in range(3)]
    slots = [
        pltpu.make_async_copy(xall.at[k], x_every.at[:, pl.ds(k * block, block)], io_sem.at[8 + k]) for k in range(seqn)
    ]

    def deck_and_across(u):
        stage_deck(u)
        send_across(u, acc.at[u])

    across, line, final, half_stage = later
    ready, late_from_unit = DOWNS, DOWNS + early
    plan = (
        (stage_core, ready, early, 1, 1),
        (deck_and_across, ready, early, 4, 2),
        (across, 0, DOWNS, 3, 2),
        (line, 0, DOWNS, 6, 2),
        (final, 0, DOWNS, 8, 2),
        (half_stage, 0, DOWNS, 10, 2),
        (across, ready, early, 11, 4),
        (stage_core, late_from_unit, 3, 15, 3),
        (line, ready, early, 16, 4),
        (final, ready, early, 18, 4),
        (half_stage, ready, early, 20, 4),
        (deck_and_across, late_from_unit, 3, 22, 3),
        (across, late_from_unit, 3, 29, 2),
        (line, late_from_unit, 3, 32, 2),
        (final, late_from_unit, 3, 34, 2),
        (half_stage, late_from_unit, 3, 36, 2),
    )
    ticks = 41

    def tick(t):
        for stage, first, count, start, gap in plan:
            d = t - start

            @pl.when((d >= 0) & (d < count * gap) & (lax.rem(d, gap) == 0))
            def _(stage=stage, first=first, d=d, gap=gap):
                stage(order(first + d // gap))

    def one(t, carry):
        tick(t)
        return carry

    def attention(attended, d_attended, query, keys, values, buckets, low_two, ds_sum):
        loads = [
            pltpu.make_async_copy(src, dst, io_sem.at[i])
            for i, (src, dst) in enumerate(
                ((attended_in, attended), (da_in, d_attended), (query_in, query), (keys_in, keys), (values_in, values))
            )
        ]

        def take(i, slot):
            return pltpu.make_async_copy(probs.at[i], low_two.at[slot], low_sem.at[slot])

        barrier, count = greet_all(dp, sq, shards, seqn)
        for load in loads:
            load.start()
        take(0, 0).start()
        for load in weights + slots:
            load.start()
        pl.semaphore_wait(barrier, count)

        def send(k, carry):
            u = order(DOWNS + k)
            send_front(u, lambda shard: grads.at[(u - 3) * shards + shard])
            return carry

        def send_down(k, carry):
            send_across(order(k), downs.at[order(k) - 8])
            return carry

        lax.fori_loop(0, early, send, 0)
        lax.fori_loop(0, DOWNS, send_down, 0)
        fill_buckets(buckets, positions, lengths, sq * block, seqs, block, span)
        counts[...] = jnp.zeros_like(counts)
        sums[...] = jnp.zeros_like(sums)
        for load in loads:
            load.wait()
        refs = (attended, d_attended, query, keys, values, buckets, dq, dk, dv, ds_sum, sums, counts)

        def pair(i, carry):
            slot = lax.rem(i, 2)

            tick(i)
            take(i, slot).wait()

            @pl.when(i + 1 < total_pairs)
            def _():
                take(i + 1, 1 - slot).start()

            attend_back_pair(i, refs, low_two.at[slot], seqs, block, span)
            return carry

        lax.fori_loop(0, total_pairs, pair, 0)

    pl.run_scoped(
        attention,
        pltpu.VMEM((2, seqs, block, width), bf16),
        pltpu.VMEM((2, seqs, block, width), bf16),
        pltpu.VMEM((2, seqs, block, width), bf16),
        pltpu.VMEM((seqs, span, width), bf16),
        pltpu.VMEM((seqs, span, width), bf16),
        pltpu.VMEM((seqs, 2, block, span), jnp.int32),
        pltpu.VMEM((2, 2, 2 * block, span), bf16),
        pltpu.VMEM((H, block, span), bf16),
    )

    tile = 256

    def weight_grads(dr1, turned, x_two):
        load = pltpu.make_async_copy(dr1_in, dr1, io_sem.at[0])
        load.start()
        loads = [pltpu.make_async_copy(x, x_two.at[t], io_sem.at[1 + t]) for t, x in enumerate((xc, xq))]
        for copy in loads:
            copy.start()
        for copy in weights + slots:
            copy.wait()
        matrix = lambda u: w[u].reshape(width, width)
        turned[...] = x_every[...].reshape(seqs * span, width).T

        def late_from(u, ref, first_tick):
            def tiles(n, carry):
                tick(first_tick + n)
                cols = pl.ds(pl.multiple_of(n * tile, tile), tile)
                grad = dot(turned[...], ref[:, :, cols].reshape(seqs * span, tile))
                late[u, :, :, cols] = grad.astype(bf16).reshape(shards, rows_of, tile)
                return carry

            lax.fori_loop(0, width // tile, tiles, 0)
            send_front(u, lambda shard: late.at[u, shard])

        for copy in loads:
            copy.wait()

        def tiles(n, carry):
            tick(12 + n)
            cols = pl.ds(pl.multiple_of(n * tile, tile), tile)
            grad = sum(
                dot(x_two[t].reshape(half, width), dq[t, :, :, cols].reshape(half, tile), TN) for t in range(2)
            )
            late[2, :, :, cols] = grad.astype(bf16).reshape(shards, rows_of, tile)
            return carry

        lax.fori_loop(0, width // tile, tiles, 0)
        send_front(2, lambda shard: late.at[2, shard])
        late_from(1, dv, 15)
        late_from(0, dk, 18)

        def every(n, carry):
            tick(21 + n)
            s, k = n // seqn, lax.rem(n, seqn)
            at = pl.ds(pl.multiple_of(k * block, block), block)
            part = dot(dk[s, at, :], matrix(0), NT) + dot(dv[s, at, :], matrix(1), NT)
            dxs[k, pl.ds(pl.multiple_of(s * block, block), block), :] = part.astype(bf16)
            return carry

        lax.fori_loop(0, seqs * seqn, every, 0)
        dx_first()
        load.wait()
        for t, d_x in enumerate((d_content, d_query_x)):
            d_x[...] = dr1[pl.ds(t * half, half), :] + dot(dq[t].reshape(half, width), matrix(2), NT)

    pl.run_scoped(
        weight_grads,
        pltpu.VMEM((2 * half, width), f32),
        pltpu.VMEM((width, seqs * span), bf16),
        pltpu.VMEM((2, seqs, block, width), bf16),
    )
    table = table_of(counts[...])
    vectors = jnp.concatenate([sums[0:2, :], dvec[2:, :], jnp.zeros((4, width), f32)], axis=0)
    pieces = [vectors[:, c * 128 : (c + 1) * 128] for c in range(width // 128)] + [table[:16], table[16:]]
    each = shards // 8
    size = 16 // each
    for p, piece in enumerate(pieces):
        for k in range(each):
            small[p * each + k] = piece[k * size : (k + 1) * size]
    small_first()
    lax.fori_loop(29, 31, one, 0)
    dx_second()
    lax.fori_loop(31, 33, one, 0)
    small_second()
    lax.fori_loop(33, 36, one, 0)
    small_third()
    lax.fori_loop(36, ticks, one, 0)
    dx_third(dx_out)
    small_last(small_out)
    front_sent()
    back_sent()


def backward(lengths, grads, downs, squares, xall, probs, attended, d_attended, query, keys, values, dr1, xc, xq, dvec, positions, shards, seqn):
    rows_of, width = squares.shape[1:]
    seqs, block, _ = xc.shape
    span = positions.shape[1]
    f32, bf16 = jnp.float32, jnp.bfloat16
    anywhere = pl.BlockSpec(memory_space=pl.ANY)
    vmem = pl.BlockSpec(memory_space=pltpu.VMEM)
    own = (seqs * block, width)
    small_shape = (shards, 128 // shards, 128)
    dma = pltpu.SemaphoreType.DMA
    return pl.pallas_call(
        functools.partial(backward_kernel, shards, seqn, seqs, block, span, rows_of),
        out_shape=(
            jax.ShapeDtypeStruct((UNITS, rows_of, width), f32),
            jax.ShapeDtypeStruct(own, f32),
            jax.ShapeDtypeStruct(own, f32),
            jax.ShapeDtypeStruct(own, f32),
            jax.ShapeDtypeStruct(small_shape, f32),
        ),
        in_specs=[pl.BlockSpec(memory_space=pltpu.SMEM)] + [anywhere] * 13 + [vmem] * 2,
        out_specs=(vmem,) * 5,
        scratch_shapes=[
            pltpu.VMEM((2, seqs, block, width), bf16),
            pltpu.VMEM((seqs, span, width), bf16),
            pltpu.VMEM((seqs, span, width), bf16),
            pltpu.VMEM((3, shards, rows_of, width), bf16),
            pltpu.VMEM((3, shards, rows_of, width), bf16),
            pltpu.VMEM((seqs, span, width), bf16),
            pltpu.VMEM((seqn,) + own, bf16),
            pltpu.VMEM((8, width), f32),
            pltpu.VMEM((NB * 16, H * 16), f32),
            pltpu.VMEM(small_shape, f32),
            dma((8 + seqn,)),
            dma((2,)),
        ]
        + front_scratch(shards, rows_of, UNITS - DOWNS)
        + back_scratch(shards, rows_of)
        + small_scratch(shards, seqn, small_shape)
        + dx_scratch(own),
        compiler_params=pltpu.CompilerParams(
            collective_id=1, has_side_effects=True, vmem_limit_bytes=67043328
        ),
        name="attend_back_reduce",
    )(lengths, grads, downs, squares, xall, probs, attended, d_attended, query, keys, values, dr1, xc, xq, dvec, positions)


def per_device(
    x_content, x_query, cot_content, cot_query,
    w_query, b_query, w_key, w_value, b_value, w_out, b_out, gain_attn, shift_attn,
    w_up, b_up, w_down, b_down, gain_ffn, shift_ffn, rel_table, lengths, positions, predicted,
    *, shards, seqn,
):
    f32 = jnp.float32
    seqs, block, width = x_content.shape
    r = w_query.shape[0]
    vecs = [
        v.reshape(1, v.shape[0])
        for v in (b_query, b_value, b_out, gain_attn, shift_attn, b_down, gain_ffn, shift_ffn, b_up)
    ]
    (squares, xall, probs, attended, query, keys, values, y_c, y_q, dr1, d_attended, grads, downs, dvec) = forward(
        w_key, w_value, w_query, w_out, w_up, w_down, x_content, x_query, cot_content, cot_query, vecs,
        lengths, positions, predicted, rel_table, shards, seqn,
    )
    sums, dx, d_content, d_query_x, small = backward(
        lengths, grads, downs, squares, xall, probs, attended, d_attended.reshape(attended.shape),
        query, keys, values, dr1, x_content, x_query, dvec, positions, shards, seqn,
    )
    small = small.reshape(8, 16, 128)
    summed = jnp.transpose(small[:6, :12], (1, 0, 2)).reshape(UNITS, width)
    mine = lax.axis_index("dp")
    tiny = lax.dynamic_slice_in_dim(summed[:8], mine * r, r, 1)
    g_c1 = lax.dynamic_slice_in_dim(summed[8:].reshape(4 * width), mine * 4 * r, 4 * r, 0)
    g_table = small[6:].reshape(NB, 128)[:, :H]
    shape = (seqs, block, width)
    grad_content = (d_content + dx).reshape(shape)
    g_bq, g_bv, g_bo, g_g1, g_b1, g_c2, g_g2, g_b2 = (tiny[i] for i in range(8))
    g_w1 = jnp.transpose(sums[4:8], (1, 0, 2)).reshape(r, 4 * width)
    g_w2 = sums[8:12].reshape(4 * r, width)
    return (
        y_c.reshape(shape), y_q.reshape(shape), grad_content, d_query_x.reshape(shape),
        sums[2], g_bq, sums[0], sums[1], g_bv, sums[3], g_bo, g_g1, g_b1,
        g_w1, g_c1, g_w2, g_c2, g_g2, g_b2, g_table,
    )


def solution(mesh):
    in_specs = (
        P("dp", "seq", None),
        P("dp", "seq", None),
        P("dp", "seq", None),
        P("dp", "seq", None),
        P("dp", None),
        P("dp"),
        P("dp", None),
        P("dp", None),
        P("dp"),
        P("dp", None),
        P("dp"),
        P("dp"),
        P("dp"),
        P("dp", None),
        P("dp"),
        P("dp", None),
        P("dp"),
        P("dp"),
        P("dp"),
        P(),
        P("dp"),
        P("dp", None),
        P("dp", "seq"),
    )
    out_specs = (
        P("dp", "seq", None),
        P("dp", "seq", None),
        P("dp", "seq", None),
        P("dp", "seq", None),
        P("dp", None),
        P("dp"),
        P("dp", None),
        P("dp", None),
        P("dp"),
        P("dp", None),
        P("dp"),
        P("dp"),
        P("dp"),
        P("dp", None),
        P("dp"),
        P("dp", None),
        P("dp"),
        P("dp"),
        P("dp"),
        P(),
    )
    return jax.shard_map(
        functools.partial(per_device, shards=mesh.shape["dp"], seqn=mesh.shape["seq"]),
        mesh=mesh, in_specs=in_specs, out_specs=out_specs, check_vma=False
    )
```

time: 259 us -> 224 us (0.86)
  Pallas kernels: 236 us -> 205 us
  other arithmetic: 5.25 us -> 2.49 us
    pallas_call x1 -> x0, Pallas kernels: 40.5 us -> none  [middle(): pl.pallas_call(functools.partial(middle_kernel, seqs, block), out_shape=(...]
    pallas_call x1, Pallas kernels: 82.4 us -> 113 us  [forward(): pl.pallas_call(functools.partial(forward_kernel, shards, seqn, seqs, bloc...]
    pallas_call x1, Pallas kernels: 113 us -> 92.1 us  [backward(): pl.pallas_call(functools.partial(backward_kernel, shards, seqn, seqs, blo...]
    unnamed x14 -> x17, local copies, waits for them, and re-layouts: 2.19 us -> 5.32 us
where the time goes in v4:
time: 224 us; the launch traced here: 223 us
  Pallas kernels  205 us (92%)
  local copies, waits for them, and re-layouts  15.2 us (7%)
  other arithmetic  2.49 us (1%)
    pallas_call x1, Pallas kernels, forward(): pl.pallas_call(functools.partial(forward_kernel, shards, seqn, seqs, bloc...  113 us
    pallas_call x1, Pallas kernels, backward(): pl.pallas_call(functools.partial(backward_kernel, shards, seqn, seqs, blo...  92.1 us
    unnamed x17, local copies, waits for them, and re-layouts  5.32 us

profile of v4, /device:TPU:1, one launch (start us, length us, event | category | flops | bytes accessed | tf_op | source)
XLA Modules:
  0.0 223.3 jit_solution(775955786309906722)
XLA Ops:
  0.7 1.4 copy.45.rel_table
  2.0 1.2 reshape.126.c1
  3.3 112.9 %gather_attend_ffn.1 = (bf16[24,96,768]{2,1,0:T(8,128)(2,1)}, bf16[4,2,128,768]{3,2,1,0:T(8,128)(2,1)}, bf16[12,2,256,512]{3,2,1,0:T(8,128)(2,1)}, bf16[2,2,128,...) custom-call(s32[2]{0:T(128)} %lengths.3, ...), custom_call_target="tpu_custom_call" | custom-call | tf_op jit(solution)/shard_map/gather_attend_ffn/pallas_call | solution.py:1022
  116.1 92.1 %attend_back_reduce.1 = (f32[12,96,768]{2,1,0:T(8,128)}, f32[256,768]{1,0:T(8,128)}, f32[256,768]{1,0:T(8,128)}, f32[256,768]{1,0:T(8,128)}, f32[8,16,128]{2,1,0:T(8,128)}) custom-call(s32[2]{0:T(128)} %lengths.3, bf16[40,96,768]{2,1,0:T(8,128)(2,1)} %get-tuple-element.41.grads, bf16[4,4,2,48,768]{4,3,2,1,0:T(8,128)(2,1)} %get-tuple-element.42.downs, ...), custom_call_target="tpu_custom_call" | custom-call | tf_op jit(solution)/shard_map/attend_back_reduce/pallas_call | solution.py:1337
  208.3 0.0 copy-start
  208.3 2.5 %add.9 = f32[256,768]{1,0:T(8,128)} add(f32[256,768]{1,0:T(8,128)} %get-tuple-element.53, f32[256,768]{1,0:T(8,128)} %get-tuple-element.54) | non-fusion elementwise | flops 196608 | bytes 2359296 | tf_op jit(solution)/shard_map/add | solution.py:1401
  210.8 0.0 copy-start.5
  210.8 2.3 %slice_bitcast_fusion.1 = (f32[96,768]{1,0:T(8,128)}, f32[96,768]{1,0:T(8,128)}, f32[96,768]{1,0:T(8,128)}, f32[96,768]{1,0:T(8,128)}) fusion(f32[12,96,768]{2,1,0:T(8,128)} %get-tuple-element.56), kind=kLoop, calls=%fused_computation.1 | loop fusion | bytes 2359296 | tf_op jit(solution)/shard_map/squeeze | solution.py:1407
  213.0 0.0 copy-done.5
  213.0 0.0 copy-start.4
  213.1 0.6 copy-done.4
  213.7 0.6 slice_bitcast_fusion.6
  214.3 0.8 constant_dynamic-slice_fusion
  215.1 0.5 slice_bitcast_fusion.7
  215.6 0.0 copy-done
  215.6 1.2 fusion
  216.8 0.0 copy-start.2
  216.8 0.0 copy-start.1
  216.8 1.1 copy.50
  217.9 0.7 slice.82
  218.6 0.7 dynamic_slice.7
  219.3 0.7 slice.79
  220.0 0.7 copy.49
  220.7 0.0 copy-done.2
  220.7 0.0 copy-start.3
  220.7 0.9 copy.54
  221.6 0.0 copy-done.1
  221.6 0.9 copy.55
  222.5 0.0 copy-done.3
  222.5 0.9 copy.56
  (3 shorter events, 0.0 us)
Async XLA Ops:
  208.3 7.3 %copy-start = (f32[12,96,768]{2,1,0:T(8,128)S(1)}, f32[12,96,768]{2,1,0:T(8,128)}, u32[]{:S(2)}) copy-start(f32[12,96,768]{2,1,0:T(8,128)} %get-tuple-element.56) | copy-start | bytes 10616836
  210.8 2.3 %copy-start.5 = (f32[8,16,128]{2,1,0:T(8,128)S(1)}, f32[8,16,128]{2,1,0:T(8,128)}, u32[]{:S(2)}) copy-start(f32[8,16,128]{2,1,0:T(8,128)} %get-tuple-element.57) | copy-start | bytes 196612
  213.0 0.6 copy-start.4
  216.8 3.9 %copy-start.2 = (f32[256,768]{1,0:T(8,128)S(1)}, f32[256,768]{1,0:T(8,128)}, u32[]{:S(2)}) copy-start(f32[256,768]{1,0:T(8,128)} %get-tuple-element.39) | copy-start | bytes 2359300
  216.8 4.8 %copy-start.1 = (f32[256,768]{1,0:T(8,128)S(1)}, f32[256,768]{1,0:T(8,128)}, u32[]{:S(2)}) copy-start(f32[256,768]{1,0:T(8,128)} %get-tuple-element.40) | copy-start | bytes 2359300
  220.7 1.8 copy-start.3

commit v5 on v4

--- a/solution.py
+++ b/solution.py
@@ -68,6 +68,8 @@
 
 
 AHEAD = 2
+X_LAG = 1
+Y_LAG = 1
 
 
 def gather_steps(shards, seqn, ins, outs, scratch):
@@ -182,7 +184,7 @@
             return carry
 
         lax.fori_loop(1, rows, hop, 0)
-        ux = n - (rows - 1)
+        ux = n - (rows - 1) - X_LAG
 
         @pl.when((ux >= 0) & (ux < UNITS))
         def _():
@@ -195,7 +197,7 @@
 
             lax.fori_loop(0, rows, pass_on, 0)
 
-        uy = n - rows
+        uy = n - rows - X_LAG - Y_LAG
 
         @pl.when((uy >= 0) & (uy < UNITS))
         def _():
@@ -420,8 +422,8 @@
 
     def stage_half(u):
         half_copy(u).wait_recv()
-        out[(u,) + mine] = half[u].astype(f32)
-        out[(u,) + siblings] = got_half[u].astype(f32)
+        out[(u,) + mine] = half[u]
+        out[(u,) + siblings] = got_half[u]
 
     def sent():
         def one(u, carry):
@@ -541,7 +543,7 @@
 
     def third(dx_out):
         deck_dx.wait()
-        dx_out[...] = dx_own[deck].astype(f32) + dx_deck[...].astype(f32)
+        dx_out[...] += dx_own[deck].astype(f32) + dx_deck[...].astype(f32)
 
     return first, second, third
 
@@ -640,7 +642,8 @@
     )
 
 
-EARLY = 8
+EARLY = 9
+BIAS_STEPS = 8
 TILE = 256
 LONG = 384
 DOWNS = 4
@@ -669,7 +672,7 @@
     vall[me] = jnp.zeros(vall.shape[1:], f32)
     for i, piece in enumerate((bq, bv, bo, g1, b1, c2, g2, b2)):
         vall[me, i : i + 1, 0:r] = piece[...].astype(f32)
-    vall[me, 8:9, :] = c1[...].astype(f32)
+    vall[me, 8:9, :] = c1[...].astype(f32).reshape(1, wide)
     begin()
 
     def one(n, carry):
@@ -692,7 +695,7 @@
         eye = (
             lax.broadcasted_iota(jnp.int32, (NB, 128), 0) == lax.broadcasted_iota(jnp.int32, (NB, 128), 1)
         )
-        by_head = dot(rel_table[...], jnp.where(eye, 1.0, 0.0).astype(bf16), TN)
+        by_head = dot(rel_table[...], jnp.where(eye, 1.0, 0.0).astype(bf16))
         lane = lax.broadcasted_iota(jnp.int32, by_head.shape, 1)
         table[...] = jnp.where(lane < NB, by_head, -1e30)
         for s in range(seqs):
@@ -700,7 +703,7 @@
             chosen = column_of(predicted[s : s + 1, :])[:, 0:1] > 0
             keep[s * block : (s + 1) * block, :] = jnp.where(live, 1.0, 0.0)
             keep[half + s * block : half + (s + 1) * block, :] = jnp.where(live & chosen, 1.0, 0.0)
-        share = seqs * H // EARLY
+        share = seqs * H // BIAS_STEPS
 
         def one_and_bias(n, carry):
             step(n)
@@ -711,9 +714,10 @@
 
             return lax.fori_loop(0, share, bias, carry)
 
-        lax.fori_loop(0, EARLY - 2, one_and_bias, 0)
+        lax.fori_loop(0, BIAS_STEPS - 2, one_and_bias, 0)
         pass_x()
-        lax.fori_loop(EARLY - 2, EARLY, one_and_bias, 0)
+        lax.fori_loop(BIAS_STEPS - 2, BIAS_STEPS, one_and_bias, 0)
+        lax.fori_loop(BIAS_STEPS, EARLY, one, 0)
         wait_x()
         wait_vec()
         vectors[...] = jnp.zeros_like(vectors)
@@ -735,6 +739,10 @@
             whole(u)
 
         def project(k, carry):
+            @pl.when(k == 2)
+            def _():
+                step(EARLY)
+
             x = xall[k].reshape(half, width)
             at = pl.ds(pl.multiple_of(k * block, block), block)
             keys[:, at, :] = dot(x, matrix(0)).astype(bf16).reshape(seqs, block, width)
@@ -758,9 +766,9 @@
         def attend_one(i, carry):
             slot = lax.rem(i, 2)
 
-            @pl.when(lax.rem(i, 4) == 0)
+            @pl.when(lax.rem(i, 3) == 1)
             def _():
-                step(EARLY + i // 4)
+                step(EARLY + 1 + i // 3)
 
             @pl.when(i >= 2)
             def _():
@@ -785,7 +793,7 @@
         pltpu.VMEM((2, 2, 2 * block, span), bf16),
         pltpu.VMEM((seqs * H, 2, block, span), f32),
     )
-    done = EARLY + seqs * H // 8
+    done = EARLY + 1 + seqs * H // 6
     more = [
         pltpu.make_async_copy(full.at[pl.ds(0, 3 * shards)], squares, io_sem.at[3]),
         pltpu.make_async_copy(xall, x_out, io_sem.at[4]),
@@ -840,7 +848,7 @@
             whole(u)
             return carry
 
-        lax.fori_loop(done + 5, UNITS + shards // 2, one, 0)
+        lax.fori_loop(done + 5, UNITS + shards // 2 + X_LAG + Y_LAG, one, 0)
         lax.fori_loop(8, UNITS, last, 0)
 
         def phase_feed(n, carry):
@@ -875,15 +883,12 @@
             copy.start()
         longs = width // LONG
 
-        def phase_down(step_, carry):
-            j, n = step_ // longs, lax.rem(step_, longs)
-            cols = pl.ds(pl.multiple_of(n * LONG, 128), LONG)
-            grad = dot(active[j, :, cols], dr2_low[...], TN).astype(bf16)
-            per = LONG // r
-            stage_down[pl.ds(step_ * per, per)] = grad.reshape(per, r, width)
-            return carry
-
-        lax.fori_loop(0, 4 * longs, phase_down, 0)
+        def phase_down(j, carry):
+            grad = dot(active[j], dr2_low[...], TN).astype(bf16)
+            stage_down[pl.ds(j * shards, shards)] = grad.reshape(shards, r, width)
+            return carry
+
+        lax.fori_loop(0, 4, phase_down, 0)
 
         def start_down(k, carry):
             send_front(k, lambda shard: stage_down.at[shard * 4 + k])
@@ -891,29 +896,18 @@
 
         lax.fori_loop(0, DOWNS, start_down, 0)
 
-        def phase_slope(step_, carry):
-            j, n = step_ // longs, lax.rem(step_, longs)
-            cols = pl.ds(pl.multiple_of(n * LONG, 128), LONG)
-            du = slope[j, :, cols].astype(f32) * dot(dr2_low[...], row_block(8 + j, n), NT)
-            dvec[pl.ds(8 + j, 1), cols] = jnp.sum(du, axis=0, keepdims=True)
-            active[j, :, cols] = du.astype(bf16)
-
-            @pl.when(n == longs - 1)
-            def _():
-                stage_core(j)
-
-            return carry
-
-        lax.fori_loop(0, 4 * longs, phase_slope, 0)
+        def phase_slope(j, carry):
+            du = slope[j].astype(f32) * dot(dr2_low[...], matrix(8 + j), NT)
+            dvec[pl.ds(8 + j, 1), :] = jnp.sum(du, axis=0, keepdims=True)
+            active[j] = du.astype(bf16)
+            stage_core(j)
+            return carry
+
+        lax.fori_loop(0, 4, phase_slope, 0)
 
         def phase_up(j, carry):
-            def tile(n, inner):
-                cols = pl.ds(pl.multiple_of(n * TILE, TILE), TILE)
-                grad = dot(hidden_turn[...], active[j, :, cols]).astype(bf16)
-                stage[1 + j, :, :, cols] = grad.reshape(shards, r, TILE)
-                return inner
-
-            lax.fori_loop(0, tiles, tile, 0)
+            grad = dot(hidden_turn[...], active[j]).astype(bf16)
+            stage[1 + j] = grad.reshape(shards, r, width)
             pltpu.make_async_copy(
                 stage.at[1 + j], grads.at[pl.ds((1 + j) * shards, shards)], io_sem.at[10 + j]
             ).start()
@@ -1056,7 +1050,7 @@
         name="gather_attend_ffn",
     )(
         lengths, wk, wv, wq, wo, wu, wd.reshape(4, rows_of, width), xc, flat(xc), flat(xq), flat(cot_c), flat(cot_q),
-        positions, predicted, rel_table, *vecs,
+        positions, predicted, rel_table.T, *vecs,
     )
 
 
@@ -1117,7 +1111,7 @@
     shards, seqn, seqs, block, span, rows_of,
     lengths, grads, downs, squares, xall, probs, attended_in, da_in, query_in, keys_in, values_in, dr1_in,
     xc, xq, dvec, positions,
-    out, dx_out, d_content, d_query_x, small_out,
+    out, d_content, d_query_x, small_out,
     dq, dk, dv, late, w, x_every, dxs, sums, counts, small, io_sem, low_sem, *scratch,
 ):
     f32, bf16 = jnp.float32, jnp.bfloat16
@@ -1318,7 +1312,7 @@
     lax.fori_loop(33, 36, one, 0)
     small_third()
     lax.fori_loop(36, ticks, one, 0)
-    dx_third(dx_out)
+    dx_third(d_content)
     small_last(small_out)
     front_sent()
     back_sent()
@@ -1337,14 +1331,13 @@
     return pl.pallas_call(
         functools.partial(backward_kernel, shards, seqn, seqs, block, span, rows_of),
         out_shape=(
-            jax.ShapeDtypeStruct((UNITS, rows_of, width), f32),
-            jax.ShapeDtypeStruct(own, f32),
+            jax.ShapeDtypeStruct((UNITS, rows_of, width), bf16),
             jax.ShapeDtypeStruct(own, f32),
             jax.ShapeDtypeStruct(own, f32),
             jax.ShapeDtypeStruct(small_shape, f32),
         ),
         in_specs=[pl.BlockSpec(memory_space=pltpu.SMEM)] + [anywhere] * 13 + [vmem] * 2,
-        out_specs=(vmem,) * 5,
+        out_specs=(vmem,) * 4,
         scratch_shapes=[
             pltpu.VMEM((2, seqs, block, width), bf16),
             pltpu.VMEM((seqs, span, width), bf16),
@@ -1370,6 +1363,84 @@
     )(lengths, grads, downs, squares, xall, probs, attended, d_attended, query, keys, values, dr1, xc, xq, dvec, positions)
 
 
+def present_kernel(
+    shards, rows_of,
+    sums, small, y_c_in, y_q_in, g_c_in, g_q_in,
+    y_c, y_q, g_c, g_q, wk, wv, wq, wo, wu, wd, *rest,
+):
+    vectors, table, wide_rows, low, units, passing, in_sem, out_sem, pass_sem = rest[:9], rest[9], *rest[10:]
+    f32 = jnp.float32
+    width = H * HD
+    r = rows_of
+    get = pltpu.make_async_copy(sums, low, in_sem.at[4])
+    get.start()
+    moves = []
+    for i, (src, dst) in enumerate(((y_c_in, y_c), (y_q_in, y_q), (g_c_in, g_c), (g_q_in, g_q))):
+        come = pltpu.make_async_copy(src, passing.at[i], in_sem.at[i])
+        come.start()
+        moves.append((come, pltpu.make_async_copy(passing.at[i], dst, pass_sem.at[i])))
+    get.wait()
+    pieces = [wk, wv, wq, wo] + [wu.at[:, pl.ds(j * width, width)] for j in range(4)]
+    pieces += [wd.at[j] for j in range(4)]
+    outs = [pltpu.make_async_copy(units.at[u], piece, out_sem.at[u]) for u, piece in enumerate(pieces)]
+    for u, out in enumerate(outs):
+        units[u] = low[u].astype(f32)
+        out.start()
+        if u % 3 == 2:
+            come, go = moves[u // 3]
+            come.wait()
+            go.start()
+    me = lax.axis_index("dp")
+    whole = jnp.concatenate([small[c] for c in range(width // 128)], axis=1)
+    place_of = lax.broadcasted_iota(jnp.int32, (width, r), 0)
+    lane = lax.broadcasted_iota(jnp.int32, (width, r), 1)
+    mine = jnp.dot(whole, jnp.where(place_of == me * r + lane, 1.0, 0.0), precision=lax.Precision.HIGHEST)
+    for i in range(8):
+        vectors[i][...] = mine[i]
+    per = width // (4 * r)
+    place_of = lax.broadcasted_iota(jnp.int32, (width, 4 * r), 0)
+    lane = lax.broadcasted_iota(jnp.int32, (width, 4 * r), 1)
+    at = jnp.where(place_of == lax.rem(me, per) * (4 * r) + lane, 1.0, 0.0)
+    wide_rows[...] = jnp.dot(whole, at, precision=lax.Precision.HIGHEST)
+    vectors[8][...] = wide_rows[pl.ds(8 + me // per, 1), :].reshape(4 * r)
+    table[...] = jnp.concatenate([small[6], small[7]], axis=0).T[:H, :]
+    for out in outs:
+        out.wait()
+    for come, go in moves:
+        go.wait()
+
+
+def present(sums, small, y_c, y_q, g_c, g_q, shards):
+    _, r, width = sums.shape
+    f32, bf16 = jnp.float32, jnp.bfloat16
+    anywhere = pl.BlockSpec(memory_space=pl.ANY)
+    vmem = pl.BlockSpec(memory_space=pltpu.VMEM)
+    own = y_c.shape
+    shape = lambda *dims: jax.ShapeDtypeStruct(dims, f32)
+    dma = pltpu.SemaphoreType.DMA
+    return pl.pallas_call(
+        functools.partial(present_kernel, shards, r),
+        out_shape=(shape(*own),) * 4
+        + (shape(r, width),) * 4
+        + (shape(r, 4 * width), shape(4, r, width))
+        + (shape(r),) * 8
+        + (shape(4 * r), shape(H, NB)),
+        in_specs=[anywhere, vmem] + [anywhere] * 4,
+        out_specs=(anywhere,) * 10 + (vmem,) * 10,
+        scratch_shapes=[
+            pltpu.VMEM((16, 4 * r), f32),
+            pltpu.VMEM((UNITS, r, width), bf16),
+            pltpu.VMEM((UNITS, r, width), f32),
+            pltpu.VMEM((4,) + own, f32),
+            dma((5,)),
+            dma((UNITS,)),
+            dma((4,)),
+        ],
+        compiler_params=pltpu.CompilerParams(vmem_limit_bytes=67043328),
+        name="present",
+    )(sums, small.reshape(8, 16, 128), y_c, y_q, g_c, g_q)
+
+
 def per_device(
     x_content, x_query, cot_content, cot_query,
     w_query, b_query, w_key, w_value, b_value, w_out, b_out, gain_attn, shift_attn,
@@ -1380,32 +1451,25 @@
     seqs, block, width = x_content.shape
     r = w_query.shape[0]
     vecs = [
-        v.reshape(1, v.shape[0])
-        for v in (b_query, b_value, b_out, gain_attn, shift_attn, b_down, gain_ffn, shift_ffn, b_up)
-    ]
+        v.reshape(1, r) for v in (b_query, b_value, b_out, gain_attn, shift_attn, b_down, gain_ffn, shift_ffn)
+    ] + [b_up]
     (squares, xall, probs, attended, query, keys, values, y_c, y_q, dr1, d_attended, grads, downs, dvec) = forward(
         w_key, w_value, w_query, w_out, w_up, w_down, x_content, x_query, cot_content, cot_query, vecs,
         lengths, positions, predicted, rel_table, shards, seqn,
     )
-    sums, dx, d_content, d_query_x, small = backward(
+    sums, g_content, g_x_query, small = backward(
         lengths, grads, downs, squares, xall, probs, attended, d_attended.reshape(attended.shape),
         query, keys, values, dr1, x_content, x_query, dvec, positions, shards, seqn,
     )
-    small = small.reshape(8, 16, 128)
-    summed = jnp.transpose(small[:6, :12], (1, 0, 2)).reshape(UNITS, width)
-    mine = lax.axis_index("dp")
-    tiny = lax.dynamic_slice_in_dim(summed[:8], mine * r, r, 1)
-    g_c1 = lax.dynamic_slice_in_dim(summed[8:].reshape(4 * width), mine * 4 * r, 4 * r, 0)
-    g_table = small[6:].reshape(NB, 128)[:, :H]
+    (
+        y_c, y_q, g_content, g_x_query, g_wk, g_wv, g_wq, g_wo, g_w1, g_w2,
+        g_bq, g_bv, g_bo, g_g1, g_b1, g_c2, g_g2, g_b2, g_c1, g_table,
+    ) = present(sums, small, y_c, y_q, g_content, g_x_query, shards)
     shape = (seqs, block, width)
-    grad_content = (d_content + dx).reshape(shape)
-    g_bq, g_bv, g_bo, g_g1, g_b1, g_c2, g_g2, g_b2 = (tiny[i] for i in range(8))
-    g_w1 = jnp.transpose(sums[4:8], (1, 0, 2)).reshape(r, 4 * width)
-    g_w2 = sums[8:12].reshape(4 * r, width)
     return (
-        y_c.reshape(shape), y_q.reshape(shape), grad_content, d_query_x.reshape(shape),
-        sums[2], g_bq, sums[0], sums[1], g_bv, sums[3], g_bo, g_g1, g_b1,
-        g_w1, g_c1, g_w2, g_c2, g_g2, g_b2, g_table,
+        y_c.reshape(shape), y_q.reshape(shape), g_content.reshape(shape), g_x_query.reshape(shape),
+        g_wq, g_bq, g_wk, g_wv, g_bv, g_wo, g_bo, g_g1, g_b1,
+        g_w1, g_c1, g_w2.reshape(4 * r, width), g_c2, g_g2, g_b2, g_table.T,
     )
 
 

time: 224 us -> 204 us (0.911)
  local copies, waits for them, and re-layouts: 15.2 us -> 0 us
  other arithmetic: 2.49 us -> 0 us
    pallas_call x1, Pallas kernels: 113 us -> 105 us  [forward(): pl.pallas_call(functools.partial(forward_kernel, shards, seqn, seqs, bloc...]
    pallas_call x0 -> x1, Pallas kernels: none -> 5.94 us  [present(): pl.pallas_call(functools.partial(present_kernel, shards, r), out_shape=(s...]
    unnamed x17 -> x0, local copies, waits for them, and re-layouts: 5.32 us -> none
    slice x5 -> x0, local copies, waits for them, and re-layouts: 3.24 us -> none  [the longest x1 1.17 us: per_device(): g_w2 = sums[8:12].reshape(4 * r, width)]
    squeeze x2 -> x0, local copies, waits for them, and re-layouts: 2.83 us -> none  [the longest x1 2.29 us: per_device(): sums[3]]
    add x1 -> x0, other arithmetic: 2.49 us -> none  [per_device(): grad_content = (d_content + dx).reshape(shape)]
    reshape x3 -> x0, local copies, waits for them, and re-layouts: 2.37 us -> none  [the longest x1 1.24 us: per_device(): v.reshape(1, v.shape[0])]
where the time goes in v5:
time: 204 us
  Pallas kernels  203 us (100%)
    pallas_call x1, Pallas kernels, forward(): pl.pallas_call(functools.partial(forward_kernel, shards, seqn, seqs, bloc...  105 us
    pallas_call x1, Pallas kernels, backward(): pl.pallas_call(functools.partial(backward_kernel, shards, seqn, seqs, blo...  91.8 us
    pallas_call x1, Pallas kernels, present(): pl.pallas_call(functools.partial(present_kernel, shards, r), out_shape=(s...  5.94 us

profile of v5, /device:TPU:1, one launch (start us, length us, event | category | flops | bytes accessed | tf_op | source)
XLA Modules:
  0.0 203.7 jit_solution(7870045098707539312)
XLA Ops:
  0.7 105.1 %gather_attend_ffn.1 = (bf16[24,96,768]{2,1,0:T(8,128)(2,1)}, bf16[4,2,128,768]{3,2,1,0:T(8,128)(2,1)}, bf16[12,2,256,512]{3,2,1,0:T(8,128)(2,1)}, bf16[2,2,128,...) custom-call(s32[2]{0:T(128)} %lengths.3, ...), custom_call_target="tpu_custom_call" | custom-call | tf_op jit(solution)/shard_map/gather_attend_ffn/pallas_call | solution.py:1016
  105.8 91.8 %attend_back_reduce.1 = (bf16[12,96,768]{2,1,0:T(8,128)(2,1)}, f32[256,768]{1,0:T(8,128)}, f32[256,768]{1,0:T(8,128)}, f32[8,16,128]{2,1,0:T(8,128)}) custom-call(s32[2]{0:T(128)} %lengths.3, bf16[40,96,768]{2,1,0:T(8,128)(2,1)} %get-tuple-element.58.grads, bf16[4,4,2,48,768]{4,3,2,1,0:T(8,128)(2,1)} %get-tuple-element.59.downs, ...), custom_call_target="tpu_custom_call" | custom-call | tf_op jit(solution)/shard_map/attend_back_reduce/pallas_call | solution.py:1331
  197.6 5.9 %present.1 = (f32[256,768]{1,0:T(8,128)}, f32[256,768]{1,0:T(8,128)}, f32[256,768]{1,0:T(8,128)}, f32[256,768]{1,0:T(8,128)}, f32[96,768]{1,0:T(8,128)}, /*index...) custom-call(bf16[12,96,768]{2,1,0:T(8,128)(2,1)} %get-tuple-element., ...), custom_call_target="tpu_custom_call" | custom-call | tf_op jit(solution)/shard_map/present/pallas_call | solution.py:1421

commit v6 on v5

--- a/solution.py
+++ b/solution.py
@@ -643,7 +643,8 @@
 
 
 EARLY = 9
-BIAS_STEPS = 8
+BIAS_FROM = 3
+BIAS_STEPS = 6
 TILE = 256
 LONG = 384
 DOWNS = 4
@@ -651,10 +652,10 @@
 
 def forward_kernel(
     shards, seqn, seqs, block, span, rows_of,
-    lengths, wk, wv, wq, wo, wu, wd, xc, xc_rows, xq_rows, cot_c, cot_q, positions, predicted, rel_table,
+    lengths, wk, wv, wq, wo, wu, wd, xc, xc_in, xq_in, cot_c_in, cot_q_in, positions, predicted, rel_table,
     bq, bv, bo, g1, b1, c2, g2, b2, c1,
     squares, x_out, probs, attended_out, query_out, keys_out, values_out, y_c, y_q, dr1_out, da_out, grads, downs, dvec,
-    full, xall, vall, vectors, keep, attended, table, io_sem, low_sem, *scratch,
+    full, xall, vall, vectors, keep, attended, table, xc_rows, xq_rows, cot_c, cot_q, io_sem, low_sem, row_sem, *scratch,
 ):
     f32, bf16 = jnp.float32, jnp.bfloat16
     width = H * HD
@@ -674,6 +675,12 @@
         vall[me, i : i + 1, 0:r] = piece[...].astype(f32)
     vall[me, 8:9, :] = c1[...].astype(f32).reshape(1, wide)
     begin()
+    streams = [
+        pltpu.make_async_copy(src, dst, row_sem.at[i])
+        for i, (src, dst) in enumerate(((xc_in, xc_rows), (xq_in, xq_rows), (cot_c_in, cot_c), (cot_q_in, cot_q)))
+    ]
+    for copy in streams:
+        copy.start()
 
     def one(n, carry):
         step(n)
@@ -709,17 +716,20 @@
             step(n)
 
             def bias(k, inner):
-                fill_bias(n * share + k, biases, buckets, table, block, span)
+                fill_bias((n - BIAS_FROM) * share + k, biases, buckets, table, block, span)
                 return inner
 
             return lax.fori_loop(0, share, bias, carry)
 
-        lax.fori_loop(0, BIAS_STEPS - 2, one_and_bias, 0)
+        lax.fori_loop(0, BIAS_FROM, one, 0)
+        lax.fori_loop(BIAS_FROM, BIAS_FROM + 3, one_and_bias, 0)
         pass_x()
-        lax.fori_loop(BIAS_STEPS - 2, BIAS_STEPS, one_and_bias, 0)
-        lax.fori_loop(BIAS_STEPS, EARLY, one, 0)
+        lax.fori_loop(BIAS_FROM + 3, BIAS_FROM + BIAS_STEPS, one_and_bias, 0)
+        lax.fori_loop(BIAS_FROM + BIAS_STEPS, EARLY, one, 0)
         wait_x()
         wait_vec()
+        for copy in streams:
+            copy.wait()
         vectors[...] = jnp.zeros_like(vectors)
 
         def spread(i, carry):
@@ -1031,7 +1041,7 @@
             jax.ShapeDtypeStruct((DOWNS, rows, 2) + shape(3), bf16),
             jax.ShapeDtypeStruct((UNITS, width), f32),
         ),
-        in_specs=[pl.BlockSpec(memory_space=pltpu.SMEM)] + [anywhere] * 7 + [vmem] * 16,
+        in_specs=[pl.BlockSpec(memory_space=pltpu.SMEM)] + [anywhere] * 11 + [vmem] * 12,
         out_specs=(anywhere,) * 13 + (vmem,),
         scratch_shapes=[
             pltpu.VMEM((UNITS * shards, rows_of, width), bf16),
@@ -1041,8 +1051,13 @@
             pltpu.VMEM((2 * half, 1), f32),
             pltpu.VMEM(stream, bf16),
             pltpu.VMEM((H, 128), f32),
+            pltpu.VMEM((half, width), bf16),
+            pltpu.VMEM((half, width), bf16),
+            pltpu.VMEM((half, width), bf16),
+            pltpu.VMEM((half, width), bf16),
             dma((18,)),
             dma((2,)),
+            dma((4,)),
         ]
         + gather_scratch(shards)
         + front_scratch(shards, rows_of, DOWNS),
@@ -1141,23 +1156,23 @@
     ready, late_from_unit = DOWNS, DOWNS + early
     plan = (
         (stage_core, ready, early, 1, 1),
-        (deck_and_across, ready, early, 4, 2),
-        (across, 0, DOWNS, 3, 2),
-        (line, 0, DOWNS, 6, 2),
-        (final, 0, DOWNS, 8, 2),
-        (half_stage, 0, DOWNS, 10, 2),
-        (across, ready, early, 11, 4),
-        (stage_core, late_from_unit, 3, 15, 3),
-        (line, ready, early, 16, 4),
-        (final, ready, early, 18, 4),
-        (half_stage, ready, early, 20, 4),
-        (deck_and_across, late_from_unit, 3, 22, 3),
-        (across, late_from_unit, 3, 29, 2),
-        (line, late_from_unit, 3, 32, 2),
-        (final, late_from_unit, 3, 34, 2),
-        (half_stage, late_from_unit, 3, 36, 2),
+        (across, 0, DOWNS, 6, 3),
+        (deck_and_across, ready, early, 9, 3),
+        (line, 0, DOWNS, 12, 3),
+        (final, 0, DOWNS, 15, 3),
+        (half_stage, 0, DOWNS, 18, 3),
+        (across, ready, early, 18, 3),
+        (stage_core, late_from_unit, 3, 18, 3),
+        (line, ready, early, 24, 3),
+        (deck_and_across, late_from_unit, 3, 24, 3),
+        (final, ready, early, 27, 3),
+        (half_stage, ready, early, 30, 3),
+        (across, late_from_unit, 3, 32, 3),
+        (line, late_from_unit, 3, 38, 3),
+        (final, late_from_unit, 3, 42, 3),
+        (half_stage, late_from_unit, 3, 45, 3),
     )
-    ticks = 41
+    ticks = 52
 
     def tick(t):
         for stage, first, count, start, gap in plan:

time: 204 us -> 194 us (0.951)
  Pallas kernels: 203 us -> 193 us
    pallas_call x1, Pallas kernels: 91.8 us -> 82.2 us  [backward(): pl.pallas_call(functools.partial(backward_kernel, shards, seqn, seqs, blo...]
where the time goes in v6:
time: 194 us
  Pallas kernels  193 us (99%)
    pallas_call x1, Pallas kernels, forward(): pl.pallas_call(functools.partial(forward_kernel, shards, seqn, seqs, bloc...  105 us
    pallas_call x1, Pallas kernels, backward(): pl.pallas_call(functools.partial(backward_kernel, shards, seqn, seqs, blo...  82.2 us
    pallas_call x1, Pallas kernels, present(): pl.pallas_call(functools.partial(present_kernel, shards, r), out_shape=(s...  5.94 us

profile of v6, /device:TPU:1, one launch (start us, length us, event | category | flops | bytes accessed | tf_op | source)
XLA Modules:
  0.0 193.8 jit_solution(8983297292962695882)
XLA Ops:
  0.7 104.8 %gather_attend_ffn.1 = (bf16[24,96,768]{2,1,0:T(8,128)(2,1)}, bf16[4,2,128,768]{3,2,1,0:T(8,128)(2,1)}, bf16[12,2,256,512]{3,2,1,0:T(8,128)(2,1)}, bf16[2,2,128,...) custom-call(s32[2]{0:T(128)} %lengths.3, ...), custom_call_target="tpu_custom_call" | custom-call | tf_op jit(solution)/shard_map/gather_attend_ffn/pallas_call | solution.py:1026
  105.5 82.2 %attend_back_reduce.1 = (bf16[12,96,768]{2,1,0:T(8,128)(2,1)}, f32[256,768]{1,0:T(8,128)}, f32[256,768]{1,0:T(8,128)}, f32[8,16,128]{2,1,0:T(8,128)}) custom-call(s32[2]{0:T(128)} %lengths.3, bf16[40,96,768]{2,1,0:T(8,128)(2,1)} %get-tuple-element.58.grads, bf16[4,4,2,48,768]{4,3,2,1,0:T(8,128)(2,1)} %get-tuple-element.59.downs, ...), custom_call_target="tpu_custom_call" | custom-call | tf_op jit(solution)/shard_map/attend_back_reduce/pallas_call | solution.py:1346
  187.7 5.9 %present.1 = (f32[256,768]{1,0:T(8,128)}, f32[256,768]{1,0:T(8,128)}, f32[256,768]{1,0:T(8,128)}, f32[256,768]{1,0:T(8,128)}, f32[96,768]{1,0:T(8,128)}, /*index...) custom-call(bf16[12,96,768]{2,1,0:T(8,128)(2,1)} %get-tuple-element., ...), custom_call_target="tpu_custom_call" | custom-call | tf_op jit(solution)/shard_map/present/pallas_call | solution.py:1436

commit v7 on v6

--- a/solution.py
+++ b/solution.py
@@ -1160,19 +1160,19 @@
         (deck_and_across, ready, early, 9, 3),
         (line, 0, DOWNS, 12, 3),
         (final, 0, DOWNS, 15, 3),
+        (stage_core, late_from_unit, 3, 16, 3),
         (half_stage, 0, DOWNS, 18, 3),
         (across, ready, early, 18, 3),
-        (stage_core, late_from_unit, 3, 18, 3),
+        (deck_and_across, late_from_unit, 3, 21, 3),
         (line, ready, early, 24, 3),
-        (deck_and_across, late_from_unit, 3, 24, 3),
         (final, ready, early, 27, 3),
         (half_stage, ready, early, 30, 3),
-        (across, late_from_unit, 3, 32, 3),
-        (line, late_from_unit, 3, 38, 3),
-        (final, late_from_unit, 3, 42, 3),
-        (half_stage, late_from_unit, 3, 45, 3),
+        (across, late_from_unit, 3, 30, 3),
+        (line, late_from_unit, 3, 36, 3),
+        (final, late_from_unit, 3, 40, 3),
+        (half_stage, late_from_unit, 3, 43, 3),
     )
-    ticks = 52
+    ticks = 50
 
     def tick(t):
         for stage, first, count, start, gap in plan:

time: 194 us -> 192 us (0.990)
  Pallas kernels: 193 us -> 191 us
    pallas_call x1, Pallas kernels: 82.2 us -> 80 us  [backward(): pl.pallas_call(functools.partial(backward_kernel, shards, seqn, seqs, blo...]
where the time goes in v7:
time: 192 us
  Pallas kernels  191 us (99%)
    pallas_call x1, Pallas kernels, forward(): pl.pallas_call(functools.partial(forward_kernel, shards, seqn, seqs, bloc...  105 us
    pallas_call x1, Pallas kernels, backward(): pl.pallas_call(functools.partial(backward_kernel, shards, seqn, seqs, blo...  80 us
    pallas_call x1, Pallas kernels, present(): pl.pallas_call(functools.partial(present_kernel, shards, r), out_shape=(s...  5.94 us

profile of v7, /device:TPU:1, one launch (start us, length us, event | category | flops | bytes accessed | tf_op | source)
XLA Modules:
  0.0 191.5 jit_solution(18260904314058074777)
XLA Ops:
  0.7 104.8 %gather_attend_ffn.1 = (bf16[24,96,768]{2,1,0:T(8,128)(2,1)}, bf16[4,2,128,768]{3,2,1,0:T(8,128)(2,1)}, bf16[12,2,256,512]{3,2,1,0:T(8,128)(2,1)}, bf16[2,2,128,...) custom-call(s32[2]{0:T(128)} %lengths.3, ...), custom_call_target="tpu_custom_call" | custom-call | tf_op jit(solution)/shard_map/gather_attend_ffn/pallas_call | solution.py:1026
  105.5 80.0 %attend_back_reduce.1 = (bf16[12,96,768]{2,1,0:T(8,128)(2,1)}, f32[256,768]{1,0:T(8,128)}, f32[256,768]{1,0:T(8,128)}, f32[8,16,128]{2,1,0:T(8,128)}) custom-call(s32[2]{0:T(128)} %lengths.3, bf16[40,96,768]{2,1,0:T(8,128)(2,1)} %get-tuple-element.58.grads, bf16[4,4,2,48,768]{4,3,2,1,0:T(8,128)(2,1)} %get-tuple-element.59.downs, ...), custom_call_target="tpu_custom_call" | custom-call | tf_op jit(solution)/shard_map/attend_back_reduce/pallas_call | solution.py:1346
  185.4 5.9 %present.1 = (f32[256,768]{1,0:T(8,128)}, f32[256,768]{1,0:T(8,128)}, f32[256,768]{1,0:T(8,128)}, f32[256,768]{1,0:T(8,128)}, f32[96,768]{1,0:T(8,128)}, /*index...) custom-call(bf16[12,96,768]{2,1,0:T(8,128)(2,1)} %get-tuple-element., ...), custom_call_target="tpu_custom_call" | custom-call | tf_op jit(solution)/shard_map/present/pallas_call | solution.py:1436

commit v8 on v7

--- a/solution.py
+++ b/solution.py
@@ -647,14 +647,15 @@
 BIAS_STEPS = 6
 TILE = 256
 LONG = 384
-DOWNS = 4
+DOWNS = 3
 
 
 def forward_kernel(
     shards, seqn, seqs, block, span, rows_of,
     lengths, wk, wv, wq, wo, wu, wd, xc, xc_in, xq_in, cot_c_in, cot_q_in, positions, predicted, rel_table,
     bq, bv, bo, g1, b1, c2, g2, b2, c1,
-    squares, x_out, probs, attended_out, query_out, keys_out, values_out, y_c, y_q, dr1_out, da_out, grads, downs, dvec,
+    squares, x_out, probs, attended_out, query_out, keys_out, values_out, y_c, y_q, dr1_out, da_out, grads, downs, rest,
+    dvec,
     full, xall, vall, vectors, keep, attended, table, xc_rows, xq_rows, cot_c, cot_q, io_sem, low_sem, row_sem, *scratch,
 ):
     f32, bf16 = jnp.float32, jnp.bfloat16
@@ -901,16 +902,18 @@
         lax.fori_loop(0, 4, phase_down, 0)
 
         def start_down(k, carry):
-            send_front(k, lambda shard: stage_down.at[shard * 4 + k])
+            send_front(k, lambda shard: stage_down.at[shard * 4 + 4 - DOWNS + k])
             return carry
 
         lax.fori_loop(0, DOWNS, start_down, 0)
+        rest_copy = pltpu.make_async_copy(stage_down, rest, io_sem.at[8])
+        rest_copy.start()
 
         def phase_slope(j, carry):
             du = slope[j].astype(f32) * dot(dr2_low[...], matrix(8 + j), NT)
             dvec[pl.ds(8 + j, 1), :] = jnp.sum(du, axis=0, keepdims=True)
             active[j] = du.astype(bf16)
-            stage_core(j)
+            pl.when(j < DOWNS)(lambda: stage_core(j))
             return carry
 
         lax.fori_loop(0, 4, phase_slope, 0)
@@ -932,8 +935,6 @@
             stage_deck(k)
             put_down(k).start()
 
-        finish_down(0)
-
         def phase_hidden(n, carry):
             cols = pl.ds(pl.multiple_of(n * LONG, 128), LONG)
             dr2[:, cols] += sum(dot(active[j], row_block(4 + j, n), NT) for j in range(4))
@@ -942,7 +943,7 @@
         lax.fori_loop(0, longs, phase_hidden, 0)
         for copy in y_copies:
             copy.wait()
-        finish_down(1)
+        finish_down(0)
 
         def phase_five(c, carry):
             at = pl.ds(pl.multiple_of(c * chunk, chunk), chunk)
@@ -965,7 +966,8 @@
         ]
         for copy in finals:
             copy.start()
-        finish_down(2)
+        for k in range(1, DOWNS - 1):
+            finish_down(k)
         turned = attended[...].reshape(rows, width).T
 
         def phase_out(n, carry):
@@ -978,12 +980,14 @@
         lax.fori_loop(0, tiles, phase_out, 0)
         out_copy = pltpu.make_async_copy(stage.at[0], grads.at[pl.ds(0, shards)], io_sem.at[9])
         out_copy.start()
-        finish_down(3)
+        finish_down(DOWNS - 1)
         for j in range(4):
             pltpu.make_async_copy(
                 stage.at[1 + j], grads.at[pl.ds((1 + j) * shards, shards)], io_sem.at[10 + j]
             ).wait()
-            put_down(j).wait()
+        for k in range(DOWNS):
+            put_down(k).wait()
+        rest_copy.wait()
         out_copy.wait()
         for copy in finals + more:
             copy.wait()
@@ -1039,10 +1043,11 @@
             jax.ShapeDtypeStruct((2 * half, width), bf16),
             jax.ShapeDtypeStruct((5 * shards, rows_of, width), bf16),
             jax.ShapeDtypeStruct((DOWNS, rows, 2) + shape(3), bf16),
+            jax.ShapeDtypeStruct((4 * shards, rows_of, width), bf16),
             jax.ShapeDtypeStruct((UNITS, width), f32),
         ),
         in_specs=[pl.BlockSpec(memory_space=pltpu.SMEM)] + [anywhere] * 11 + [vmem] * 12,
-        out_specs=(anywhere,) * 13 + (vmem,),
+        out_specs=(anywhere,) * 14 + (vmem,),
         scratch_shapes=[
             pltpu.VMEM((UNITS * shards, rows_of, width), bf16),
             pltpu.VMEM((seqn,) + xc.shape, bf16),
@@ -1124,7 +1129,7 @@
 
 def backward_kernel(
     shards, seqn, seqs, block, span, rows_of,
-    lengths, grads, downs, squares, xall, probs, attended_in, da_in, query_in, keys_in, values_in, dr1_in,
+    lengths, grads, downs, rest, squares, xall, probs, attended_in, da_in, query_in, keys_in, values_in, dr1_in,
     xc, xq, dvec, positions,
     out, d_content, d_query_x, small_out,
     dq, dk, dv, late, w, x_every, dxs, sums, counts, small, io_sem, low_sem, *scratch,
@@ -1205,16 +1210,22 @@
             load.start()
         pl.semaphore_wait(barrier, count)
 
+        def send_rest(k, carry):
+            u = order(DOWNS + k)
+            send_front(u, lambda shard: rest.at[shard * 4 + u - 8])
+            return carry
+
         def send(k, carry):
-            u = order(DOWNS + k)
+            u = order(4 + k)
             send_front(u, lambda shard: grads.at[(u - 3) * shards + shard])
             return carry
 
         def send_down(k, carry):
-            send_across(order(k), downs.at[order(k) - 8])
-            return carry
-
-        lax.fori_loop(0, early, send, 0)
+            send_across(order(k), downs.at[order(k) - (UNITS - DOWNS)])
+            return carry
+
+        lax.fori_loop(0, 4 - DOWNS, send_rest, 0)
+        lax.fori_loop(0, 5, send, 0)
         lax.fori_loop(0, DOWNS, send_down, 0)
         fill_buckets(buckets, positions, lengths, sq * block, seqs, block, span)
         counts[...] = jnp.zeros_like(counts)
@@ -1333,7 +1344,7 @@
     back_sent()
 
 
-def backward(lengths, grads, downs, squares, xall, probs, attended, d_attended, query, keys, values, dr1, xc, xq, dvec, positions, shards, seqn):
+def backward(lengths, grads, downs, rest, squares, xall, probs, attended, d_attended, query, keys, values, dr1, xc, xq, dvec, positions, shards, seqn):
     rows_of, width = squares.shape[1:]
     seqs, block, _ = xc.shape
     span = positions.shape[1]
@@ -1351,7 +1362,7 @@
             jax.ShapeDtypeStruct(own, f32),
             jax.ShapeDtypeStruct(small_shape, f32),
         ),
-        in_specs=[pl.BlockSpec(memory_space=pltpu.SMEM)] + [anywhere] * 13 + [vmem] * 2,
+        in_specs=[pl.BlockSpec(memory_space=pltpu.SMEM)] + [anywhere] * 14 + [vmem] * 2,
         out_specs=(vmem,) * 4,
         scratch_shapes=[
             pltpu.VMEM((2, seqs, block, width), bf16),
@@ -1375,7 +1386,7 @@
             collective_id=1, has_side_effects=True, vmem_limit_bytes=67043328
         ),
         name="attend_back_reduce",
-    )(lengths, grads, downs, squares, xall, probs, attended, d_attended, query, keys, values, dr1, xc, xq, dvec, positions)
+    )(lengths, grads, downs, rest, squares, xall, probs, attended, d_attended, query, keys, values, dr1, xc, xq, dvec, positions)
 
 
 def present_kernel(
@@ -1468,12 +1479,12 @@
     vecs = [
         v.reshape(1, r) for v in (b_query, b_value, b_out, gain_attn, shift_attn, b_down, gain_ffn, shift_ffn)
     ] + [b_up]
-    (squares, xall, probs, attended, query, keys, values, y_c, y_q, dr1, d_attended, grads, downs, dvec) = forward(
+    (squares, xall, probs, attended, query, keys, values, y_c, y_q, dr1, d_attended, grads, downs, rest, dvec) = forward(
         w_key, w_value, w_query, w_out, w_up, w_down, x_content, x_query, cot_content, cot_query, vecs,
         lengths, positions, predicted, rel_table, shards, seqn,
     )
     sums, g_content, g_x_query, small = backward(
-        lengths, grads, downs, squares, xall, probs, attended, d_attended.reshape(attended.shape),
+        lengths, grads, downs, rest, squares, xall, probs, attended, d_attended.reshape(attended.shape),
         query, keys, values, dr1, x_content, x_query, dvec, positions, shards, seqn,
     )
     (

time: 192 us -> 196 us (1.021)
  Pallas kernels: 191 us -> 195 us
    pallas_call x1, Pallas kernels: 80 us -> 87.9 us  [backward(): pl.pallas_call(functools.partial(backward_kernel, shards, seqn, seqs, blo...]
    pallas_call x1, Pallas kernels: 105 us -> 101 us  [forward(): pl.pallas_call(functools.partial(forward_kernel, shards, seqn, seqs, bloc...]
where the time goes in v8:
time: 196 us; the launch traced here: 195 us
  Pallas kernels  195 us (99%)
    pallas_call x1, Pallas kernels, forward(): pl.pallas_call(functools.partial(forward_kernel, shards, seqn, seqs, bloc...  101 us
    pallas_call x1, Pallas kernels, backward(): pl.pallas_call(functools.partial(backward_kernel, shards, seqn, seqs, blo...  87.9 us
    pallas_call x1, Pallas kernels, present(): pl.pallas_call(functools.partial(present_kernel, shards, r), out_shape=(s...  5.94 us

profile of v8, /device:TPU:1, one launch (start us, length us, event | category | flops | bytes accessed | tf_op | source)
XLA Modules:
  0.0 195.4 jit_solution(5771214560109012354)
XLA Ops:
  0.7 100.7 %gather_attend_ffn.1 = (bf16[24,96,768]{2,1,0:T(8,128)(2,1)}, bf16[4,2,128,768]{3,2,1,0:T(8,128)(2,1)}, bf16[12,2,256,512]{3,2,1,0:T(8,128)(2,1)}, bf16[2,2,128,...) custom-call(s32[2]{0:T(128)} %lengths.3, ...), custom_call_target="tpu_custom_call" | custom-call | tf_op jit(solution)/shard_map/gather_attend_ffn/pallas_call | solution.py:1030
  101.4 87.9 %attend_back_reduce.1 = (bf16[12,96,768]{2,1,0:T(8,128)(2,1)}, f32[256,768]{1,0:T(8,128)}, f32[256,768]{1,0:T(8,128)}, f32[8,16,128]{2,1,0:T(8,128)}) custom-call(s32[2]{0:T(128)} %lengths.3, bf16[40,96,768]{2,1,0:T(8,128)(2,1)} %get-tuple-element.59.grads, bf16[3,4,2,48,768]{4,3,2,1,0:T(8,128)(2,1)} %get-tuple-element.60.downs, ...), custom_call_target="tpu_custom_call" | custom-call | tf_op jit(solution)/shard_map/attend_back_reduce/pallas_call | solution.py:1357
  189.3 5.9 %present.1 = (f32[256,768]{1,0:T(8,128)}, f32[256,768]{1,0:T(8,128)}, f32[256,768]{1,0:T(8,128)}, f32[256,768]{1,0:T(8,128)}, f32[96,768]{1,0:T(8,128)}, /*index...) custom-call(bf16[12,96,768]{2,1,0:T(8,128)(2,1)} %get-tuple-element., ...), custom_call_target="tpu_custom_call" | custom-call | tf_op jit(solution)/shard_map/present/pallas_call | solution.py:1447
